TPU v7x, 32 devices: a whole 2x2x4 slice. The times are simulated.
32 devices in a mesh: depth: 16 (over z, x, core), lat: 2 (over y).
Axes of the slice: x: 2, y: 2, z: 4, core: 2. Of those that a mesh axis runs over, the one named last changes fastest.
Arguments:
- in_flight: float32 [16, 4, 64, 256], P('depth', None, 'lat'), may hold values from -6 to 6
- entering: float32 [2, 4, 64, 256], P(None, None, 'lat'), may hold values from -6 to 6
- classes: int32 [16, 64, 256], P('depth', 'lat'), may hold values from 0 to 31
- freq_phase: float32 [18], replicated, may hold values from 4 to 8.5
- class_slowness: float32 [32], replicated, may hold values from 0.8 to 1.4
Outputs:
- images: float32 [16, 8, 64, 256], P('depth', None, 'lat')
- wave_out: float32 [16, 4, 64, 256], P('depth', None, 'lat')
All inputs are finite; a program needn't handle non-finite values.
Results may differ from a plain program's by a relative error of at most 0.0003.
Values sent between devices are 32-bit elements; how exact they have to be, the bound alone decides.
No kernel may reach another device: no remote copies, remote signals or barrier semaphores. Data moves between devices by JAX's collectives and lax.ppermute only.
A program may use at most 64 MiB of HBM per device.

v0:
```python
import functools

import jax
import jax.numpy as jnp
from jax import lax
from jax.experimental import pallas as pl
from jax.experimental.pallas import tpu as pltpu
from jax.sharding import PartitionSpec as P

TERMS = 16
OFFSETS = 8
TURNS = 3
LANES = 128
SUBLANES = 8
BLOCKS = 4
MARGIN = OFFSETS // 2
VMEM_BYTES = 4 << 20

hale_weight = 0.0255
edge_weight = 0.25 - 0.5 * hale_weight
corner_weight = 0.125 + 0.25 * hale_weight
miller_start = 32

VMEM = pl.BlockSpec(memory_space=pltpu.VMEM)
SMEM = pl.BlockSpec(memory_space=pltpu.SMEM)
ANY = pl.BlockSpec(memory_space=pl.ANY)


def call(kernel, outs, in_specs, scratch, args, flops=0):
    moved = 4 * sum(int(a.size) for a in (*args, *outs))
    return pl.pallas_call(
        kernel,
        out_shape=outs,
        in_specs=in_specs,
        out_specs=[VMEM] * len(outs),
        scratch_shapes=scratch,
        compiler_params=pltpu.CompilerParams(vmem_limit_bytes=VMEM_BYTES),
        cost_estimate=pl.CostEstimate(flops=flops, bytes_accessed=moved, transcendentals=0),
    )(*args)


def f32(*shape):
    return jax.ShapeDtypeStruct(shape, jnp.float32)


def table_kernel(phase_ref, slow_ref, out_ref, z_ref):
    first = lax.axis_size("depth") - 1 - lax.axis_index("depth")
    classes = slow_ref.shape[1]
    z_ref[...] = jnp.full(z_ref.shape, 6.0, jnp.float32)
    for turn in range(TURNS):
        z_ref[turn : turn + 1, 0:classes] = slow_ref[...] * phase_ref[first + turn]
    phases = z_ref[...]
    values = [None] * (miller_start + 1)
    upper = jnp.zeros_like(phases)
    current = jnp.ones_like(phases)
    values[miller_start] = current
    inverse = 1.0 / phases
    for k in range(miller_start, 0, -1):
        lower = (2.0 * k * inverse) * current - upper
        values[k - 1] = lower
        upper, current = current, lower
    evens = values[2]
    for k in range(4, miller_start + 1, 2):
        evens = evens + values[k]
    scale = 1.0 / (values[0] + 2.0 * evens)
    for k in range(TERMS):
        factor = (1.0 if k == 0 else 2.0) * (1.0 if k % 4 < 2 else -1.0)
        ratio = values[k] * scale * factor
        for turn in range(TURNS):
            out_ref[turn, k] = jnp.broadcast_to(ratio[turn : turn + 1, :], (SUBLANES, LANES))


def advance(a, b, even, odd, classes, table, turn, sigma, valid_rows, emit):
    length, tiles = a.shape[0], a.shape[1]
    tile = (SUBLANES, LANES)
    lane = lax.broadcasted_iota(jnp.int32, tile, 1)
    sublane = lax.broadcasted_iota(jnp.int32, tile, 0)
    block = sublane % BLOCKS
    at_left, at_right = lane == 0, lane == LANES - 1
    zero = jnp.zeros(tile, jnp.float32)

    def doubled(source, i, rows):
        above, middle, below = rows
        spread, straight = [], []
        for h in range(tiles):
            vertical = above[h] + below[h]
            edge = (2.0 * edge_weight) * middle[h]
            spread.append((2.0 * corner_weight) * vertical + edge)
            straight.append((2.0 * edge_weight) * vertical - (edge + edge))
        from_left = [pltpu.roll(q, 1, 1) for q in spread]
        from_right = [pltpu.roll(q, LANES - 1, 1) for q in spread]
        result = []
        for h in range(tiles):
            left = jnp.where(at_left, from_left[h - 1] if h else zero, from_left[h])
            right = jnp.where(at_right, from_right[h + 1] if h + 1 < tiles else zero, from_right[h])
            result.append((left + right) + straight[h])
        return result

    def sweep(source, target, k, total, first):
        wrap_above = [
            jnp.where(block == 0, zero, pltpu.roll(source[length - 1, h], 1, 0)) for h in range(tiles)
        ]
        wrap_below = [
            jnp.where(block == BLOCKS - 1, zero, pltpu.roll(source[0, h], SUBLANES - 1, 0))
            for h in range(tiles)
        ]
        row = table[turn, k]
        above, middle = wrap_above, [source[0, h] for h in range(tiles)]
        for i in range(length):
            below = [source[i + 1, h] for h in range(tiles)] if i + 1 < length else wrap_below
            result = doubled(source, i, (above, middle, below))
            if valid_rows is not None:
                at = block * length + i
                inside = (at >= valid_rows[0]) & (at < valid_rows[1])
            for h in range(tiles):
                value = 0.5 * result[h] if first else result[h] - target[i, h]
                if valid_rows is not None:
                    value = jnp.where(inside, value, zero)
                target[i, h] = value
                coefficient = jnp.take_along_axis(row, classes[i, h], axis=1, mode="promise_in_bounds")
                term = coefficient * value
                if first:
                    total[i, h] = term
                    start = jnp.take_along_axis(
                        table[turn, 0], classes[i, h], axis=1, mode="promise_in_bounds"
                    )
                    even[i, h] = start * source[i, h]
                else:
                    total[i, h] = total[i, h] + term
            above, middle = middle, below

    sweep(a, b, 1, odd, True)

    def pair(n, carry):
        sweep(b, a, 2 * n, even, False)
        sweep(a, b, 2 * n + 1, odd, False)
        return carry

    lax.fori_loop(1, TERMS // 2, pair, 0)
    turned = jnp.where(sublane < BLOCKS, -sigma, sigma)
    for i in range(length):
        for h in range(tiles):
            emit(i, h, even[i, h] + turned * pltpu.roll(odd[i, h], BLOCKS, 0))


def sign_of(side):
    return jnp.where(side == 0, 1.0, -1.0).astype(jnp.float32)


def gather_blocks(natural, target, count):
    length = target.shape[0]
    for h in range(target.shape[1]):
        for i in range(length):
            target[i, h] = natural[h, pl.ds(PAD + i, count, stride=length), :]


PAD = 8


def windows(natural, length, strip_rows, side, own_ref, send_ref):
    rows = BLOCKS * length
    tall = strip_rows + 2 * MARGIN
    at = lax.broadcasted_iota(jnp.int32, (tall, LANES), 0)
    for ref, strip in ((own_ref, side), (send_ref, 1 - side)):
        begin = strip * strip_rows - MARGIN
        inside = (at + begin >= 0) & (at + begin < rows)
        for component in range(2):
            for h in range(natural.shape[0]):
                found = natural[h, pl.ds(PAD + component * rows + begin, tall), :]
                ref[component, h] = jnp.where(inside, found, 0.0)


def place(natural, source, component, rows, row, count):
    for h in range(natural.shape[0]):
        natural[h, pl.ds(pl.multiple_of(PAD + component * rows + row, 8), count), :] = source[
            :, h * LANES : (h + 1) * LANES
        ]


def split_kernel(in_ref, class_ref, own_ref, send_ref, whole, whole_classes, sem):
    side = lax.axis_index("lat")
    fields = pltpu.make_async_copy(in_ref.at[0], whole, sem.at[0])
    cells = pltpu.make_async_copy(class_ref.at[0], whole_classes, sem.at[1])
    fields.start()
    cells.start()
    cells.wait()
    as_float = whole_classes[...].astype(jnp.float32)
    own_ref[2] = as_float
    send_ref[2] = as_float
    fields.wait()
    for component in range(2):
        own_ref[component] = whole[side * 2 + component]
        send_ref[component] = whole[(1 - side) * 2 + component]


def first_kernel(own_ref, got_ref, table_ref, hand_ref, blocks_ref, mine_ref, send_ref, a, b, even, odd, natural):
    side = lax.axis_index("lat")
    strip_rows = own_ref.shape[1]
    rows = 2 * strip_rows
    length = a.shape[0]
    for component in range(2):
        place(natural, own_ref[2], component, rows, side * strip_rows, strip_rows)
        place(natural, got_ref[2], component, rows, (1 - side) * strip_rows, strip_rows)
    gather_blocks(natural, a, SUBLANES)
    for i in range(length):
        for h in range(a.shape[1]):
            blocks_ref[i, h] = a[i, h].astype(jnp.int32)
    for component in range(2):
        place(natural, own_ref[component], component, rows, side * strip_rows, strip_rows)
        place(natural, got_ref[component], component, rows, (1 - side) * strip_rows, strip_rows)
    gather_blocks(natural, a, SUBLANES)

    def emit(i, h, value):
        hand_ref[i, h] = value
        natural[h, pl.ds(PAD + i, SUBLANES, stride=length), :] = value

    advance(a, b, even, odd, blocks_ref, table_ref, 0, sign_of(side), None, emit)
    windows(natural, length, strip_rows, side, mine_ref, send_ref)


def next_kernel(turn, last, got_ref, enter_ref, enter_got_ref, blocks_ref, table_ref, *rest):
    if last:
        mine_ref, send_ref, a, b, even, odd, natural, strips, sem = rest
        hand_ref = None
    else:
        hand_ref, mine_ref, send_ref, a, b, even, odd, natural, strips, sem = rest
    side = lax.axis_index("lat")
    top = lax.axis_index("depth") == 0
    strip_rows = strips.shape[2]
    rows = 2 * strip_rows
    length = a.shape[0]

    @pl.when(top)
    def _():
        copies = []
        for j, ref in enumerate((enter_ref, enter_got_ref)):
            copies.append(
                pltpu.make_async_copy(ref.at[turn - 1, pl.ds(2 * side, 2)], strips.at[j], sem.at[j])
            )
        for copy in copies:
            copy.start()
        for copy in copies:
            copy.wait()
        for component in range(2):
            place(natural, strips[0, component], component, rows, side * strip_rows, strip_rows)
            place(natural, strips[1, component], component, rows, (1 - side) * strip_rows, strip_rows)
        gather_blocks(natural, a, SUBLANES)

    @pl.when(jnp.logical_not(top))
    def _():
        a[...] = got_ref[...]

    def emit(i, h, value):
        if not last:
            hand_ref[i, h] = value
        natural[h, pl.ds(PAD + i, SUBLANES, stride=length), :] = value

    advance(a, b, even, odd, blocks_ref, table_ref, turn, sign_of(side), None, emit)
    windows(natural, length, strip_rows, side, mine_ref, send_ref)


def image_kernel(*refs):
    pairs = [(refs[2 * t], refs[2 * t + 1]) for t in range(TURNS)]
    images_ref, wave_ref, source, receiver = refs[2 * TURNS :]
    side = lax.axis_index("lat")
    strip_rows = wave_ref.shape[2]
    tiles = source.shape[2]

    @pl.when(side == 0)
    def _():
        for t, (mine, got) in enumerate(pairs):
            source[t] = mine[...]
            receiver[t] = got[...]

    @pl.when(side == 1)
    def _():
        for t, (mine, got) in enumerate(pairs):
            source[t] = got[...]
            receiver[t] = mine[...]

    for h in range(tiles):
        at = slice(h * LANES, (h + 1) * LANES)
        for o in range(OFFSETS):
            lag = o - MARGIN
            total = None
            for t in range(TURNS):
                for component in range(2):
                    product = (
                        source[t, component, h, MARGIN - lag : MARGIN - lag + strip_rows, :]
                        * receiver[t, component, h, MARGIN + lag : MARGIN + lag + strip_rows, :]
                    )
                    total = product if total is None else total + product
            images_ref[0, o, :, at] = total
        for component in range(2):
            rows = slice(MARGIN, MARGIN + strip_rows)
            wave_ref[0, component, :, at] = source[TURNS - 1, component, h, rows, :]
            wave_ref[0, 2 + component, :, at] = receiver[TURNS - 1, component, h, rows, :]


def field_scratch(length, tiles):
    return [pltpu.VMEM((length, tiles, SUBLANES, LANES), jnp.float32)] * 4


def coefficients(freq_phase, class_slowness):
    (table,) = call(
        table_kernel,
        [f32(TURNS, TERMS, SUBLANES, LANES)],
        [SMEM, VMEM],
        [pltpu.VMEM((SUBLANES, LANES), jnp.float32)],
        (freq_phase, class_slowness.reshape(1, -1)),
    )
    return table


def paired(in_flight, entering, classes, freq_phase, class_slowness):
    depth = lax.axis_size("depth")
    _, _, strip_rows, width = in_flight.shape
    tiles = width // LANES
    length = 2 * strip_rows // BLOCKS
    swap = [(0, 1), (1, 0)]
    shift = [(i, i + 1) for i in range(depth - 1)]
    blocks = f32(length, tiles, SUBLANES, LANES)
    window = f32(2, tiles, strip_rows + 2 * MARGIN, LANES)
    natural = pltpu.VMEM((tiles, 2 * BLOCKS * length + 2 * PAD, LANES), jnp.float32)
    strips = f32(3, strip_rows, width)
    flops = 20 * TERMS * 2 * BLOCKS * length * width

    own, send = call(
        split_kernel,
        [strips, strips],
        [ANY, ANY],
        [
            pltpu.VMEM((4, strip_rows, width), jnp.float32),
            pltpu.VMEM((strip_rows, width), jnp.int32),
            pltpu.SemaphoreType.DMA((2,)),
        ],
        (in_flight, classes),
    )
    got = lax.ppermute(send, "lat", swap)
    enter_got = lax.ppermute(entering, ("depth", "lat"), swap)
    table = coefficients(freq_phase, class_slowness)
    hand, cells, mine, send = call(
        first_kernel,
        [blocks, jax.ShapeDtypeStruct(blocks.shape, jnp.int32), window, window],
        [VMEM] * 3,
        field_scratch(length, tiles) + [natural],
        (own, got, table),
        flops,
    )
    pairs = []
    for turn in range(1, TURNS):
        handed = lax.ppermute(hand, "depth", shift)
        pairs += [mine, lax.ppermute(send, "lat", swap)]
        last = turn == TURNS - 1
        outs = call(
            functools.partial(next_kernel, turn, last),
            ([] if last else [blocks]) + [window, window],
            [VMEM, ANY, ANY, VMEM, VMEM],
            field_scratch(length, tiles)
            + [natural, pltpu.VMEM((2, 2, strip_rows, width), jnp.float32), pltpu.SemaphoreType.DMA((2,))],
            (handed, entering, enter_got, cells, table),
            flops,
        )
        if last:
            mine, send = outs
        else:
            hand, mine, send = outs
    pairs += [mine, lax.ppermute(send, "lat", swap)]
    return tuple(
        call(
            image_kernel,
            [f32(1, OFFSETS, strip_rows, width), f32(1, 4, strip_rows, width)],
            [VMEM] * len(pairs),
            [pltpu.VMEM((TURNS, *window.shape), jnp.float32)] * 2,
            pairs,
        )
    )


def inside_kernel(turn, limits_ref, field_ref, blocks_ref, table_ref, out_ref, a, b, even, odd):
    a[...] = field_ref[...]

    def emit(i, h, value):
        out_ref[i, h] = value

    side = lax.axis_index("lat") % 2
    valid = (limits_ref[0], limits_ref[1])
    advance(a, b, even, odd, blocks_ref, table_ref, turn, sign_of(side), valid, emit)


def grouped(in_flight, entering, classes, freq_phase, class_slowness):
    depth, strips = lax.axis_size("depth"), lax.axis_size("lat")
    strip = lax.axis_index("lat")
    side, group = strip % 2, strip // 2
    _, _, strip_rows, width = in_flight.shape
    tiles = width // LANES
    core = 2 * strip_rows
    halo = TERMS - 1 + MARGIN
    while (core + 2 * halo) % BLOCKS:
        halo += 1
    rows = core + 2 * halo
    length = rows // BLOCKS
    swap = [(i, i ^ 1) for i in range(strips)]
    shift = [(i, i + 1) for i in range(depth - 1)]
    blocks = f32(length, tiles, SUBLANES, LANES)

    def both_strips(mine, sent):
        got = lax.ppermute(sent, "lat", swap)
        return jnp.where(
            side == 0, jnp.concatenate([mine, got], 1), jnp.concatenate([got, mine], 1)
        )

    def own_components(fields):
        return both_strips(
            lax.dynamic_slice_in_dim(fields, 2 * side, 2, 0),
            lax.dynamic_slice_in_dim(fields, 2 * (1 - side), 2, 0),
        )

    def with_halo(cells):
        above = lax.ppermute(cells[:, core - halo :], "lat", [(i, i + 2) for i in range(strips - 2)])
        below = lax.ppermute(cells[:, :halo], "lat", [(i + 2, i) for i in range(strips - 2)])
        return jnp.concatenate([above, cells, below], 1)

    def to_blocks(cells):
        split = cells.reshape(2, BLOCKS, length, tiles, LANES)
        return split.transpose(2, 3, 0, 1, 4).reshape(blocks.shape)

    def to_rows(cells):
        split = cells.reshape(length, tiles, 2, BLOCKS, LANES)
        return split.transpose(2, 3, 0, 1, 4).reshape(2, rows, width)

    def window(cells, which):
        begin = halo - MARGIN + which * strip_rows
        return lax.dynamic_slice_in_dim(cells, begin, strip_rows + 2 * MARGIN, 1)

    cells = with_halo(both_strips(classes, classes))
    cells = to_blocks(jnp.concatenate([cells, cells], 0))
    table = coefficients(freq_phase, class_slowness)
    before = group * core - halo
    limits = jnp.stack([jnp.maximum(-before, 0), jnp.minimum(strips * strip_rows - before, rows)])
    field = own_components(in_flight[0])
    images = jnp.zeros((OFFSETS, strip_rows, width), jnp.float32)
    for turn in range(TURNS):
        (advanced,) = call(
            functools.partial(inside_kernel, turn),
            [blocks],
            [SMEM, VMEM, VMEM, VMEM],
            field_scratch(length, tiles),
            (limits.astype(jnp.int32), to_blocks(with_halo(field)), cells, table),
        )
        advanced = to_rows(advanced)
        mine = window(advanced, side)
        got = lax.ppermute(window(advanced, 1 - side), "lat", swap)
        source, receiver = jnp.where(side == 0, mine, got), jnp.where(side == 0, got, mine)
        products = []
        for o in range(OFFSETS):
            lag = o - MARGIN
            first = source[:, MARGIN - lag : MARGIN - lag + strip_rows]
            second = receiver[:, MARGIN + lag : MARGIN + lag + strip_rows]
            products.append(first[0] * second[0] + first[1] * second[1])
        images = images + jnp.stack(products)
        if turn + 1 < TURNS:
            handed = lax.ppermute(advanced[:, halo : halo + core], "depth", shift)
            entered = own_components(entering[turn])
            field = jnp.where(lax.axis_index("depth") == 0, entered, handed)
    own = slice(MARGIN, MARGIN + strip_rows)
    return images[None], jnp.concatenate([source[:, own], receiver[:, own]], 0)[None]


def solution(mesh):
    in_specs = (
        P("depth", None, "lat", None),
        P(None, None, "lat", None),
        P("depth", "lat", None),
        P(),
        P(),
    )
    out_specs = (P("depth", None, "lat", None), P("depth", None, "lat", None))
    local = paired if mesh.shape["lat"] == 2 else grouped
    return jax.shard_map(local, mesh=mesh, in_specs=in_specs, out_specs=out_specs, check_vma=False)
```

profile of v0, /device:TPU:12, one launch (start us, length us, event | category | flops | bytes accessed | tf_op | source)
XLA Modules:
  0.0 39.3 jit_solution(368472746338859139)
XLA Ops:
  0.6 0.7 %collective-permute-start.3 = (f32[2,4,32,256]{3,2,1,0:T(8,128)}, f32[2,4,32,256]{3,2,1,0:T(8,128)S(1)}, u32[]{:S(2)}, u32[]{:S(2)}) collective-permute-start(f32[2,4,32,256]{3,2,1,0:T(8,128)} %enter_ref.3), channel_id=1, source_target_pairs={{0,1},{1,0}} | collective-permute-start | bytes 786440 | tf_op jit(solution)/shard_map/ppermute | solution.py:340
  1.3 0.0 copy-start.1
  1.3 0.9 %copy-done.1 = f32[1,4,32,256]{3,2,1,0:T(8,128)S(1)} copy-done((f32[1,4,32,256]{3,2,1,0:T(8,128)S(1)}, f32[1,4,32,256]{3,2,1,0:T(8,128)}, u32[]{:S(2)}) %copy-start.1) | copy-done | bytes 131096
  2.2 0.0 copy-start.2
  2.2 0.8 %copy-done.2 = s32[1,32,256]{2,1,0:T(8,128)S(1)} copy-done((s32[1,32,256]{2,1,0:T(8,128)S(1)}, s32[1,32,256]{2,1,0:T(8,128)}, u32[]{:S(2)}) %copy-start.2) | copy-done | bytes 32792
  3.0 0.2 shard_map.68
  3.2 0.0 copy-start.3
  3.2 0.0 copy-start.4
  3.2 0.6 %collective-permute-start = (f32[3,32,256]{2,1,0:T(8,128)S(1)}, f32[3,32,256]{2,1,0:T(8,128)S(1)}, u32[]{:S(2)}, u32[]{:S(2)}) collective-permute-start(f32[3,32,256]{2,1,0:T(8,128)S(1)} %get-tuple-element.14), channel_id=1, source_target_pairs={{0,1},{1,0},{2,3},{3,2},{4,5},{5,4},{6,7},{7,6},{8,9},{9,8},{10,11... | collective-permute-start | bytes 294920 | tf_op jit(solution)/shard_map/ppermute | solution.py:339
  3.8 0.1 copy-done.3
  3.9 0.0 copy-done.4
  3.9 0.0 copy-start
  3.9 0.7 %shard_map.69.table_ref = f32[3,16,8,128]{3,2,1,0:T(8,128)S(1)} custom-call(f32[18]{0:T(128)S(1)} %copy-done.3, f32[1,32]{1,0:T(1,128)S(1)} %bitcast.1), custom_call_target="tpu_custom_call" | custom-call | bytes 196808 | tf_op jit(solution)/shard_map/pallas_call | solution.py:31
  4.5 3.4 %collective-permute-done.got_ref = f32[3,32,256]{2,1,0:T(8,128)S(1)} collective-permute-done((f32[3,32,256]{2,1,0:T(8,128)S(1)}, f32[3,32,256]{2,1,0:T(8,128)S(1)}, u32[]{:S(2)}, u32[]{:S(2)}) %collective-permute-start) | collective-permute-done | bytes 98336 | tf_op jit(solution)/shard_map/ppermute | solution.py:339
  7.9 3.9 %shard_map.70 = (f32[16,2,8,128]{3,2,1,0:T(8,128)S(1)}, s32[16,2,8,128]{3,2,1,0:T(8,128)S(1)}, f32[2,2,40,128]{3,2,1,0:T(8,128)S(1)}, f32[2,2,40,128]{3,2,1,0:T(8,128)S(1)}) custom-call(f32[3,32,256]{2,1,0:T(8,128)S(1)} %get-tuple-element.13.own_ref, f32[3,32,256]{2,1,0:T(8,128)S(1)} %collective-permute-done.got_ref, f32[3,16,8,128]{3,2,1,0:T(8,128)S(1)} %shard_map.69.table_ref), custom_call_target="tpu_custom_call" | custom-call | flops 10485760 | bytes 819200 | tf_op jit(solution)/shard_map/pallas_call | solution.py:31
  11.8 1.9 %collective-permute-start.2 = (f32[16,2,8,128]{3,2,1,0:T(8,128)S(1)}, f32[16,2,8,128]{3,2,1,0:T(8,128)S(1)}, u32[]{:S(2)}, u32[]{:S(2)}) collective-permute-start(f32[16,2,8,128]{3,2,1,0:T(8,128)S(1)} %get-tuple-element.17), channel_id=1, source_target_pairs={{0,2},{2,4},{4,6},{6,8},{8,10},{10,12},{12,14},{14,16},{16,18},{18... | collective-permute-start | bytes 393224 | tf_op jit(solution)/shard_map/ppermute | solution.py:352
  13.7 5.3 %collective-permute-done.2.got_ref = f32[16,2,8,128]{3,2,1,0:T(8,128)S(1)} collective-permute-done((f32[16,2,8,128]{3,2,1,0:T(8,128)S(1)}, f32[16,2,8,128]{3,2,1,0:T(8,128)S(1)}, u32[]{:S(2)}, u32[]{:S(2)}) %collective-permute-start.2) | collective-permute-done | bytes 131104 | tf_op jit(solution)/shard_map/ppermute | solution.py:352
  19.0 0.0 collective-permute-done.3.enter_got_ref
  19.0 0.0 copy-done
  19.0 3.8 %shard_map.71 = (f32[16,2,8,128]{3,2,1,0:T(8,128)S(1)}, f32[2,2,40,128]{3,2,1,0:T(8,128)S(1)}, f32[2,2,40,128]{3,2,1,0:T(8,128)S(1)}) custom-call(f32[16,2,8,128]{3,2,1,0:T(8,128)S(1)} %collective-permute-done.2.got_ref, f32[2,4,32,256]{3,2,1,0:T(8,128)S(1)} %copy-done, f32[2,4,32,256]{3,2,1,0:T(8,128)S(1)} %collective-permute-done.3.enter_got_ref, ...), custom_call_target="tpu_custom_call" | custom-call | flops 10485760 | bytes 1277952 | tf_op jit(solution)/shard_map/pallas_call | solution.py:31
  22.9 1.9 %collective-permute-start.5 = (f32[16,2,8,128]{3,2,1,0:T(8,128)S(1)}, f32[16,2,8,128]{3,2,1,0:T(8,128)S(1)}, u32[]{:S(2)}, u32[]{:S(2)}) collective-permute-start(f32[16,2,8,128]{3,2,1,0:T(8,128)S(1)} %get-tuple-element.21), channel_id=1, source_target_pairs={{0,2},{2,4},{4,6},{6,8},{8,10},{10,12},{12,14},{14,16},{16,18},{18... | collective-permute-start | bytes 393224 | tf_op jit(solution)/shard_map/ppermute | solution.py:352
  24.8 0.6 %collective-permute-start.1 = (f32[2,2,40,128]{3,2,1,0:T(8,128)S(1)}, f32[2,2,40,128]{3,2,1,0:T(8,128)S(1)}, u32[]{:S(2)}, u32[]{:S(2)}) collective-permute-start(f32[2,2,40,128]{3,2,1,0:T(8,128)S(1)} %get-tuple-element.16), channel_id=1, source_target_pairs={{0,1},{1,0},{2,3},{3,2},{4,5},{5,4},{6,7},{7,6},{8,9},{9,8},{10,11... | collective-permute-start | bytes 245768 | tf_op jit(solution)/shard_map/ppermute | solution.py:353
  25.4 1.5 %collective-permute-start.4 = (f32[2,2,40,128]{3,2,1,0:T(8,128)S(1)}, f32[2,2,40,128]{3,2,1,0:T(8,128)S(1)}, u32[]{:S(2)}, u32[]{:S(2)}) collective-permute-start(f32[2,2,40,128]{3,2,1,0:T(8,128)S(1)} %get-tuple-element.20), channel_id=1, source_target_pairs={{0,1},{1,0},{2,3},{3,2},{4,5},{5,4},{6,7},{7,6},{8,9},{9,8},{10,11... | collective-permute-start | bytes 245768 | tf_op jit(solution)/shard_map/ppermute | solution.py:353
  26.9 3.2 %collective-permute-done.5.got_ref = f32[16,2,8,128]{3,2,1,0:T(8,128)S(1)} collective-permute-done((f32[16,2,8,128]{3,2,1,0:T(8,128)S(1)}, f32[16,2,8,128]{3,2,1,0:T(8,128)S(1)}, u32[]{:S(2)}, u32[]{:S(2)}) %collective-permute-start.5) | collective-permute-done | bytes 131104 | tf_op jit(solution)/shard_map/ppermute | solution.py:352
  30.0 3.8 %shard_map.72 = (f32[2,2,40,128]{3,2,1,0:T(8,128)S(1)}, f32[2,2,40,128]{3,2,1,0:T(8,128)S(1)}) custom-call(f32[16,2,8,128]{3,2,1,0:T(8,128)S(1)} %collective-permute-done.5.got_ref, f32[2,4,32,256]{3,2,1,0:T(8,128)S(1)} %copy-done, f32[2,4,32,256]{3,2,1,0:T(8,128)S(1)} %collective-permute-done.3.enter_got_ref, ...), custom_call_target="tpu_custom_call" | custom-call | flops 10485760 | bytes 1146880 | tf_op jit(solution)/shard_map/pallas_call | solution.py:31
  33.9 0.6 %collective-permute-start.6 = (f32[2,2,40,128]{3,2,1,0:T(8,128)S(1)}, f32[2,2,40,128]{3,2,1,0:T(8,128)S(1)}, u32[]{:S(2)}, u32[]{:S(2)}) collective-permute-start(f32[2,2,40,128]{3,2,1,0:T(8,128)S(1)} %get-tuple-element.23), channel_id=1, source_target_pairs={{0,1},{1,0},{2,3},{3,2},{4,5},{5,4},{6,7},{7,6},{8,9},{9,8},{10,11... | collective-permute-start | bytes 245768 | tf_op jit(solution)/shard_map/ppermute | solution.py:368
  34.5 0.0 collective-permute-done.1.refs_1_
  34.5 0.0 collective-permute-done.4.refs_3_
  34.5 3.9 %collective-permute-done.6.refs_5_ = f32[2,2,40,128]{3,2,1,0:T(8,128)S(1)} collective-permute-done((f32[2,2,40,128]{3,2,1,0:T(8,128)S(1)}, f32[2,2,40,128]{3,2,1,0:T(8,128)S(1)}, u32[]{:S(2)}, u32[]{:S(2)}) %collective-permute-start.6) | collective-permute-done | bytes 81952 | tf_op jit(solution)/shard_map/ppermute | solution.py:368
  38.4 0.9 %shard_map.73 = (f32[1,8,32,256]{3,2,1,0:T(8,128)}, f32[1,4,32,256]{3,2,1,0:T(8,128)}) custom-call(f32[2,2,40,128]{3,2,1,0:T(8,128)S(1)} %get-tuple-element.15.refs_0_, f32[2,2,40,128]{3,2,1,0:T(8,128)S(1)} %collective-permute-done.1.refs_1_, f32[2,2,40,128]{3,2,1,0:T(8,128)S(1)} %get-tuple-element.19.refs_2_, ...), custom_call_target="tpu_custom_call" | custom-call | bytes 884736 | tf_op jit(solution)/shard_map/pallas_call | solution.py:31
Async XLA Ops:
  0.6 18.4 %collective-permute-start.3 = (f32[2,4,32,256]{3,2,1,0:T(8,128)}, f32[2,4,32,256]{3,2,1,0:T(8,128)S(1)}, u32[]{:S(2)}, u32[]{:S(2)}) collective-permute-start(f32[2,4,32,256]{3,2,1,0:T(8,128)} %enter_ref.3), channel_id=1, source_target_pairs={{0,1},{1,0}} | collective-permute-start | bytes 786440 | tf_op jit(solution)/shard_map/ppermute | solution.py:340
  1.3 0.9 %copy-start.1 = (f32[1,4,32,256]{3,2,1,0:T(8,128)S(1)}, f32[1,4,32,256]{3,2,1,0:T(8,128)}, u32[]{:S(2)}) copy-start(f32[1,4,32,256]{3,2,1,0:T(8,128)} %in_ref.1) | copy-start | bytes 393220
  2.2 0.8 %copy-start.2 = (s32[1,32,256]{2,1,0:T(8,128)S(1)}, s32[1,32,256]{2,1,0:T(8,128)}, u32[]{:S(2)}) copy-start(s32[1,32,256]{2,1,0:T(8,128)} %class_ref.1) | copy-start | bytes 98308
  3.2 0.7 %copy-start.3 = (f32[18]{0:T(128)S(1)}, f32[18]{0:T(128)}, u32[]{:S(2)}) copy-start(f32[18]{0:T(128)} %phase_ref.1) | copy-start | bytes 220
  3.2 0.7 %copy-start.4 = (f32[32]{0:T(128)S(1)}, f32[32]{0:T(128)}, u32[]{:S(2)}) copy-start(f32[32]{0:T(128)} %param.9) | copy-start | bytes 388
  3.2 4.7 %collective-permute-start = (f32[3,32,256]{2,1,0:T(8,128)S(1)}, f32[3,32,256]{2,1,0:T(8,128)S(1)}, u32[]{:S(2)}, u32[]{:S(2)}) collective-permute-start(f32[3,32,256]{2,1,0:T(8,128)S(1)} %get-tuple-element.14), channel_id=1, source_target_pairs={{0,1},{1,0},{2,3},{3,2},{4,5},{5,4},{6,7},{7,6},{8,9},{9,8},{10,11... | collective-permute-start | bytes 294920 | tf_op jit(solution)/shard_map/ppermute | solution.py:339
  3.9 15.1 %copy-start = (f32[2,4,32,256]{3,2,1,0:T(8,128)S(1)}, f32[2,4,32,256]{3,2,1,0:T(8,128)}, u32[]{:S(2)}) copy-start(f32[2,4,32,256]{3,2,1,0:T(8,128)} %enter_ref.3) | copy-start | bytes 786436
  11.8 7.2 %collective-permute-start.2 = (f32[16,2,8,128]{3,2,1,0:T(8,128)S(1)}, f32[16,2,8,128]{3,2,1,0:T(8,128)S(1)}, u32[]{:S(2)}, u32[]{:S(2)}) collective-permute-start(f32[16,2,8,128]{3,2,1,0:T(8,128)S(1)} %get-tuple-element.17), channel_id=1, source_target_pairs={{0,2},{2,4},{4,6},{6,8},{8,10},{10,12},{12,14},{14,16},{16,18},{18... | collective-permute-start | bytes 393224 | tf_op jit(solution)/shard_map/ppermute | solution.py:352
  22.9 7.2 %collective-permute-start.5 = (f32[16,2,8,128]{3,2,1,0:T(8,128)S(1)}, f32[16,2,8,128]{3,2,1,0:T(8,128)S(1)}, u32[]{:S(2)}, u32[]{:S(2)}) collective-permute-start(f32[16,2,8,128]{3,2,1,0:T(8,128)S(1)} %get-tuple-element.21), channel_id=1, source_target_pairs={{0,2},{2,4},{4,6},{6,8},{8,10},{10,12},{12,14},{14,16},{16,18},{18... | collective-permute-start | bytes 393224 | tf_op jit(solution)/shard_map/ppermute | solution.py:352
  24.8 9.7 %collective-permute-start.1 = (f32[2,2,40,128]{3,2,1,0:T(8,128)S(1)}, f32[2,2,40,128]{3,2,1,0:T(8,128)S(1)}, u32[]{:S(2)}, u32[]{:S(2)}) collective-permute-start(f32[2,2,40,128]{3,2,1,0:T(8,128)S(1)} %get-tuple-element.16), channel_id=1, source_target_pairs={{0,1},{1,0},{2,3},{3,2},{4,5},{5,4},{6,7},{7,6},{8,9},{9,8},{10,11... | collective-permute-start | bytes 245768 | tf_op jit(solution)/shard_map/ppermute | solution.py:353
  25.4 9.1 %collective-permute-start.4 = (f32[2,2,40,128]{3,2,1,0:T(8,128)S(1)}, f32[2,2,40,128]{3,2,1,0:T(8,128)S(1)}, u32[]{:S(2)}, u32[]{:S(2)}) collective-permute-start(f32[2,2,40,128]{3,2,1,0:T(8,128)S(1)} %get-tuple-element.20), channel_id=1, source_target_pairs={{0,1},{1,0},{2,3},{3,2},{4,5},{5,4},{6,7},{7,6},{8,9},{9,8},{10,11... | collective-permute-start | bytes 245768 | tf_op jit(solution)/shard_map/ppermute | solution.py:353
  33.9 4.5 %collective-permute-start.6 = (f32[2,2,40,128]{3,2,1,0:T(8,128)S(1)}, f32[2,2,40,128]{3,2,1,0:T(8,128)S(1)}, u32[]{:S(2)}, u32[]{:S(2)}) collective-permute-start(f32[2,2,40,128]{3,2,1,0:T(8,128)S(1)} %get-tuple-element.23), channel_id=1, source_target_pairs={{0,1},{1,0},{2,3},{3,2},{4,5},{5,4},{6,7},{7,6},{8,9},{9,8},{10,11... | collective-permute-start | bytes 245768 | tf_op jit(solution)/shard_map/ppermute | solution.py:368
where the time goes:
time: 39.6 us; the launch traced here: 39.3 us
  waiting for transfers between devices  15.7 us (40%)
  Pallas kernels  13.4 us (34%)
  starting transfers between devices  7.75 us (20%)
  local copies, waits for them, and re-layouts  1.74 us (4%)
  between operations  0.73 us (2%)
    pallas_call x6, Pallas kernels, call(): pl.pallas_call(kernel, out_shape=outs, in_specs=in_specs, out_specs=[VMEM...  13.4 us
    ppermute x2, waiting for transfers between devices, paired(): handed = lax.ppermute(hand, 'depth', shift)  8.42 us
    ppermute x3, waiting for transfers between devices, paired(): pairs += [mine, lax.ppermute(send, 'lat', swap)]  3.93 us
    ppermute x2, starting transfers between devices, paired(): handed = lax.ppermute(hand, 'depth', shift)  3.84 us
    ppermute x1, waiting for transfers between devices, paired(): got = lax.ppermute(send, 'lat', swap)  3.36 us
    ppermute x3, starting transfers between devices, paired(): pairs += [mine, lax.ppermute(send, 'lat', swap)]  2.66 us
    unnamed x10, local copies, waits for them, and re-layouts  1.74 us
  transfers between devices with their start and end apart: 7, of which 4 were waited for; matrix products, arithmetic and copies ran while one was open for 0% of the time, Pallas kernels for 22%

commit v1 on v0

--- a/solution.py
+++ b/solution.py
@@ -12,7 +12,8 @@
 TURNS = 3
 LANES = 128
 SUBLANES = 8
-BLOCKS = 4
+PLANE = 4
+BLOCKS = 8
 MARGIN = OFFSETS // 2
 VMEM_BYTES = 4 << 20
 
@@ -23,6 +24,7 @@
 
 VMEM = pl.BlockSpec(memory_space=pltpu.VMEM)
 SMEM = pl.BlockSpec(memory_space=pltpu.SMEM)
+HBM = pl.BlockSpec(memory_space=pltpu.HBM)
 ANY = pl.BlockSpec(memory_space=pl.ANY)
 
 
@@ -39,11 +41,23 @@
     )(*args)
 
 
+def in_hbm(*arrays):
+    return tuple(pltpu.with_memory_space_constraint(x, pltpu.HBM) for x in arrays)
+
+
 def f32(*shape):
     return jax.ShapeDtypeStruct(shape, jnp.float32)
 
 
-def table_kernel(phase_ref, slow_ref, out_ref, z_ref):
+def table_kernel(phase_hbm, slow_hbm, out_ref, z_ref, phase_ref, slow_ref, sem):
+    copies = [
+        pltpu.make_async_copy(phase_hbm, phase_ref, sem.at[0]),
+        pltpu.make_async_copy(slow_hbm, slow_ref, sem.at[1]),
+    ]
+    for copy in copies:
+        copy.start()
+    for copy in copies:
+        copy.wait()
     first = lax.axis_size("depth") - 1 - lax.axis_index("depth")
     classes = slow_ref.shape[1]
     z_ref[...] = jnp.full(z_ref.shape, 6.0, jnp.float32)
@@ -70,17 +84,28 @@
             out_ref[turn, k] = jnp.broadcast_to(ratio[turn : turn + 1, :], (SUBLANES, LANES))
 
 
-def advance(a, b, even, odd, classes, table, turn, sigma, valid_rows, emit):
-    length, tiles = a.shape[0], a.shape[1]
+def pick(row, classes):
+    dimensions = lax.GatherDimensionNumbers(
+        offset_dims=(),
+        collapsed_slice_dims=(1,),
+        start_index_map=(1,),
+        operand_batching_dims=(0,),
+        start_indices_batching_dims=(0,),
+    )
+    return lax.gather(
+        row, classes[..., None], dimensions, (1, 1), mode=lax.GatherScatterMode.PROMISE_IN_BOUNDS
+    )
+
+
+def advance(a, b, total, classes, table, turn, sigma, valid_rows, emit):
+    length, tiles = a.shape[1], a.shape[2]
     tile = (SUBLANES, LANES)
     lane = lax.broadcasted_iota(jnp.int32, tile, 1)
-    sublane = lax.broadcasted_iota(jnp.int32, tile, 0)
-    block = sublane % BLOCKS
+    block = lax.broadcasted_iota(jnp.int32, tile, 0)
     at_left, at_right = lane == 0, lane == LANES - 1
     zero = jnp.zeros(tile, jnp.float32)
 
-    def doubled(source, i, rows):
-        above, middle, below = rows
+    def doubled(above, middle, below):
         spread, straight = [], []
         for h in range(tiles):
             vertical = above[h] + below[h]
@@ -96,62 +121,84 @@
             result.append((left + right) + straight[h])
         return result
 
-    def sweep(source, target, k, total, first):
-        wrap_above = [
-            jnp.where(block == 0, zero, pltpu.roll(source[length - 1, h], 1, 0)) for h in range(tiles)
-        ]
-        wrap_below = [
-            jnp.where(block == BLOCKS - 1, zero, pltpu.roll(source[0, h], SUBLANES - 1, 0))
-            for h in range(tiles)
-        ]
+    def sweep(source, target, k, odd, first):
+        def row_of(c, i):
+            if i < 0:
+                return [
+                    jnp.where(block == 0, zero, pltpu.roll(source[c, length - 1, h], 1, 0))
+                    for h in range(tiles)
+                ]
+            if i == length:
+                return [
+                    jnp.where(block == BLOCKS - 1, zero, pltpu.roll(source[c, 0, h], SUBLANES - 1, 0))
+                    for h in range(tiles)
+                ]
+            return [source[c, i, h] for h in range(tiles)]
+
         row = table[turn, k]
-        above, middle = wrap_above, [source[0, h] for h in range(tiles)]
+        if odd:
+            row = row * sigma
+        near = [(row_of(c, -1), row_of(c, 0)) for c in range(2)]
         for i in range(length):
-            below = [source[i + 1, h] for h in range(tiles)] if i + 1 < length else wrap_below
-            result = doubled(source, i, (above, middle, below))
             if valid_rows is not None:
                 at = block * length + i
                 inside = (at >= valid_rows[0]) & (at < valid_rows[1])
+            values = []
+            for c in range(2):
+                above, middle = near[c]
+                below = row_of(c, i + 1)
+                near[c] = (middle, below)
+                result = doubled(above, middle, below)
+                for h in range(tiles):
+                    value = 0.5 * result[h] if first else result[h] - target[c, i, h]
+                    if valid_rows is not None:
+                        value = jnp.where(inside, value, zero)
+                    target[c, i, h] = value
+                    result[h] = value
+                values.append(result)
             for h in range(tiles):
-                value = 0.5 * result[h] if first else result[h] - target[i, h]
-                if valid_rows is not None:
-                    value = jnp.where(inside, value, zero)
-                target[i, h] = value
-                coefficient = jnp.take_along_axis(row, classes[i, h], axis=1, mode="promise_in_bounds")
-                term = coefficient * value
+                at_class = classes[i, h]
+                coefficient = pick(row, at_class)
                 if first:
-                    total[i, h] = term
-                    start = jnp.take_along_axis(
-                        table[turn, 0], classes[i, h], axis=1, mode="promise_in_bounds"
-                    )
-                    even[i, h] = start * source[i, h]
+                    start = pick(table[turn, 0], at_class)
+                    sums = [start * source[c, i, h] for c in range(2)]
                 else:
-                    total[i, h] = total[i, h] + term
-            above, middle = middle, below
-
-    sweep(a, b, 1, odd, True)
+                    sums = [total[c, i, h] for c in range(2)]
+                if odd:
+                    total[0, i, h] = sums[0] - coefficient * values[1][h]
+                    total[1, i, h] = sums[1] + coefficient * values[0][h]
+                else:
+                    total[0, i, h] = sums[0] + coefficient * values[0][h]
+                    total[1, i, h] = sums[1] + coefficient * values[1][h]
+
+    sweep(a, b, 1, True, True)
 
     def pair(n, carry):
-        sweep(b, a, 2 * n, even, False)
-        sweep(a, b, 2 * n + 1, odd, False)
+        sweep(b, a, 2 * n, False, False)
+        sweep(a, b, 2 * n + 1, True, False)
         return carry
 
     lax.fori_loop(1, TERMS // 2, pair, 0)
-    turned = jnp.where(sublane < BLOCKS, -sigma, sigma)
-    for i in range(length):
-        for h in range(tiles):
-            emit(i, h, even[i, h] + turned * pltpu.roll(odd[i, h], BLOCKS, 0))
+    for c in range(2):
+        for i in range(length):
+            for h in range(tiles):
+                emit(c, i, h, total[c, i, h])
 
 
 def sign_of(side):
     return jnp.where(side == 0, 1.0, -1.0).astype(jnp.float32)
 
 
-def gather_blocks(natural, target, count):
-    length = target.shape[0]
-    for h in range(target.shape[1]):
+def block_of(natural, c, i, h, length):
+    return natural[h, pl.ds(PAD + c * BLOCKS * length + i, BLOCKS, stride=length), :]
+
+
+def gather_blocks(natural, target):
+    length = target.shape[1]
+    for c in range(2):
         for i in range(length):
-            target[i, h] = natural[h, pl.ds(PAD + i, count, stride=length), :]
+            for h in range(target.shape[2]):
+                target[c, i, h] = block_of(natural, c, i, h, length)
 
 
 PAD = 8
@@ -193,70 +240,94 @@
         send_ref[component] = whole[(1 - side) * 2 + component]
 
 
-def first_kernel(own_ref, got_ref, table_ref, hand_ref, blocks_ref, mine_ref, send_ref, a, b, even, odd, natural):
+def pack(strips, target):
+    for component in range(2):
+        for j in range(strips.shape[1] // SUBLANES):
+            for h in range(target.shape[2]):
+                at = (component, slice(j * SUBLANES, (j + 1) * SUBLANES), slice(h * LANES, (h + 1) * LANES))
+                target[component, j, h] = strips[at]
+
+
+def unpack(source, natural, component, rows, row, count):
+    for h in range(natural.shape[0]):
+        for j in range(count // SUBLANES):
+            at = pl.multiple_of(PAD + component * rows + row + j * SUBLANES, 8)
+            natural[h, pl.ds(at, SUBLANES), :] = source[component, j, h]
+
+
+def turn_of(turn, a, b, total, natural, blocks_ref, table_ref, enter_ref, strip, sem, outs):
+    side = lax.axis_index("lat")
+    length = a.shape[1]
+    rows = BLOCKS * length
+    mine_ref, send_ref = outs[-2:]
+    last = len(outs) == 2
+    top = lax.axis_index("depth") == 0
+    if not last:
+        hand_ref, cross_ref = outs[:2]
+        fetch = pltpu.make_async_copy(enter_ref.at[turn, pl.ds(2 * (1 - side), 2)], strip, sem)
+        fetch.start()
+
+    def emit(c, i, h, value):
+        if not last:
+            hand_ref[c, i, h] = value
+            cross_ref[c, i, h] = value
+        natural[h, pl.ds(PAD + c * rows + i, BLOCKS, stride=length), :] = value
+
+    advance(a, b, total, blocks_ref, table_ref, turn, sign_of(side), None, emit)
+    windows(natural, length, rows // 2, side, mine_ref, send_ref)
+    if not last:
+        fetch.wait()
+
+        @pl.when(top)
+        def _():
+            pack(strip, cross_ref)
+
+
+def first_kernel(own_ref, got_ref, table_ref, enter_ref, *rest):
+    hand_ref, cross_ref, blocks_ref, mine_ref, send_ref, a, b, total, natural, strip, sem = rest
     side = lax.axis_index("lat")
     strip_rows = own_ref.shape[1]
     rows = 2 * strip_rows
-    length = a.shape[0]
-    for component in range(2):
-        place(natural, own_ref[2], component, rows, side * strip_rows, strip_rows)
-        place(natural, got_ref[2], component, rows, (1 - side) * strip_rows, strip_rows)
-    gather_blocks(natural, a, SUBLANES)
+    length = a.shape[1]
+    place(natural, own_ref[2], 0, rows, side * strip_rows, strip_rows)
+    place(natural, got_ref[2], 0, rows, (1 - side) * strip_rows, strip_rows)
     for i in range(length):
-        for h in range(a.shape[1]):
-            blocks_ref[i, h] = a[i, h].astype(jnp.int32)
+        for h in range(a.shape[2]):
+            blocks_ref[i, h] = block_of(natural, 0, i, h, length).astype(jnp.int32)
     for component in range(2):
         place(natural, own_ref[component], component, rows, side * strip_rows, strip_rows)
         place(natural, got_ref[component], component, rows, (1 - side) * strip_rows, strip_rows)
-    gather_blocks(natural, a, SUBLANES)
-
-    def emit(i, h, value):
-        hand_ref[i, h] = value
-        natural[h, pl.ds(PAD + i, SUBLANES, stride=length), :] = value
-
-    advance(a, b, even, odd, blocks_ref, table_ref, 0, sign_of(side), None, emit)
-    windows(natural, length, strip_rows, side, mine_ref, send_ref)
-
-
-def next_kernel(turn, last, got_ref, enter_ref, enter_got_ref, blocks_ref, table_ref, *rest):
-    if last:
-        mine_ref, send_ref, a, b, even, odd, natural, strips, sem = rest
-        hand_ref = None
-    else:
-        hand_ref, mine_ref, send_ref, a, b, even, odd, natural, strips, sem = rest
+    gather_blocks(natural, a)
+    outs = (hand_ref, cross_ref, mine_ref, send_ref)
+    turn_of(0, a, b, total, natural, blocks_ref, table_ref, enter_ref, strip, sem.at[0], outs)
+
+
+def next_kernel(turn, plane, got_ref, crossed_ref, blocks_ref, table_ref, enter_ref, *rest):
+    *outs, a, b, total, natural, strip, sem = rest
     side = lax.axis_index("lat")
-    top = lax.axis_index("depth") == 0
-    strip_rows = strips.shape[2]
+    slab = lax.axis_index("depth")
+    strip_rows = strip.shape[1]
     rows = 2 * strip_rows
-    length = a.shape[0]
-
-    @pl.when(top)
+
+    @pl.when(slab == 0)
     def _():
-        copies = []
-        for j, ref in enumerate((enter_ref, enter_got_ref)):
-            copies.append(
-                pltpu.make_async_copy(ref.at[turn - 1, pl.ds(2 * side, 2)], strips.at[j], sem.at[j])
-            )
-        for copy in copies:
-            copy.start()
-        for copy in copies:
-            copy.wait()
+        fetch = pltpu.make_async_copy(enter_ref.at[turn - 1, pl.ds(2 * side, 2)], strip, sem.at[1])
+        fetch.start()
+        fetch.wait()
         for component in range(2):
-            place(natural, strips[0, component], component, rows, side * strip_rows, strip_rows)
-            place(natural, strips[1, component], component, rows, (1 - side) * strip_rows, strip_rows)
-        gather_blocks(natural, a, SUBLANES)
-
-    @pl.when(jnp.logical_not(top))
+            place(natural, strip[component], component, rows, side * strip_rows, strip_rows)
+            unpack(crossed_ref, natural, component, rows, (1 - side) * strip_rows, strip_rows)
+        gather_blocks(natural, a)
+
+    @pl.when((slab > 0) & (slab % plane == 0))
+    def _():
+        a[...] = crossed_ref[...]
+
+    @pl.when(slab % plane > 0)
     def _():
         a[...] = got_ref[...]
 
-    def emit(i, h, value):
-        if not last:
-            hand_ref[i, h] = value
-        natural[h, pl.ds(PAD + i, SUBLANES, stride=length), :] = value
-
-    advance(a, b, even, odd, blocks_ref, table_ref, turn, sign_of(side), None, emit)
-    windows(natural, length, strip_rows, side, mine_ref, send_ref)
+    turn_of(turn, a, b, total, natural, blocks_ref, table_ref, enter_ref, strip, sem.at[0], outs)
 
 
 def image_kernel(*refs):
@@ -298,16 +369,21 @@
 
 
 def field_scratch(length, tiles):
-    return [pltpu.VMEM((length, tiles, SUBLANES, LANES), jnp.float32)] * 4
+    return [pltpu.VMEM((2, length, tiles, BLOCKS, LANES), jnp.float32)] * 3
 
 
 def coefficients(freq_phase, class_slowness):
     (table,) = call(
         table_kernel,
         [f32(TURNS, TERMS, SUBLANES, LANES)],
-        [SMEM, VMEM],
-        [pltpu.VMEM((SUBLANES, LANES), jnp.float32)],
-        (freq_phase, class_slowness.reshape(1, -1)),
+        [HBM, HBM],
+        [
+            pltpu.VMEM((SUBLANES, LANES), jnp.float32),
+            pltpu.SMEM(freq_phase.shape, jnp.float32),
+            pltpu.VMEM((1, class_slowness.shape[0]), jnp.float32),
+            pltpu.SemaphoreType.DMA((2,)),
+        ],
+        in_hbm(freq_phase, class_slowness.reshape(1, -1)),
     )
     return table
 
@@ -318,53 +394,67 @@
     tiles = width // LANES
     length = 2 * strip_rows // BLOCKS
     swap = [(0, 1), (1, 0)]
-    shift = [(i, i + 1) for i in range(depth - 1)]
-    blocks = f32(length, tiles, SUBLANES, LANES)
+    plane = PLANE if depth % PLANE == 0 else depth
+    ring = [(i, i - i % plane + (i + 1) % plane) for i in range(depth)]
+    across = {}
+    for first in range(plane, depth, plane):
+        across[first - 1], across[first] = first, first - 1
+    cross = [
+        (2 * d + c, 2 * across[d] + c if d in across else 2 * d + 1 - c)
+        for d in range(depth)
+        for c in range(2)
+    ]
+    blocks = f32(2, length, tiles, BLOCKS, LANES)
     window = f32(2, tiles, strip_rows + 2 * MARGIN, LANES)
     natural = pltpu.VMEM((tiles, 2 * BLOCKS * length + 2 * PAD, LANES), jnp.float32)
+    scratch = field_scratch(length, tiles) + [
+        natural,
+        pltpu.VMEM((2, strip_rows, width), jnp.float32),
+        pltpu.SemaphoreType.DMA((2,)),
+    ]
     strips = f32(3, strip_rows, width)
-    flops = 20 * TERMS * 2 * BLOCKS * length * width
+    flops = 20 * TERMS * 4 * strip_rows * width
 
     own, send = call(
         split_kernel,
         [strips, strips],
-        [ANY, ANY],
+        [HBM, HBM],
         [
             pltpu.VMEM((4, strip_rows, width), jnp.float32),
             pltpu.VMEM((strip_rows, width), jnp.int32),
             pltpu.SemaphoreType.DMA((2,)),
         ],
-        (in_flight, classes),
+        in_hbm(in_flight, classes),
     )
     got = lax.ppermute(send, "lat", swap)
-    enter_got = lax.ppermute(entering, ("depth", "lat"), swap)
+    freq_phase, _ = lax.optimization_barrier((freq_phase, own))
     table = coefficients(freq_phase, class_slowness)
-    hand, cells, mine, send = call(
+    hand, over, cells, mine, send = call(
         first_kernel,
-        [blocks, jax.ShapeDtypeStruct(blocks.shape, jnp.int32), window, window],
-        [VMEM] * 3,
-        field_scratch(length, tiles) + [natural],
-        (own, got, table),
+        [blocks, blocks, jax.ShapeDtypeStruct(blocks.shape[1:], jnp.int32), window, window],
+        [VMEM, VMEM, VMEM, HBM],
+        scratch,
+        (own, got, table, entering),
         flops,
     )
     pairs = []
     for turn in range(1, TURNS):
-        handed = lax.ppermute(hand, "depth", shift)
+        handed = lax.ppermute(hand, "depth", ring)
+        crossed = lax.ppermute(over, ("depth", "lat"), cross)
         pairs += [mine, lax.ppermute(send, "lat", swap)]
         last = turn == TURNS - 1
         outs = call(
-            functools.partial(next_kernel, turn, last),
-            ([] if last else [blocks]) + [window, window],
-            [VMEM, ANY, ANY, VMEM, VMEM],
-            field_scratch(length, tiles)
-            + [natural, pltpu.VMEM((2, 2, strip_rows, width), jnp.float32), pltpu.SemaphoreType.DMA((2,))],
-            (handed, entering, enter_got, cells, table),
+            functools.partial(next_kernel, turn, plane),
+            ([] if last else [blocks, blocks]) + [window, window],
+            [VMEM, VMEM, VMEM, VMEM, HBM],
+            scratch,
+            (handed, crossed, cells, table, entering),
             flops,
         )
         if last:
             mine, send = outs
         else:
-            hand, mine, send = outs
+            hand, over, mine, send = outs
     pairs += [mine, lax.ppermute(send, "lat", swap)]
     return tuple(
         call(
@@ -377,15 +467,15 @@
     )
 
 
-def inside_kernel(turn, limits_ref, field_ref, blocks_ref, table_ref, out_ref, a, b, even, odd):
+def inside_kernel(turn, limits_ref, field_ref, blocks_ref, table_ref, out_ref, a, b, total):
     a[...] = field_ref[...]
 
-    def emit(i, h, value):
-        out_ref[i, h] = value
+    def emit(c, i, h, value):
+        out_ref[c, i, h] = value
 
     side = lax.axis_index("lat") % 2
     valid = (limits_ref[0], limits_ref[1])
-    advance(a, b, even, odd, blocks_ref, table_ref, turn, sign_of(side), valid, emit)
+    advance(a, b, total, blocks_ref, table_ref, turn, sign_of(side), valid, emit)
 
 
 def grouped(in_flight, entering, classes, freq_phase, class_slowness):
@@ -402,7 +492,7 @@
     length = rows // BLOCKS
     swap = [(i, i ^ 1) for i in range(strips)]
     shift = [(i, i + 1) for i in range(depth - 1)]
-    blocks = f32(length, tiles, SUBLANES, LANES)
+    blocks = f32(2, length, tiles, BLOCKS, LANES)
 
     def both_strips(mine, sent):
         got = lax.ppermute(sent, "lat", swap)
@@ -422,19 +512,17 @@
         return jnp.concatenate([above, cells, below], 1)
 
     def to_blocks(cells):
-        split = cells.reshape(2, BLOCKS, length, tiles, LANES)
-        return split.transpose(2, 3, 0, 1, 4).reshape(blocks.shape)
+        split = cells.reshape(-1, BLOCKS, length, tiles, LANES)
+        return split.transpose(0, 2, 3, 1, 4)
 
     def to_rows(cells):
-        split = cells.reshape(length, tiles, 2, BLOCKS, LANES)
-        return split.transpose(2, 3, 0, 1, 4).reshape(2, rows, width)
+        return cells.transpose(0, 3, 1, 2, 4).reshape(2, rows, width)
 
     def window(cells, which):
         begin = halo - MARGIN + which * strip_rows
         return lax.dynamic_slice_in_dim(cells, begin, strip_rows + 2 * MARGIN, 1)
 
-    cells = with_halo(both_strips(classes, classes))
-    cells = to_blocks(jnp.concatenate([cells, cells], 0))
+    cells = to_blocks(with_halo(both_strips(classes, classes)))[0]
     table = coefficients(freq_phase, class_slowness)
     before = group * core - halo
     limits = jnp.stack([jnp.maximum(-before, 0), jnp.minimum(strips * strip_rows - before, rows)])

time: 39.6 us -> 34.7 us (0.88)
  the two profiles are of different devices: /device:TPU:12 before, /device:TPU:0 now
where the time goes in v1:
time: 34.7 us; the launch traced here: 34.6 us
  Pallas kernels  11.7 us (34%)
  starting transfers between devices  11.4 us (33%)
  waiting for transfers between devices  10.8 us (31%)
  between operations  0.69 us (2%)
    pallas_call x6, Pallas kernels, call(): pl.pallas_call(kernel, out_shape=outs, in_specs=in_specs, out_specs=[VMEM...  11.7 us
    ppermute x3, starting transfers between devices, paired(): pairs += [mine, lax.ppermute(send, 'lat', swap)]  3.92 us
    ppermute x2, starting transfers between devices, paired(): crossed = lax.ppermute(over, ('depth', 'lat'), cross)  3.71 us
    ppermute x2, waiting for transfers between devices, paired(): crossed = lax.ppermute(over, ('depth', 'lat'), cross)  3.71 us
    ppermute x1, starting transfers between devices, paired(): got = lax.ppermute(send, 'lat', swap)  3.06 us
    ppermute x3, waiting for transfers between devices, paired(): pairs += [mine, lax.ppermute(send, 'lat', swap)]  2.61 us
    ppermute x2, waiting for transfers between devices, paired(): handed = lax.ppermute(hand, 'depth', ring)  2.49 us
    ppermute x1, waiting for transfers between devices, paired(): got = lax.ppermute(send, 'lat', swap)  1.98 us
  transfers between devices with their start and end apart: 8, of which 5 were waited for; matrix products, arithmetic and copies ran while one was open for 0% of the time, Pallas kernels for 11%

profile of v1, /device:TPU:0, one launch (start us, length us, event | category | flops | bytes accessed | tf_op | source)
XLA Modules:
  0.0 34.6 jit_solution(4599268081464115105)
XLA Ops:
  0.6 0.0 copy-start
  0.6 1.0 %shard_map.68 = (f32[3,32,256]{2,1,0:T(8,128)S(1)}, f32[3,32,256]{2,1,0:T(8,128)S(1)}) custom-call(f32[1,4,32,256]{3,2,1,0:T(8,128)} %in_ref.1, s32[1,32,256]{2,1,0:T(8,128)} %class_ref.1), custom_call_target="tpu_custom_call" | custom-call | bytes 360448 | tf_op jit(solution)/shard_map/pallas_call | solution.py:33
  1.6 3.1 %collective-permute-start = (f32[3,32,256]{2,1,0:T(8,128)S(1)}, f32[3,32,256]{2,1,0:T(8,128)S(1)}, u32[]{:S(2)}, u32[]{:S(2)}) collective-permute-start(f32[3,32,256]{2,1,0:T(8,128)S(1)} %get-tuple-element.17), channel_id=1, source_target_pairs={{0,1},{1,0},{2,3},{3,2},{4,5},{5,4},{6,7},{7,6},{8,9},{9,8},{10,11... | collective-permute-start | bytes 294920 | tf_op jit(solution)/shard_map/ppermute | solution.py:429
  4.7 0.8 %shard_map.69.table_ref = f32[3,16,8,128]{3,2,1,0:T(8,128)S(1)} custom-call(f32[18]{0:T(128)} %phase_hbm, f32[1,32]{1,0:T(1,128)} %bitcast.1), custom_call_target="tpu_custom_call" | custom-call | bytes 196808 | tf_op jit(solution)/shard_map/pallas_call | solution.py:33
  5.5 2.0 %collective-permute-done.got_ref = f32[3,32,256]{2,1,0:T(8,128)S(1)} collective-permute-done((f32[3,32,256]{2,1,0:T(8,128)S(1)}, f32[3,32,256]{2,1,0:T(8,128)S(1)}, u32[]{:S(2)}, u32[]{:S(2)}) %collective-permute-start) | collective-permute-done | bytes 98336 | tf_op jit(solution)/shard_map/ppermute | solution.py:429
  7.5 0.0 copy-done
  7.5 3.0 %shard_map.70 = (f32[2,8,2,8,128]{4,3,2,1,0:T(8,128)S(1)}, f32[2,8,2,8,128]{4,3,2,1,0:T(8,128)S(1)}, s32[8,2,8,128]{3,2,1,0:T(8,128)S(1)}, f32[2,2,40,128]{3,2,1,0:T(8,128)S(1)}, f32[2,2,40,128]{3,2,1,0:T(8,128)S(1)}) custom-call(f32[3,32,256]{2,1,0:T(8,128)S(1)} %get-tuple-element.16.own_ref, f32[3,32,256]{2,1,0:T(8,128)S(1)} %collective-permute-done.got_ref, ...), custom_call_target="tpu_custom_call" | custom-call | flops 10485760 | bytes 1146880 | tf_op jit(solution)/shard_map/pallas_call | solution.py:33
  10.5 0.1 collective-permute-start.2
  10.6 1.9 %collective-permute-start.3 = (f32[2,8,2,8,128]{4,3,2,1,0:T(8,128)S(1)}, f32[2,8,2,8,128]{4,3,2,1,0:T(8,128)S(1)}, u32[]{:S(2)}, u32[]{:S(2)}) collective-permute-start(f32[2,8,2,8,128]{4,3,2,1,0:T(8,128)S(1)} %get-tuple-element.22), channel_id=1, source_target_pairs={{0,1},{1,0},{2,3},{3,2},{4,5},{5,4},{6,8},{7,9},{8,6},{9,7},{10,11... | collective-permute-start | bytes 393224 | tf_op jit(solution)/shard_map/ppermute | solution.py:443
  12.5 2.5 %collective-permute-done.2.got_ref = f32[2,8,2,8,128]{4,3,2,1,0:T(8,128)S(1)} collective-permute-done((f32[2,8,2,8,128]{4,3,2,1,0:T(8,128)S(1)}, f32[2,8,2,8,128]{4,3,2,1,0:T(8,128)S(1)}, u32[]{:S(2)}, u32[]{:S(2)}) %collective-permute-start.2) | collective-permute-done | bytes 131104 | tf_op jit(solution)/shard_map/ppermute | solution.py:442
  14.9 1.2 %collective-permute-done.3.crossed_ref = f32[2,8,2,8,128]{4,3,2,1,0:T(8,128)S(1)} collective-permute-done((f32[2,8,2,8,128]{4,3,2,1,0:T(8,128)S(1)}, f32[2,8,2,8,128]{4,3,2,1,0:T(8,128)S(1)}, u32[]{:S(2)}, u32[]{:S(2)}) %collective-permute-start.3) | collective-permute-done | bytes 131104 | tf_op jit(solution)/shard_map/ppermute | solution.py:443
  16.1 3.1 %shard_map.71 = (f32[2,8,2,8,128]{4,3,2,1,0:T(8,128)S(1)}, f32[2,8,2,8,128]{4,3,2,1,0:T(8,128)S(1)}, f32[2,2,40,128]{3,2,1,0:T(8,128)S(1)}, f32[2,2,40,128]{3,2,1,0:T(8,128)S(1)}) custom-call(f32[2,8,2,8,128]{4,3,2,1,0:T(8,128)S(1)} %collective-permute-done.2.got_ref, f32[2,8,2,8,128]{4,3,2,1,0:T(8,128)S(1)} %collective-permute-done.3.crossed_ref, ...), custom_call_target="tpu_custom_call" | custom-call | flops 10485760 | bytes 1212416 | tf_op jit(solution)/shard_map/pallas_call | solution.py:33
  19.2 0.6 %collective-permute-start.5 = (f32[2,8,2,8,128]{4,3,2,1,0:T(8,128)S(1)}, f32[2,8,2,8,128]{4,3,2,1,0:T(8,128)S(1)}, u32[]{:S(2)}, u32[]{:S(2)}) collective-permute-start(f32[2,8,2,8,128]{4,3,2,1,0:T(8,128)S(1)} %get-tuple-element.26), channel_id=1, source_target_pairs={{0,2},{2,4},{4,6},{6,0},{8,10},{10,12},{12,14},{14,8},{16,18},{18,... | collective-permute-start | bytes 393224 | tf_op jit(solution)/shard_map/ppermute | solution.py:442
  19.8 1.8 %collective-permute-start.6 = (f32[2,8,2,8,128]{4,3,2,1,0:T(8,128)S(1)}, f32[2,8,2,8,128]{4,3,2,1,0:T(8,128)S(1)}, u32[]{:S(2)}, u32[]{:S(2)}) collective-permute-start(f32[2,8,2,8,128]{4,3,2,1,0:T(8,128)S(1)} %get-tuple-element.27), channel_id=1, source_target_pairs={{0,1},{1,0},{2,3},{3,2},{4,5},{5,4},{6,8},{7,9},{8,6},{9,7},{10,11... | collective-permute-start | bytes 393224 | tf_op jit(solution)/shard_map/ppermute | solution.py:443
  21.7 0.2 collective-permute-start.1
  21.9 1.8 %collective-permute-start.4 = (f32[2,2,40,128]{3,2,1,0:T(8,128)S(1)}, f32[2,2,40,128]{3,2,1,0:T(8,128)S(1)}, u32[]{:S(2)}, u32[]{:S(2)}) collective-permute-start(f32[2,2,40,128]{3,2,1,0:T(8,128)S(1)} %get-tuple-element.25), channel_id=1, source_target_pairs={{0,1},{1,0},{2,3},{3,2},{4,5},{5,4},{6,7},{7,6},{8,9},{9,8},{10,11... | collective-permute-start | bytes 245768 | tf_op jit(solution)/shard_map/ppermute | solution.py:444
  23.7 0.0 collective-permute-done.5.got_ref
  23.7 2.5 %collective-permute-done.6.crossed_ref = f32[2,8,2,8,128]{4,3,2,1,0:T(8,128)S(1)} collective-permute-done((f32[2,8,2,8,128]{4,3,2,1,0:T(8,128)S(1)}, f32[2,8,2,8,128]{4,3,2,1,0:T(8,128)S(1)}, u32[]{:S(2)}, u32[]{:S(2)}) %collective-permute-start.6) | collective-permute-done | bytes 131104 | tf_op jit(solution)/shard_map/ppermute | solution.py:443
  26.2 3.0 %shard_map.72 = (f32[2,2,40,128]{3,2,1,0:T(8,128)S(1)}, f32[2,2,40,128]{3,2,1,0:T(8,128)S(1)}) custom-call(f32[2,8,2,8,128]{4,3,2,1,0:T(8,128)S(1)} %collective-permute-done.5.got_ref, f32[2,8,2,8,128]{4,3,2,1,0:T(8,128)S(1)} %collective-permute-done.6.crossed_ref, s32[8,2,8,128]{3,2,1,0:T(8,128)S(1)} %get-tuple-element.23.blocks_ref, ...), custom_call_target="tpu_custom_call" | custom-call | flops 10485760 | bytes 950272 | tf_op jit(solution)/shard_map/pallas_call | solution.py:33
  29.2 1.9 %collective-permute-start.7 = (f32[2,2,40,128]{3,2,1,0:T(8,128)S(1)}, f32[2,2,40,128]{3,2,1,0:T(8,128)S(1)}, u32[]{:S(2)}, u32[]{:S(2)}) collective-permute-start(f32[2,2,40,128]{3,2,1,0:T(8,128)S(1)} %get-tuple-element.29), channel_id=1, source_target_pairs={{0,1},{1,0},{2,3},{3,2},{4,5},{5,4},{6,7},{7,6},{8,9},{9,8},{10,11... | collective-permute-start | bytes 245768 | tf_op jit(solution)/shard_map/ppermute | solution.py:458
  31.1 0.0 collective-permute-done.1.refs_1_
  31.1 0.0 collective-permute-done.4.refs_3_
  31.1 2.6 %collective-permute-done.7.refs_5_ = f32[2,2,40,128]{3,2,1,0:T(8,128)S(1)} collective-permute-done((f32[2,2,40,128]{3,2,1,0:T(8,128)S(1)}, f32[2,2,40,128]{3,2,1,0:T(8,128)S(1)}, u32[]{:S(2)}, u32[]{:S(2)}) %collective-permute-start.7) | collective-permute-done | bytes 81952 | tf_op jit(solution)/shard_map/ppermute | solution.py:458
  33.7 0.9 %shard_map.73 = (f32[1,8,32,256]{3,2,1,0:T(8,128)}, f32[1,4,32,256]{3,2,1,0:T(8,128)}) custom-call(f32[2,2,40,128]{3,2,1,0:T(8,128)S(1)} %get-tuple-element.19.refs_0_, f32[2,2,40,128]{3,2,1,0:T(8,128)S(1)} %collective-permute-done.1.refs_1_, f32[2,2,40,128]{3,2,1,0:T(8,128)S(1)} %get-tuple-element.24.refs_2_, ...), custom_call_target="tpu_custom_call" | custom-call | bytes 884736 | tf_op jit(solution)/shard_map/pallas_call | solution.py:33
Async XLA Ops:
  0.6 6.8 %copy-start = (f32[2,4,32,256]{3,2,1,0:T(8,128)S(1)}, f32[2,4,32,256]{3,2,1,0:T(8,128)}, u32[]{:S(2)}) copy-start(f32[2,4,32,256]{3,2,1,0:T(8,128)} %enter_ref.5) | copy-start | bytes 786436
  1.6 5.9 %collective-permute-start = (f32[3,32,256]{2,1,0:T(8,128)S(1)}, f32[3,32,256]{2,1,0:T(8,128)S(1)}, u32[]{:S(2)}, u32[]{:S(2)}) collective-permute-start(f32[3,32,256]{2,1,0:T(8,128)S(1)} %get-tuple-element.17), channel_id=1, source_target_pairs={{0,1},{1,0},{2,3},{3,2},{4,5},{5,4},{6,7},{7,6},{8,9},{9,8},{10,11... | collective-permute-start | bytes 294920 | tf_op jit(solution)/shard_map/ppermute | solution.py:429
  10.5 4.4 %collective-permute-start.2 = (f32[2,8,2,8,128]{4,3,2,1,0:T(8,128)S(1)}, f32[2,8,2,8,128]{4,3,2,1,0:T(8,128)S(1)}, u32[]{:S(2)}, u32[]{:S(2)}) collective-permute-start(f32[2,8,2,8,128]{4,3,2,1,0:T(8,128)S(1)} %get-tuple-element.21), channel_id=1, source_target_pairs={{0,2},{2,4},{4,6},{6,0},{8,10},{10,12},{12,14},{14,8},{16,18},{18,... | collective-permute-start | bytes 393224 | tf_op jit(solution)/shard_map/ppermute | solution.py:442
  10.6 5.6 %collective-permute-start.3 = (f32[2,8,2,8,128]{4,3,2,1,0:T(8,128)S(1)}, f32[2,8,2,8,128]{4,3,2,1,0:T(8,128)S(1)}, u32[]{:S(2)}, u32[]{:S(2)}) collective-permute-start(f32[2,8,2,8,128]{4,3,2,1,0:T(8,128)S(1)} %get-tuple-element.22), channel_id=1, source_target_pairs={{0,1},{1,0},{2,3},{3,2},{4,5},{5,4},{6,8},{7,9},{8,6},{9,7},{10,11... | collective-permute-start | bytes 393224 | tf_op jit(solution)/shard_map/ppermute | solution.py:443
  19.2 4.5 %collective-permute-start.5 = (f32[2,8,2,8,128]{4,3,2,1,0:T(8,128)S(1)}, f32[2,8,2,8,128]{4,3,2,1,0:T(8,128)S(1)}, u32[]{:S(2)}, u32[]{:S(2)}) collective-permute-start(f32[2,8,2,8,128]{4,3,2,1,0:T(8,128)S(1)} %get-tuple-element.26), channel_id=1, source_target_pairs={{0,2},{2,4},{4,6},{6,0},{8,10},{10,12},{12,14},{14,8},{16,18},{18,... | collective-permute-start | bytes 393224 | tf_op jit(solution)/shard_map/ppermute | solution.py:442
  19.8 6.4 %collective-permute-start.6 = (f32[2,8,2,8,128]{4,3,2,1,0:T(8,128)S(1)}, f32[2,8,2,8,128]{4,3,2,1,0:T(8,128)S(1)}, u32[]{:S(2)}, u32[]{:S(2)}) collective-permute-start(f32[2,8,2,8,128]{4,3,2,1,0:T(8,128)S(1)} %get-tuple-element.27), channel_id=1, source_target_pairs={{0,1},{1,0},{2,3},{3,2},{4,5},{5,4},{6,8},{7,9},{8,6},{9,7},{10,11... | collective-permute-start | bytes 393224 | tf_op jit(solution)/shard_map/ppermute | solution.py:443
  21.7 9.4 %collective-permute-start.1 = (f32[2,2,40,128]{3,2,1,0:T(8,128)S(1)}, f32[2,2,40,128]{3,2,1,0:T(8,128)S(1)}, u32[]{:S(2)}, u32[]{:S(2)}) collective-permute-start(f32[2,2,40,128]{3,2,1,0:T(8,128)S(1)} %get-tuple-element.20), channel_id=1, source_target_pairs={{0,1},{1,0},{2,3},{3,2},{4,5},{5,4},{6,7},{7,6},{8,9},{9,8},{10,11... | collective-permute-start | bytes 245768 | tf_op jit(solution)/shard_map/ppermute | solution.py:444
  21.9 9.2 %collective-permute-start.4 = (f32[2,2,40,128]{3,2,1,0:T(8,128)S(1)}, f32[2,2,40,128]{3,2,1,0:T(8,128)S(1)}, u32[]{:S(2)}, u32[]{:S(2)}) collective-permute-start(f32[2,2,40,128]{3,2,1,0:T(8,128)S(1)} %get-tuple-element.25), channel_id=1, source_target_pairs={{0,1},{1,0},{2,3},{3,2},{4,5},{5,4},{6,7},{7,6},{8,9},{9,8},{10,11... | collective-permute-start | bytes 245768 | tf_op jit(solution)/shard_map/ppermute | solution.py:444
  29.2 4.5 %collective-permute-start.7 = (f32[2,2,40,128]{3,2,1,0:T(8,128)S(1)}, f32[2,2,40,128]{3,2,1,0:T(8,128)S(1)}, u32[]{:S(2)}, u32[]{:S(2)}) collective-permute-start(f32[2,2,40,128]{3,2,1,0:T(8,128)S(1)} %get-tuple-element.29), channel_id=1, source_target_pairs={{0,1},{1,0},{2,3},{3,2},{4,5},{5,4},{6,7},{7,6},{8,9},{9,8},{10,11... | collective-permute-start | bytes 245768 | tf_op jit(solution)/shard_map/ppermute | solution.py:458

commit v2 on v1

--- a/solution.py
+++ b/solution.py
@@ -20,6 +20,7 @@
 hale_weight = 0.0255
 edge_weight = 0.25 - 0.5 * hale_weight
 corner_weight = 0.125 + 0.25 * hale_weight
+growth = 1.0 / (2.0 * edge_weight)
 miller_start = 32
 
 VMEM = pl.BlockSpec(memory_space=pltpu.VMEM)
@@ -28,13 +29,13 @@
 ANY = pl.BlockSpec(memory_space=pl.ANY)
 
 
-def call(kernel, outs, in_specs, scratch, args, flops=0):
+def call(kernel, outs, in_specs, scratch, args, flops=0, out_specs=None):
     moved = 4 * sum(int(a.size) for a in (*args, *outs))
     return pl.pallas_call(
         kernel,
         out_shape=outs,
         in_specs=in_specs,
-        out_specs=[VMEM] * len(outs),
+        out_specs=out_specs or [VMEM] * len(outs),
         scratch_shapes=scratch,
         compiler_params=pltpu.CompilerParams(vmem_limit_bytes=VMEM_BYTES),
         cost_estimate=pl.CostEstimate(flops=flops, bytes_accessed=moved, transcendentals=0),
@@ -78,7 +79,7 @@
         evens = evens + values[k]
     scale = 1.0 / (values[0] + 2.0 * evens)
     for k in range(TERMS):
-        factor = (1.0 if k == 0 else 2.0) * (1.0 if k % 4 < 2 else -1.0)
+        factor = (1.0 if k == 0 else 2.0) * (1.0 if k % 4 < 2 else -1.0) * growth**-k
         ratio = values[k] * scale * factor
         for turn in range(TURNS):
             out_ref[turn, k] = jnp.broadcast_to(ratio[turn : turn + 1, :], (SUBLANES, LANES))
@@ -97,28 +98,24 @@
     )
 
 
-def advance(a, b, total, classes, table, turn, sigma, valid_rows, emit):
+def advance(a, b, total, coefficients_of, valid_rows):
     length, tiles = a.shape[1], a.shape[2]
     tile = (SUBLANES, LANES)
     lane = lax.broadcasted_iota(jnp.int32, tile, 1)
     block = lax.broadcasted_iota(jnp.int32, tile, 0)
-    at_left, at_right = lane == 0, lane == LANES - 1
+    after_first, before_last = lane > 0, lane < LANES - 1
     zero = jnp.zeros(tile, jnp.float32)
 
     def doubled(above, middle, below):
-        spread, straight = [], []
-        for h in range(tiles):
-            vertical = above[h] + below[h]
-            edge = (2.0 * edge_weight) * middle[h]
-            spread.append((2.0 * corner_weight) * vertical + edge)
-            straight.append((2.0 * edge_weight) * vertical - (edge + edge))
-        from_left = [pltpu.roll(q, 1, 1) for q in spread]
-        from_right = [pltpu.roll(q, LANES - 1, 1) for q in spread]
+        vertical = [above[h] + below[h] for h in range(tiles)]
+        spread = [(corner_weight / edge_weight) * vertical[h] + middle[h] for h in range(tiles)]
+        from_left = jnp.where(after_first, pltpu.roll(spread[tiles - 1], 1, 1), zero)
+        from_right = jnp.where(before_last, pltpu.roll(spread[0], LANES - 1, 1), zero)
         result = []
         for h in range(tiles):
-            left = jnp.where(at_left, from_left[h - 1] if h else zero, from_left[h])
-            right = jnp.where(at_right, from_right[h + 1] if h + 1 < tiles else zero, from_right[h])
-            result.append((left + right) + straight[h])
+            left = spread[h - 1] if h else from_left
+            right = spread[h + 1] if h + 1 < tiles else from_right
+            result.append((left + right) + (vertical[h] - (middle[h] + middle[h])))
         return result
 
     def sweep(source, target, k, odd, first):
@@ -135,9 +132,9 @@
                 ]
             return [source[c, i, h] for h in range(tiles)]
 
-        row = table[turn, k]
-        if odd:
-            row = row * sigma
+        coefficient_at = coefficients_of(k, odd)
+        if first:
+            start_at = coefficients_of(0, False)
         near = [(row_of(c, -1), row_of(c, 0)) for c in range(2)]
         for i in range(length):
             if valid_rows is not None:
@@ -150,17 +147,16 @@
                 near[c] = (middle, below)
                 result = doubled(above, middle, below)
                 for h in range(tiles):
-                    value = 0.5 * result[h] if first else result[h] - target[c, i, h]
+                    value = 0.5 * result[h] if first else result[h] - (growth * growth) * target[c, i, h]
                     if valid_rows is not None:
                         value = jnp.where(inside, value, zero)
                     target[c, i, h] = value
                     result[h] = value
                 values.append(result)
             for h in range(tiles):
-                at_class = classes[i, h]
-                coefficient = pick(row, at_class)
+                coefficient = coefficient_at(i, h)
                 if first:
-                    start = pick(table[turn, 0], at_class)
+                    start = start_at(i, h)
                     sums = [start * source[c, i, h] for c in range(2)]
                 else:
                     sums = [total[c, i, h] for c in range(2)]
@@ -179,10 +175,52 @@
         return carry
 
     lax.fori_loop(1, TERMS // 2, pair, 0)
-    for c in range(2):
-        for i in range(length):
-            for h in range(tiles):
-                emit(c, i, h, total[c, i, h])
+
+
+def looked_up(classes, table, turn, side):
+    def coefficients_of(k, odd):
+        row = table[turn, k]
+        if odd:
+            row = row * sign_of(side)
+        return lambda i, h: pick(row, classes[i, h])
+
+    return coefficients_of
+
+
+def stored(ref):
+    return lambda k, odd: lambda i, h: ref[k, i, h]
+
+
+def coefficient_kernel(turn, blocks_ref, table_ref, out_ref):
+    coefficients_of = looked_up(blocks_ref, table_ref, turn, lax.axis_index("lat"))
+    for k in range(TERMS):
+        coefficient_at = coefficients_of(k, k % 2 == 1)
+        for i in range(out_ref.shape[1]):
+            for h in range(out_ref.shape[2]):
+                out_ref[k, i, h] = coefficient_at(i, h)
+
+
+def picked(sources, indices, which):
+    result = pick(sources[0], indices)
+    for n in range(1, len(sources)):
+        result = jnp.where(which == n, pick(sources[n], indices), result)
+    return result
+
+
+def interleaved(tiles_of, rows):
+    tiles = len(tiles_of)
+    lane = lax.broadcasted_iota(jnp.int32, (rows, LANES), 1)
+    return [
+        picked(tiles_of, (tiles * lane + j) % LANES, (tiles * lane + j) // LANES) for j in range(tiles)
+    ]
+
+
+def natural_order(tiles_of, rows):
+    tiles = len(tiles_of)
+    lane = lax.broadcasted_iota(jnp.int32, (rows, LANES), 1)
+    return [
+        picked(tiles_of, (LANES * t + lane) // tiles, (LANES * t + lane) % tiles) for t in range(tiles)
+    ]
 
 
 def sign_of(side):
@@ -204,24 +242,38 @@
 PAD = 8
 
 
-def windows(natural, length, strip_rows, side, own_ref, send_ref):
+def windows(blocks, natural, own_ref, send_ref):
+    side = lax.axis_index("lat")
+    _, length, tiles, _, _ = blocks.shape
     rows = BLOCKS * length
-    tall = strip_rows + 2 * MARGIN
-    at = lax.broadcasted_iota(jnp.int32, (tall, LANES), 0)
+    strip_rows = rows // 2
+    for c in range(2):
+        for i in range(length):
+            for h in range(tiles):
+                natural[h, pl.ds(PAD + c * rows + i, BLOCKS, stride=length), :] = blocks[c, i, h]
     for ref, strip in ((own_ref, side), (send_ref, 1 - side)):
         begin = strip * strip_rows - MARGIN
-        inside = (at + begin >= 0) & (at + begin < rows)
         for component in range(2):
-            for h in range(natural.shape[0]):
-                found = natural[h, pl.ds(PAD + component * rows + begin, tall), :]
-                ref[component, h] = jnp.where(inside, found, 0.0)
-
-
-def place(natural, source, component, rows, row, count):
-    for h in range(natural.shape[0]):
-        natural[h, pl.ds(pl.multiple_of(PAD + component * rows + row, 8), count), :] = source[
-            :, h * LANES : (h + 1) * LANES
-        ]
+            for r in range(0, strip_rows + 2 * MARGIN, SUBLANES):
+                at = PAD + component * rows + begin + r
+                found = [natural[h, pl.ds(at, SUBLANES), :] for h in range(tiles)]
+                row = lax.broadcasted_iota(jnp.int32, (SUBLANES, LANES), 0) + (begin + r)
+                inside = (row >= 0) & (row < rows)
+                for h, part in enumerate(natural_order(found, SUBLANES)):
+                    ref[component, h, r : r + SUBLANES, :] = jnp.where(inside, part, 0.0)
+
+
+def window_kernel(blocks_ref, own_ref, send_ref, natural):
+    windows(blocks_ref, natural, own_ref, send_ref)
+
+
+def place(natural, source, component, rows, row):
+    tiles = natural.shape[0]
+    for r in range(0, source.shape[0], SUBLANES):
+        parts = [source[r : r + SUBLANES, h * LANES : (h + 1) * LANES] for h in range(tiles)]
+        at = pl.multiple_of(PAD + component * rows + row + r, 8)
+        for h, part in enumerate(interleaved(parts, SUBLANES)):
+            natural[h, pl.ds(at, SUBLANES), :] = part
 
 
 def split_kernel(in_ref, class_ref, own_ref, send_ref, whole, whole_classes, sem):
@@ -249,60 +301,54 @@
 
 
 def unpack(source, natural, component, rows, row, count):
-    for h in range(natural.shape[0]):
-        for j in range(count // SUBLANES):
-            at = pl.multiple_of(PAD + component * rows + row + j * SUBLANES, 8)
-            natural[h, pl.ds(at, SUBLANES), :] = source[component, j, h]
-
-
-def turn_of(turn, a, b, total, natural, blocks_ref, table_ref, enter_ref, strip, sem, outs):
+    tiles = natural.shape[0]
+    for j in range(count // SUBLANES):
+        at = pl.multiple_of(PAD + component * rows + row + j * SUBLANES, 8)
+        parts = [source[component, j, h] for h in range(tiles)]
+        for h, part in enumerate(interleaved(parts, SUBLANES)):
+            natural[h, pl.ds(at, SUBLANES), :] = part
+
+
+def turn_of(turn, coefficients_of, a, b, enter_ref, strip, sem, hand_ref, cross_ref):
     side = lax.axis_index("lat")
-    length = a.shape[1]
-    rows = BLOCKS * length
-    mine_ref, send_ref = outs[-2:]
-    last = len(outs) == 2
-    top = lax.axis_index("depth") == 0
-    if not last:
-        hand_ref, cross_ref = outs[:2]
-        fetch = pltpu.make_async_copy(enter_ref.at[turn, pl.ds(2 * (1 - side), 2)], strip, sem)
+    slab = lax.axis_index("depth")
+    fetch = pltpu.make_async_copy(enter_ref.at[turn, pl.ds(2 * (1 - side), 2)], strip, sem)
+
+    @pl.when(slab == 0)
+    def _():
         fetch.start()
 
-    def emit(c, i, h, value):
-        if not last:
-            hand_ref[c, i, h] = value
-            cross_ref[c, i, h] = value
-        natural[h, pl.ds(PAD + c * rows + i, BLOCKS, stride=length), :] = value
-
-    advance(a, b, total, blocks_ref, table_ref, turn, sign_of(side), None, emit)
-    windows(natural, length, rows // 2, side, mine_ref, send_ref)
-    if not last:
+    advance(a, b, hand_ref, coefficients_of, None)
+
+    @pl.when(slab == 0)
+    def _():
         fetch.wait()
-
-        @pl.when(top)
-        def _():
-            pack(strip, cross_ref)
+        pack(strip, cross_ref)
+
+    @pl.when(slab > 0)
+    def _():
+        cross_ref[...] = hand_ref[...]
 
 
 def first_kernel(own_ref, got_ref, table_ref, enter_ref, *rest):
-    hand_ref, cross_ref, blocks_ref, mine_ref, send_ref, a, b, total, natural, strip, sem = rest
+    hand_ref, cross_ref, blocks_ref, a, b, natural, strip, sem = rest
     side = lax.axis_index("lat")
     strip_rows = own_ref.shape[1]
     rows = 2 * strip_rows
     length = a.shape[1]
-    place(natural, own_ref[2], 0, rows, side * strip_rows, strip_rows)
-    place(natural, got_ref[2], 0, rows, (1 - side) * strip_rows, strip_rows)
+    place(natural, own_ref[2], 0, rows, side * strip_rows)
+    place(natural, got_ref[2], 0, rows, (1 - side) * strip_rows)
     for i in range(length):
         for h in range(a.shape[2]):
             blocks_ref[i, h] = block_of(natural, 0, i, h, length).astype(jnp.int32)
     for component in range(2):
-        place(natural, own_ref[component], component, rows, side * strip_rows, strip_rows)
-        place(natural, got_ref[component], component, rows, (1 - side) * strip_rows, strip_rows)
+        place(natural, own_ref[component], component, rows, side * strip_rows)
+        place(natural, got_ref[component], component, rows, (1 - side) * strip_rows)
     gather_blocks(natural, a)
-    outs = (hand_ref, cross_ref, mine_ref, send_ref)
-    turn_of(0, a, b, total, natural, blocks_ref, table_ref, enter_ref, strip, sem.at[0], outs)
-
-
-def next_kernel(turn, plane, got_ref, crossed_ref, blocks_ref, table_ref, enter_ref, *rest):
+    turn_of(0, looked_up(blocks_ref, table_ref, 0, side), a, b, enter_ref, strip, sem.at[0], hand_ref, cross_ref)
+
+
+def next_kernel(turn, plane, got_ref, crossed_ref, coefficient_ref, enter_ref, *rest):
     *outs, a, b, total, natural, strip, sem = rest
     side = lax.axis_index("lat")
     slab = lax.axis_index("depth")
@@ -315,7 +361,7 @@
         fetch.start()
         fetch.wait()
         for component in range(2):
-            place(natural, strip[component], component, rows, side * strip_rows, strip_rows)
+            place(natural, strip[component], component, rows, side * strip_rows)
             unpack(crossed_ref, natural, component, rows, (1 - side) * strip_rows, strip_rows)
         gather_blocks(natural, a)
 
@@ -327,49 +373,69 @@
     def _():
         a[...] = got_ref[...]
 
-    turn_of(turn, a, b, total, natural, blocks_ref, table_ref, enter_ref, strip, sem.at[0], outs)
-
-
-def image_kernel(*refs):
-    pairs = [(refs[2 * t], refs[2 * t + 1]) for t in range(TURNS)]
-    images_ref, wave_ref, source, receiver = refs[2 * TURNS :]
-    side = lax.axis_index("lat")
-    strip_rows = wave_ref.shape[2]
-    tiles = source.shape[2]
-
-    @pl.when(side == 0)
-    def _():
-        for t, (mine, got) in enumerate(pairs):
-            source[t] = mine[...]
-            receiver[t] = got[...]
-
-    @pl.when(side == 1)
-    def _():
-        for t, (mine, got) in enumerate(pairs):
-            source[t] = got[...]
-            receiver[t] = mine[...]
-
+    if turn == TURNS - 1:
+        advance(a, b, total, stored(coefficient_ref), None)
+        windows(total, natural, *outs)
+    else:
+        turn_of(turn, stored(coefficient_ref), a, b, enter_ref, strip, sem.at[0], *outs)
+
+
+def correlate(mine, got, strip_rows, images):
+    sign = jnp.where(lax.axis_index("lat") == 0, 1, -1)
+    tiles = mine[0].shape[1]
     for h in range(tiles):
-        at = slice(h * LANES, (h + 1) * LANES)
         for o in range(OFFSETS):
-            lag = o - MARGIN
+            lag = sign * (o - MARGIN)
             total = None
-            for t in range(TURNS):
+            for ours, theirs in zip(mine, got):
                 for component in range(2):
                     product = (
-                        source[t, component, h, MARGIN - lag : MARGIN - lag + strip_rows, :]
-                        * receiver[t, component, h, MARGIN + lag : MARGIN + lag + strip_rows, :]
+                        ours[component, h, pl.ds(MARGIN - lag, strip_rows), :]
+                        * theirs[component, h, pl.ds(MARGIN + lag, strip_rows), :]
                     )
                     total = product if total is None else total + product
-            images_ref[0, o, :, at] = total
+            images(o, h, total)
+
+
+def early_kernel(*refs):
+    *pairs, out_ref = refs
+
+    def images(o, h, total):
+        out_ref[o, h] = total
+
+    correlate(pairs[0::2], pairs[1::2], out_ref.shape[2], images)
+
+
+def image_kernel(early_ref, mine_ref, got_ref, images_out, wave_out, images_ref, wave_ref, sem):
+    side = lax.axis_index("lat")
+    strip_rows = wave_ref.shape[1]
+    tiles = mine_ref.shape[1]
+    rows = slice(MARGIN, MARGIN + strip_rows)
+    for j, (ref, which) in enumerate(((mine_ref, side), (got_ref, 1 - side))):
         for component in range(2):
-            rows = slice(MARGIN, MARGIN + strip_rows)
-            wave_ref[0, component, :, at] = source[TURNS - 1, component, h, rows, :]
-            wave_ref[0, 2 + component, :, at] = receiver[TURNS - 1, component, h, rows, :]
+            for h in range(tiles):
+                wave_ref[2 * which + component, :, h * LANES : (h + 1) * LANES] = ref[component, h, rows, :]
+    copies = [pltpu.make_async_copy(wave_ref, wave_out.at[0], sem.at[0])]
+    copies[0].start()
+    done = []
+
+    def images(o, h, total):
+        images_ref[h, o] = early_ref[o, h] + total
+        done.append(o)
+        if len(done) % OFFSETS == 0:
+            copy = pltpu.make_async_copy(
+                images_ref.at[h], images_out.at[0, :, :, pl.ds(h * LANES, LANES)], sem.at[1 + h]
+            )
+            copy.start()
+            copies.append(copy)
+
+    correlate([mine_ref], [got_ref], strip_rows, images)
+    for copy in copies:
+        copy.wait()
 
 
 def field_scratch(length, tiles):
-    return [pltpu.VMEM((2, length, tiles, BLOCKS, LANES), jnp.float32)] * 3
+    return [pltpu.VMEM((2, length, tiles, BLOCKS, LANES), jnp.float32)] * 2
 
 
 def coefficients(freq_phase, class_slowness):
@@ -429,9 +495,9 @@
     got = lax.ppermute(send, "lat", swap)
     freq_phase, _ = lax.optimization_barrier((freq_phase, own))
     table = coefficients(freq_phase, class_slowness)
-    hand, over, cells, mine, send = call(
+    hand, over, cells = call(
         first_kernel,
-        [blocks, blocks, jax.ShapeDtypeStruct(blocks.shape[1:], jnp.int32), window, window],
+        [blocks, blocks, jax.ShapeDtypeStruct(blocks.shape[1:], jnp.int32)],
         [VMEM, VMEM, VMEM, HBM],
         scratch,
         (own, got, table, entering),
@@ -441,41 +507,54 @@
     for turn in range(1, TURNS):
         handed = lax.ppermute(hand, "depth", ring)
         crossed = lax.ppermute(over, ("depth", "lat"), cross)
+        mine, send = call(window_kernel, [window, window], [VMEM], [natural], (hand,))
         pairs += [mine, lax.ppermute(send, "lat", swap)]
         last = turn == TURNS - 1
-        outs = call(
+        (coefficient,) = call(
+            functools.partial(coefficient_kernel, turn),
+            [f32(TERMS, *blocks.shape[1:])],
+            [VMEM] * 2,
+            [],
+            (cells, table),
+        )
+        hand, over = call(
             functools.partial(next_kernel, turn, plane),
-            ([] if last else [blocks, blocks]) + [window, window],
-            [VMEM, VMEM, VMEM, VMEM, HBM],
-            scratch,
-            (handed, crossed, cells, table, entering),
+            [window, window] if last else [blocks, blocks],
+            [VMEM, VMEM, VMEM, HBM],
+            scratch[:2] + [scratch[0]] + scratch[2:],
+            (handed, crossed, coefficient, entering),
             flops,
         )
-        if last:
-            mine, send = outs
-        else:
-            hand, over, mine, send = outs
-    pairs += [mine, lax.ppermute(send, "lat", swap)]
+    mine, send = hand, over
+    got = lax.ppermute(send, "lat", swap)
+    (early,) = call(
+        early_kernel,
+        [f32(OFFSETS, tiles, strip_rows, LANES)],
+        [VMEM] * len(pairs),
+        [],
+        pairs,
+    )
     return tuple(
         call(
             image_kernel,
             [f32(1, OFFSETS, strip_rows, width), f32(1, 4, strip_rows, width)],
-            [VMEM] * len(pairs),
-            [pltpu.VMEM((TURNS, *window.shape), jnp.float32)] * 2,
-            pairs,
+            [VMEM] * 3,
+            [
+                pltpu.VMEM((tiles, OFFSETS, strip_rows, LANES), jnp.float32),
+                pltpu.VMEM((4, strip_rows, width), jnp.float32),
+                pltpu.SemaphoreType.DMA((1 + tiles,)),
+            ],
+            (early, mine, got),
+            out_specs=[HBM] * 2,
         )
     )
 
 
-def inside_kernel(turn, limits_ref, field_ref, blocks_ref, table_ref, out_ref, a, b, total):
+def inside_kernel(turn, limits_ref, field_ref, blocks_ref, table_ref, out_ref, a, b):
     a[...] = field_ref[...]
-
-    def emit(c, i, h, value):
-        out_ref[c, i, h] = value
-
     side = lax.axis_index("lat") % 2
     valid = (limits_ref[0], limits_ref[1])
-    advance(a, b, total, blocks_ref, table_ref, turn, sign_of(side), valid, emit)
+    advance(a, b, out_ref, looked_up(blocks_ref, table_ref, turn, side), valid)
 
 
 def grouped(in_flight, entering, classes, freq_phase, class_slowness):
@@ -512,11 +591,11 @@
         return jnp.concatenate([above, cells, below], 1)
 
     def to_blocks(cells):
-        split = cells.reshape(-1, BLOCKS, length, tiles, LANES)
-        return split.transpose(0, 2, 3, 1, 4)
+        split = cells.reshape(-1, BLOCKS, length, LANES, tiles)
+        return split.transpose(0, 2, 4, 1, 3)
 
     def to_rows(cells):
-        return cells.transpose(0, 3, 1, 2, 4).reshape(2, rows, width)
+        return cells.transpose(0, 3, 1, 4, 2).reshape(2, rows, width)
 
     def window(cells, which):
         begin = halo - MARGIN + which * strip_rows

time: 34.7 us -> 31.9 us (0.919)
  waiting for transfers between devices: 10.8 us -> 8.24 us
    ppermute x3 -> x2, waiting for transfers between devices: 2.61 us -> 0.01 us  [paired(): pairs += [mine, lax.ppermute(send, 'lat', swap)]]
    ppermute x1 -> x2, waiting for transfers between devices: 1.98 us -> 4.32 us  [paired(): got = lax.ppermute(send, 'lat', swap)]
    ppermute x1 -> x2, starting transfers between devices: 3.06 us -> 5.09 us  [paired(): got = lax.ppermute(send, 'lat', swap)]
    ppermute x3 -> x2, starting transfers between devices: 3.92 us -> 2.16 us  [paired(): pairs += [mine, lax.ppermute(send, 'lat', swap)]]
    ppermute x2, waiting for transfers between devices: 3.71 us -> 2.19 us  [paired(): crossed = lax.ppermute(over, ('depth', 'lat'), cross)]
    ppermute x2, waiting for transfers between devices: 2.49 us -> 1.73 us  [paired(): handed = lax.ppermute(hand, 'depth', ring)]
    pallas_call x6 -> x11, Pallas kernels: 11.7 us -> 11.4 us  [call(): pl.pallas_call(kernel, out_shape=outs, in_specs=in_specs, out_specs=out_s...]
  transfers between devices with their start and end apart: 8 -> 8, of which waited for: 5 -> 5; matrix products, arithmetic and copies ran while one was open for 0% -> 0% of each run, Pallas kernels for 11% -> 16%
where the time goes in v2:
time: 31.9 us; the launch traced here: 31.8 us
  Pallas kernels  11.4 us (36%)
  starting transfers between devices  11.4 us (36%)
  waiting for transfers between devices  8.24 us (26%)
  between operations  0.72 us (2%)
    pallas_call x11, Pallas kernels, call(): pl.pallas_call(kernel, out_shape=outs, in_specs=in_specs, out_specs=out_s...  11.4 us
    ppermute x2, starting transfers between devices, paired(): got = lax.ppermute(send, 'lat', swap)  5.09 us
    ppermute x2, waiting for transfers between devices, paired(): got = lax.ppermute(send, 'lat', swap)  4.32 us
    ppermute x2, starting transfers between devices, paired(): crossed = lax.ppermute(over, ('depth', 'lat'), cross)  3.85 us
    ppermute x2, waiting for transfers between devices, paired(): crossed = lax.ppermute(over, ('depth', 'lat'), cross)  2.19 us
    ppermute x2, starting transfers between devices, paired(): pairs += [mine, lax.ppermute(send, 'lat', swap)]  2.16 us
    ppermute x2, waiting for transfers between devices, paired(): handed = lax.ppermute(hand, 'depth', ring)  1.73 us
  transfers between devices with their start and end apart: 8, of which 5 were waited for; matrix products, arithmetic and copies ran while one was open for 0% of the time, Pallas kernels for 16%

profile of v2, /device:TPU:0, one launch (start us, length us, event | category | flops | bytes accessed | tf_op | source)
XLA Modules:
  0.0 31.8 jit_solution(11851907287462941010)
XLA Ops:
  0.6 0.0 copy-start
  0.6 1.0 %shard_map.68 = (f32[3,32,256]{2,1,0:T(8,128)S(1)}, f32[3,32,256]{2,1,0:T(8,128)S(1)}) custom-call(f32[1,4,32,256]{3,2,1,0:T(8,128)} %in_ref.1, s32[1,32,256]{2,1,0:T(8,128)} %class_ref.1), custom_call_target="tpu_custom_call" | custom-call | bytes 360448 | tf_op jit(solution)/shard_map/pallas_call | solution.py:34
  1.6 3.1 %collective-permute-start = (f32[3,32,256]{2,1,0:T(8,128)S(1)}, f32[3,32,256]{2,1,0:T(8,128)S(1)}, u32[]{:S(2)}, u32[]{:S(2)}) collective-permute-start(f32[3,32,256]{2,1,0:T(8,128)S(1)} %get-tuple-element.17), channel_id=1, source_target_pairs={{0,1},{1,0},{2,3},{3,2},{4,5},{5,4},{6,7},{7,6},{8,9},{9,8},{10,11... | collective-permute-start | bytes 294920 | tf_op jit(solution)/shard_map/ppermute | solution.py:495
  4.7 0.8 %shard_map.69.table_ref = f32[3,16,8,128]{3,2,1,0:T(8,128)S(1)} custom-call(f32[18]{0:T(128)} %phase_hbm, f32[1,32]{1,0:T(1,128)} %bitcast.1), custom_call_target="tpu_custom_call" | custom-call | bytes 196808 | tf_op jit(solution)/shard_map/pallas_call | solution.py:34
  5.5 2.0 %collective-permute-done.got_ref = f32[3,32,256]{2,1,0:T(8,128)S(1)} collective-permute-done((f32[3,32,256]{2,1,0:T(8,128)S(1)}, f32[3,32,256]{2,1,0:T(8,128)S(1)}, u32[]{:S(2)}, u32[]{:S(2)}) %collective-permute-start) | collective-permute-done | bytes 98336 | tf_op jit(solution)/shard_map/ppermute | solution.py:495
  7.5 0.0 copy-done
  7.5 2.4 %shard_map.70 = (f32[2,8,2,8,128]{4,3,2,1,0:T(8,128)S(1)}, f32[2,8,2,8,128]{4,3,2,1,0:T(8,128)S(1)}, s32[8,2,8,128]{3,2,1,0:T(8,128)S(1)}) custom-call(f32[3,32,256]{2,1,0:T(8,128)S(1)} %get-tuple-element.16.own_ref, f32[3,32,256]{2,1,0:T(8,128)S(1)} %collective-permute-done.got_ref, f32[3,16,8,128]{3,2,1,0:T(8,128)S(1)} %shard_map.69.table_ref, ...), custom_call_target="tpu_custom_call" | custom-call | flops 10485760 | bytes 983040 | tf_op jit(solution)/shard_map/pallas_call | solution.py:34
  9.9 0.1 collective-permute-start.2
  10.0 1.9 %collective-permute-start.3 = (f32[2,8,2,8,128]{4,3,2,1,0:T(8,128)S(1)}, f32[2,8,2,8,128]{4,3,2,1,0:T(8,128)S(1)}, u32[]{:S(2)}, u32[]{:S(2)}) collective-permute-start(f32[2,8,2,8,128]{4,3,2,1,0:T(8,128)S(1)} %get-tuple-element.22), channel_id=1, source_target_pairs={{0,1},{1,0},{2,3},{3,2},{4,5},{5,4},{6,8},{7,9},{8,6},{9,7},{10,11... | collective-permute-start | bytes 393224 | tf_op jit(solution)/shard_map/ppermute | solution.py:509
  11.9 0.8 %shard_map.72.coefficient_ref = f32[16,8,2,8,128]{4,3,2,1,0:T(8,128)S(1)} custom-call(s32[8,2,8,128]{3,2,1,0:T(8,128)S(1)} %get-tuple-element.23.blocks_ref, f32[3,16,8,128]{3,2,1,0:T(8,128)S(1)} %shard_map.69.table_ref), custom_call_target="tpu_custom_call" | custom-call | bytes 1310720 | tf_op jit(solution)/shard_map/pallas_call | solution.py:34
  12.6 1.7 %collective-permute-done.2.got_ref = f32[2,8,2,8,128]{4,3,2,1,0:T(8,128)S(1)} collective-permute-done((f32[2,8,2,8,128]{4,3,2,1,0:T(8,128)S(1)}, f32[2,8,2,8,128]{4,3,2,1,0:T(8,128)S(1)}, u32[]{:S(2)}, u32[]{:S(2)}) %collective-permute-start.2) | collective-permute-done | bytes 131104 | tf_op jit(solution)/shard_map/ppermute | solution.py:508
  14.4 1.3 %collective-permute-done.3.crossed_ref = f32[2,8,2,8,128]{4,3,2,1,0:T(8,128)S(1)} collective-permute-done((f32[2,8,2,8,128]{4,3,2,1,0:T(8,128)S(1)}, f32[2,8,2,8,128]{4,3,2,1,0:T(8,128)S(1)}, u32[]{:S(2)}, u32[]{:S(2)}) %collective-permute-start.3) | collective-permute-done | bytes 131104 | tf_op jit(solution)/shard_map/ppermute | solution.py:509
  15.6 2.0 %shard_map.73 = (f32[2,8,2,8,128]{4,3,2,1,0:T(8,128)S(1)}, f32[2,8,2,8,128]{4,3,2,1,0:T(8,128)S(1)}) custom-call(f32[2,8,2,8,128]{4,3,2,1,0:T(8,128)S(1)} %collective-permute-done.2.got_ref, f32[2,8,2,8,128]{4,3,2,1,0:T(8,128)S(1)} %collective-permute-done.3.crossed_ref, f32[16,8,2,8,128]{4,3,2,1,0:T(8,128)S(1)} %shard_map.72.coefficient_ref, ...), custom_call_target="tpu_custom_call" | custom-call | flops 10485760 | bytes 1835008 | tf_op jit(solution)/shard_map/pallas_call | solution.py:34
  17.6 0.3 collective-permute-start.5
  17.9 2.0 %collective-permute-start.6 = (f32[2,8,2,8,128]{4,3,2,1,0:T(8,128)S(1)}, f32[2,8,2,8,128]{4,3,2,1,0:T(8,128)S(1)}, u32[]{:S(2)}, u32[]{:S(2)}) collective-permute-start(f32[2,8,2,8,128]{4,3,2,1,0:T(8,128)S(1)} %get-tuple-element.27), channel_id=1, source_target_pairs={{0,1},{1,0},{2,3},{3,2},{4,5},{5,4},{6,8},{7,9},{8,6},{9,7},{10,11... | collective-permute-start | bytes 393224 | tf_op jit(solution)/shard_map/ppermute | solution.py:509
  19.9 0.8 %shard_map.76.coefficient_ref = f32[16,8,2,8,128]{4,3,2,1,0:T(8,128)S(1)} custom-call(s32[8,2,8,128]{3,2,1,0:T(8,128)S(1)} %get-tuple-element.23.blocks_ref, f32[3,16,8,128]{3,2,1,0:T(8,128)S(1)} %shard_map.69.table_ref), custom_call_target="tpu_custom_call" | custom-call | bytes 1310720 | tf_op jit(solution)/shard_map/pallas_call | solution.py:34
  20.7 0.3 shard_map.71
  21.0 0.1 collective-permute-start.1
  21.1 0.3 shard_map.74
  21.4 2.0 %collective-permute-start.4 = (f32[2,2,40,128]{3,2,1,0:T(8,128)S(1)}, f32[2,2,40,128]{3,2,1,0:T(8,128)S(1)}, u32[]{:S(2)}, u32[]{:S(2)}) collective-permute-start(f32[2,2,40,128]{3,2,1,0:T(8,128)S(1)} %get-tuple-element.26), channel_id=1, source_target_pairs={{0,1},{1,0},{2,3},{3,2},{4,5},{5,4},{6,7},{7,6},{8,9},{9,8},{10,11... | collective-permute-start | bytes 245768 | tf_op jit(solution)/shard_map/ppermute | solution.py:511
  23.4 0.0 collective-permute-done.5.got_ref
  23.4 0.9 %collective-permute-done.6.crossed_ref = f32[2,8,2,8,128]{4,3,2,1,0:T(8,128)S(1)} collective-permute-done((f32[2,8,2,8,128]{4,3,2,1,0:T(8,128)S(1)}, f32[2,8,2,8,128]{4,3,2,1,0:T(8,128)S(1)}, u32[]{:S(2)}, u32[]{:S(2)}) %collective-permute-start.6) | collective-permute-done | bytes 131104 | tf_op jit(solution)/shard_map/ppermute | solution.py:509
  24.3 2.2 %shard_map.77 = (f32[2,2,40,128]{3,2,1,0:T(8,128)S(1)}, f32[2,2,40,128]{3,2,1,0:T(8,128)S(1)}) custom-call(f32[2,8,2,8,128]{4,3,2,1,0:T(8,128)S(1)} %collective-permute-done.5.got_ref, f32[2,8,2,8,128]{4,3,2,1,0:T(8,128)S(1)} %collective-permute-done.6.crossed_ref, f32[16,8,2,8,128]{4,3,2,1,0:T(8,128)S(1)} %shard_map.76.coefficient_ref, ...), custom_call_target="tpu_custom_call" | custom-call | flops 10485760 | bytes 1736704 | tf_op jit(solution)/shard_map/pallas_call | solution.py:34
  26.5 2.0 %collective-permute-start.7 = (f32[2,2,40,128]{3,2,1,0:T(8,128)S(1)}, f32[2,2,40,128]{3,2,1,0:T(8,128)S(1)}, u32[]{:S(2)}, u32[]{:S(2)}) collective-permute-start(f32[2,2,40,128]{3,2,1,0:T(8,128)S(1)} %get-tuple-element.29), channel_id=1, source_target_pairs={{0,1},{1,0},{2,3},{3,2},{4,5},{5,4},{6,7},{7,6},{8,9},{9,8},{10,11... | collective-permute-start | bytes 245768 | tf_op jit(solution)/shard_map/ppermute | solution.py:529
  28.5 0.0 collective-permute-done.1.refs_1_
  28.5 0.0 collective-permute-done.4.refs_3_
  28.5 0.1 shard_map.75.early_ref
  28.7 2.3 %collective-permute-done.7.got_ref = f32[2,2,40,128]{3,2,1,0:T(8,128)S(1)} collective-permute-done((f32[2,2,40,128]{3,2,1,0:T(8,128)S(1)}, f32[2,2,40,128]{3,2,1,0:T(8,128)S(1)}, u32[]{:S(2)}, u32[]{:S(2)}) %collective-permute-start.7) | collective-permute-done | bytes 81952 | tf_op jit(solution)/shard_map/ppermute | solution.py:529
  31.0 0.8 %shard_map.78 = (f32[1,8,32,256]{3,2,1,0:T(8,128)}, f32[1,4,32,256]{3,2,1,0:T(8,128)}) custom-call(f32[8,2,32,128]{3,2,1,0:T(8,128)S(1)} %shard_map.75.early_ref, f32[2,2,40,128]{3,2,1,0:T(8,128)S(1)} %get-tuple-element.28.mine_ref, f32[2,2,40,128]{3,2,1,0:T(8,128)S(1)} %collective-permute-done.7.got_ref), custom_call_target="tpu_custom_call" | custom-call | bytes 819200 | tf_op jit(solution)/shard_map/pallas_call | solution.py:34
Async XLA Ops:
  0.6 6.8 %copy-start = (f32[2,4,32,256]{3,2,1,0:T(8,128)S(1)}, f32[2,4,32,256]{3,2,1,0:T(8,128)}, u32[]{:S(2)}) copy-start(f32[2,4,32,256]{3,2,1,0:T(8,128)} %enter_ref.5) | copy-start | bytes 786436
  1.6 5.9 %collective-permute-start = (f32[3,32,256]{2,1,0:T(8,128)S(1)}, f32[3,32,256]{2,1,0:T(8,128)S(1)}, u32[]{:S(2)}, u32[]{:S(2)}) collective-permute-start(f32[3,32,256]{2,1,0:T(8,128)S(1)} %get-tuple-element.17), channel_id=1, source_target_pairs={{0,1},{1,0},{2,3},{3,2},{4,5},{5,4},{6,7},{7,6},{8,9},{9,8},{10,11... | collective-permute-start | bytes 294920 | tf_op jit(solution)/shard_map/ppermute | solution.py:495
  9.9 4.4 %collective-permute-start.2 = (f32[2,8,2,8,128]{4,3,2,1,0:T(8,128)S(1)}, f32[2,8,2,8,128]{4,3,2,1,0:T(8,128)S(1)}, u32[]{:S(2)}, u32[]{:S(2)}) collective-permute-start(f32[2,8,2,8,128]{4,3,2,1,0:T(8,128)S(1)} %get-tuple-element.19.blocks_ref), channel_id=1, source_target_pairs={{0,2},{2,4},{4,6},{6,0},{8,10},{10,12},{12,14},{14,8},{16,18},{18,... | collective-permute-start | bytes 393224 | tf_op jit(solution)/shard_map/ppermute | solution.py:508
  10.0 5.6 %collective-permute-start.3 = (f32[2,8,2,8,128]{4,3,2,1,0:T(8,128)S(1)}, f32[2,8,2,8,128]{4,3,2,1,0:T(8,128)S(1)}, u32[]{:S(2)}, u32[]{:S(2)}) collective-permute-start(f32[2,8,2,8,128]{4,3,2,1,0:T(8,128)S(1)} %get-tuple-element.22), channel_id=1, source_target_pairs={{0,1},{1,0},{2,3},{3,2},{4,5},{5,4},{6,8},{7,9},{8,6},{9,7},{10,11... | collective-permute-start | bytes 393224 | tf_op jit(solution)/shard_map/ppermute | solution.py:509
  17.6 5.7 %collective-permute-start.5 = (f32[2,8,2,8,128]{4,3,2,1,0:T(8,128)S(1)}, f32[2,8,2,8,128]{4,3,2,1,0:T(8,128)S(1)}, u32[]{:S(2)}, u32[]{:S(2)}) collective-permute-start(f32[2,8,2,8,128]{4,3,2,1,0:T(8,128)S(1)} %get-tuple-element.24.blocks_ref), channel_id=1, source_target_pairs={{0,2},{2,4},{4,6},{6,0},{8,10},{10,12},{12,14},{14,8},{16,18},{18,... | collective-permute-start | bytes 393224 | tf_op jit(solution)/shard_map/ppermute | solution.py:508
  17.9 6.4 %collective-permute-start.6 = (f32[2,8,2,8,128]{4,3,2,1,0:T(8,128)S(1)}, f32[2,8,2,8,128]{4,3,2,1,0:T(8,128)S(1)}, u32[]{:S(2)}, u32[]{:S(2)}) collective-permute-start(f32[2,8,2,8,128]{4,3,2,1,0:T(8,128)S(1)} %get-tuple-element.27), channel_id=1, source_target_pairs={{0,1},{1,0},{2,3},{3,2},{4,5},{5,4},{6,8},{7,9},{8,6},{9,7},{10,11... | collective-permute-start | bytes 393224 | tf_op jit(solution)/shard_map/ppermute | solution.py:509
  21.0 7.6 %collective-permute-start.1 = (f32[2,2,40,128]{3,2,1,0:T(8,128)S(1)}, f32[2,2,40,128]{3,2,1,0:T(8,128)S(1)}, u32[]{:S(2)}, u32[]{:S(2)}) collective-permute-start(f32[2,2,40,128]{3,2,1,0:T(8,128)S(1)} %get-tuple-element.21), channel_id=1, source_target_pairs={{0,1},{1,0},{2,3},{3,2},{4,5},{5,4},{6,7},{7,6},{8,9},{9,8},{10,11... | collective-permute-start | bytes 245768 | tf_op jit(solution)/shard_map/ppermute | solution.py:511
  21.4 7.2 %collective-permute-start.4 = (f32[2,2,40,128]{3,2,1,0:T(8,128)S(1)}, f32[2,2,40,128]{3,2,1,0:T(8,128)S(1)}, u32[]{:S(2)}, u32[]{:S(2)}) collective-permute-start(f32[2,2,40,128]{3,2,1,0:T(8,128)S(1)} %get-tuple-element.26), channel_id=1, source_target_pairs={{0,1},{1,0},{2,3},{3,2},{4,5},{5,4},{6,7},{7,6},{8,9},{9,8},{10,11... | collective-permute-start | bytes 245768 | tf_op jit(solution)/shard_map/ppermute | solution.py:511
  26.5 4.5 %collective-permute-start.7 = (f32[2,2,40,128]{3,2,1,0:T(8,128)S(1)}, f32[2,2,40,128]{3,2,1,0:T(8,128)S(1)}, u32[]{:S(2)}, u32[]{:S(2)}) collective-permute-start(f32[2,2,40,128]{3,2,1,0:T(8,128)S(1)} %get-tuple-element.29), channel_id=1, source_target_pairs={{0,1},{1,0},{2,3},{3,2},{4,5},{5,4},{6,7},{7,6},{8,9},{9,8},{10,11... | collective-permute-start | bytes 245768 | tf_op jit(solution)/shard_map/ppermute | solution.py:529

commit v3 on v2

--- a/solution.py
+++ b/solution.py
@@ -263,8 +263,11 @@
                     ref[component, h, r : r + SUBLANES, :] = jnp.where(inside, part, 0.0)
 
 
-def window_kernel(blocks_ref, own_ref, send_ref, natural):
-    windows(blocks_ref, natural, own_ref, send_ref)
+def window_kernel(blocks_ref, *rest):
+    *before, own_ref, send_ref, natural = rest
+    for ref in before:
+        send_ref[: ref.shape[0]] = ref[...]
+    windows(blocks_ref, natural, own_ref, send_ref.at[send_ref.shape[0] - 1])
 
 
 def place(natural, source, component, rows, row):
@@ -276,93 +279,101 @@
             natural[h, pl.ds(at, SUBLANES), :] = part
 
 
-def split_kernel(in_ref, class_ref, own_ref, send_ref, whole, whole_classes, sem):
+def split_kernel(in_ref, class_ref, own_ref, send_ref, whole_classes, sem):
     side = lax.axis_index("lat")
-    fields = pltpu.make_async_copy(in_ref.at[0], whole, sem.at[0])
-    cells = pltpu.make_async_copy(class_ref.at[0], whole_classes, sem.at[1])
-    fields.start()
+    cells = pltpu.make_async_copy(class_ref.at[0], whole_classes, sem.at[0])
     cells.start()
+    copies = [
+        pltpu.make_async_copy(in_ref.at[0, pl.ds(2 * which, 2)], ref.at[pl.ds(0, 2)], sem.at[j])
+        for j, (ref, which) in enumerate(((send_ref, 1 - side), (own_ref, side)), 1)
+    ]
+    for copy in copies:
+        copy.start()
     cells.wait()
     as_float = whole_classes[...].astype(jnp.float32)
     own_ref[2] = as_float
     send_ref[2] = as_float
-    fields.wait()
-    for component in range(2):
-        own_ref[component] = whole[side * 2 + component]
-        send_ref[component] = whole[(1 - side) * 2 + component]
-
-
-def pack(strips, target):
-    for component in range(2):
-        for j in range(strips.shape[1] // SUBLANES):
-            for h in range(target.shape[2]):
-                at = (component, slice(j * SUBLANES, (j + 1) * SUBLANES), slice(h * LANES, (h + 1) * LANES))
-                target[component, j, h] = strips[at]
-
-
-def unpack(source, natural, component, rows, row, count):
+    for copy in copies:
+        copy.wait()
+
+
+def pack(fields, first, target):
+    count = fields.shape[2] // SUBLANES
+    for turn in range(TURNS - 1):
+        for component in range(2):
+            for j in range(count):
+                for h in range(target.shape[2]):
+                    rows, at = slice(j * SUBLANES, (j + 1) * SUBLANES), slice(h * LANES, (h + 1) * LANES)
+                    target[component, turn * count + j, h] = fields[turn, first + component, rows, at]
+
+
+def unpack(source, turn, natural, component, rows, row):
     tiles = natural.shape[0]
-    for j in range(count // SUBLANES):
+    count = source.shape[1] // (TURNS - 1)
+    for j in range(count):
         at = pl.multiple_of(PAD + component * rows + row + j * SUBLANES, 8)
-        parts = [source[component, j, h] for h in range(tiles)]
+        parts = [source[component, turn * count + j, h] for h in range(tiles)]
         for h, part in enumerate(interleaved(parts, SUBLANES)):
             natural[h, pl.ds(at, SUBLANES), :] = part
 
 
-def turn_of(turn, coefficients_of, a, b, enter_ref, strip, sem, hand_ref, cross_ref):
+def weave_kernel(strips_ref, out_ref):
+    tiles = out_ref.shape[1]
+    for n in range(strips_ref.shape[0]):
+        for r in range(0, strips_ref.shape[1], SUBLANES):
+            parts = [
+                strips_ref[n, r : r + SUBLANES, h * LANES : (h + 1) * LANES] for h in range(tiles)
+            ]
+            for h, part in enumerate(interleaved(parts, SUBLANES)):
+                out_ref[n, h, r : r + SUBLANES, :] = part
+
+
+def lay(natural, woven, component, rows, row):
+    tiles, count = woven.shape[:2]
+    for h in range(tiles):
+        at = pl.multiple_of(PAD + component * rows + row, 8)
+        natural[h, pl.ds(at, count), :] = woven[h]
+
+
+def first_kernel(own_ref, got_ref, table_ref, enter_ref, *rest):
+    hand_ref, cross_ref, blocks_ref, a, b, natural = rest
     side = lax.axis_index("lat")
-    slab = lax.axis_index("depth")
-    fetch = pltpu.make_async_copy(enter_ref.at[turn, pl.ds(2 * (1 - side), 2)], strip, sem)
-
-    @pl.when(slab == 0)
-    def _():
-        fetch.start()
-
-    advance(a, b, hand_ref, coefficients_of, None)
-
-    @pl.when(slab == 0)
-    def _():
-        fetch.wait()
-        pack(strip, cross_ref)
-
-    @pl.when(slab > 0)
-    def _():
-        cross_ref[...] = hand_ref[...]
-
-
-def first_kernel(own_ref, got_ref, table_ref, enter_ref, *rest):
-    hand_ref, cross_ref, blocks_ref, a, b, natural, strip, sem = rest
-    side = lax.axis_index("lat")
-    strip_rows = own_ref.shape[1]
+    strip_rows = got_ref.shape[1]
     rows = 2 * strip_rows
     length = a.shape[1]
-    place(natural, own_ref[2], 0, rows, side * strip_rows)
+    lay(natural, own_ref[2], 0, rows, side * strip_rows)
     place(natural, got_ref[2], 0, rows, (1 - side) * strip_rows)
     for i in range(length):
         for h in range(a.shape[2]):
             blocks_ref[i, h] = block_of(natural, 0, i, h, length).astype(jnp.int32)
     for component in range(2):
-        place(natural, own_ref[component], component, rows, side * strip_rows)
+        lay(natural, own_ref[component], component, rows, side * strip_rows)
         place(natural, got_ref[component], component, rows, (1 - side) * strip_rows)
     gather_blocks(natural, a)
-    turn_of(0, looked_up(blocks_ref, table_ref, 0, side), a, b, enter_ref, strip, sem.at[0], hand_ref, cross_ref)
-
-
-def next_kernel(turn, plane, got_ref, crossed_ref, coefficient_ref, enter_ref, *rest):
-    *outs, a, b, total, natural, strip, sem = rest
+    advance(a, b, hand_ref, looked_up(blocks_ref, table_ref, 0, side), None)
+    top = lax.axis_index("depth") == 0
+
+    @pl.when(top)
+    def _():
+        pack(enter_ref, 2 * (1 - side), cross_ref)
+
+    @pl.when(jnp.logical_not(top))
+    def _():
+        cross_ref[...] = hand_ref[...]
+
+
+def next_kernel(turn, plane, got_ref, crossed_ref, entered_ref, coefficient_ref, enter_ref, *rest):
+    *outs, a, b, total, natural = rest
     side = lax.axis_index("lat")
     slab = lax.axis_index("depth")
-    strip_rows = strip.shape[1]
+    strip_rows = enter_ref.shape[2]
     rows = 2 * strip_rows
 
     @pl.when(slab == 0)
     def _():
-        fetch = pltpu.make_async_copy(enter_ref.at[turn - 1, pl.ds(2 * side, 2)], strip, sem.at[1])
-        fetch.start()
-        fetch.wait()
         for component in range(2):
-            place(natural, strip[component], component, rows, side * strip_rows)
-            unpack(crossed_ref, natural, component, rows, (1 - side) * strip_rows, strip_rows)
+            place(natural, enter_ref[turn - 1, 2 * side + component], component, rows, side * strip_rows)
+            unpack(entered_ref, turn - 1, natural, component, rows, (1 - side) * strip_rows)
         gather_blocks(natural, a)
 
     @pl.when((slab > 0) & (slab % plane == 0))
@@ -377,7 +388,7 @@
         advance(a, b, total, stored(coefficient_ref), None)
         windows(total, natural, *outs)
     else:
-        turn_of(turn, stored(coefficient_ref), a, b, enter_ref, strip, sem.at[0], *outs)
+        advance(a, b, outs[0], stored(coefficient_ref), None)
 
 
 def correlate(mine, got, strip_rows, images):
@@ -398,12 +409,12 @@
 
 
 def early_kernel(*refs):
-    *pairs, out_ref = refs
+    *ours, theirs, out_ref = refs
 
     def images(o, h, total):
         out_ref[o, h] = total
 
-    correlate(pairs[0::2], pairs[1::2], out_ref.shape[2], images)
+    correlate(ours, [theirs.at[t] for t in range(len(ours))], out_ref.shape[2], images)
 
 
 def image_kernel(early_ref, mine_ref, got_ref, images_out, wave_out, images_ref, wave_ref, sem):
@@ -411,7 +422,7 @@
     strip_rows = wave_ref.shape[1]
     tiles = mine_ref.shape[1]
     rows = slice(MARGIN, MARGIN + strip_rows)
-    for j, (ref, which) in enumerate(((mine_ref, side), (got_ref, 1 - side))):
+    for ref, which in ((mine_ref, side), (got_ref, 1 - side)):
         for component in range(2):
             for h in range(tiles):
                 wave_ref[2 * which + component, :, h * LANES : (h + 1) * LANES] = ref[component, h, rows, :]
@@ -462,22 +473,23 @@
     swap = [(0, 1), (1, 0)]
     plane = PLANE if depth % PLANE == 0 else depth
     ring = [(i, i - i % plane + (i + 1) % plane) for i in range(depth)]
-    across = {}
+    across, spare = {}, []
     for first in range(plane, depth, plane):
-        across[first - 1], across[first] = first, first - 1
-    cross = [
-        (2 * d + c, 2 * across[d] + c if d in across else 2 * d + 1 - c)
-        for d in range(depth)
-        for c in range(2)
-    ]
+        across[first - 1], across[first], across[first + 2] = first, first + 2, first - 1
+        spare.append(first + 1)
+
+    def crossing(pairs):
+        ways = dict(across)
+        if across:
+            for one, other in (*pairs, *zip(spare[0::2], spare[1::2])):
+                ways[one], ways[other] = other, one
+        return [(2 * d + c, 2 * ways[d] + c if d in ways else 2 * d + 1 - c) for d in range(depth) for c in range(2)]
+
+    cross = {1: crossing([(1, 2)]), 2: crossing([(0, 1)])}
     blocks = f32(2, length, tiles, BLOCKS, LANES)
     window = f32(2, tiles, strip_rows + 2 * MARGIN, LANES)
     natural = pltpu.VMEM((tiles, 2 * BLOCKS * length + 2 * PAD, LANES), jnp.float32)
-    scratch = field_scratch(length, tiles) + [
-        natural,
-        pltpu.VMEM((2, strip_rows, width), jnp.float32),
-        pltpu.SemaphoreType.DMA((2,)),
-    ]
+    scratch = field_scratch(length, tiles) + [natural]
     strips = f32(3, strip_rows, width)
     flops = 20 * TERMS * 4 * strip_rows * width
 
@@ -485,54 +497,68 @@
         split_kernel,
         [strips, strips],
         [HBM, HBM],
-        [
-            pltpu.VMEM((4, strip_rows, width), jnp.float32),
-            pltpu.VMEM((strip_rows, width), jnp.int32),
-            pltpu.SemaphoreType.DMA((2,)),
-        ],
+        [pltpu.VMEM((strip_rows, width), jnp.int32), pltpu.SemaphoreType.DMA((3,))],
         in_hbm(in_flight, classes),
     )
     got = lax.ppermute(send, "lat", swap)
     freq_phase, _ = lax.optimization_barrier((freq_phase, own))
+    (own,) = call(weave_kernel, [f32(3, tiles, strip_rows, LANES)], [VMEM], [], (own,))
     table = coefficients(freq_phase, class_slowness)
     hand, over, cells = call(
         first_kernel,
         [blocks, blocks, jax.ShapeDtypeStruct(blocks.shape[1:], jnp.int32)],
-        [VMEM, VMEM, VMEM, HBM],
+        [VMEM, VMEM, VMEM, VMEM],
         scratch,
         (own, got, table, entering),
         flops,
     )
-    pairs = []
+    mines, sent, coefficient = [], (), {}
     for turn in range(1, TURNS):
         handed = lax.ppermute(hand, "depth", ring)
-        crossed = lax.ppermute(over, ("depth", "lat"), cross)
-        mine, send = call(window_kernel, [window, window], [VMEM], [natural], (hand,))
-        pairs += [mine, lax.ppermute(send, "lat", swap)]
+        crossed = lax.ppermute(over, ("depth", "lat"), cross[min(turn, 2)])
+        if turn == 1:
+            entered = crossed
+        mine, send = call(
+            window_kernel,
+            [window, f32(turn, *window.shape)],
+            [VMEM] * (1 + len(sent)),
+            [natural],
+            (hand, *sent),
+        )
+        mines.append(mine)
+        if turn == 1:
+            for later in range(1, TURNS):
+                (coefficient[later],) = call(
+                    functools.partial(coefficient_kernel, later),
+                    [f32(TERMS, *blocks.shape[1:])],
+                    [VMEM] * 2,
+                    [],
+                    (cells, table),
+                )
+            coefficient[1], send, *others = lax.optimization_barrier(
+                (coefficient[1], send, *(coefficient[later] for later in range(2, TURNS)))
+            )
+            coefficient.update(zip(range(2, TURNS), others))
+        sent = (send,)
         last = turn == TURNS - 1
-        (coefficient,) = call(
-            functools.partial(coefficient_kernel, turn),
-            [f32(TERMS, *blocks.shape[1:])],
-            [VMEM] * 2,
-            [],
-            (cells, table),
-        )
-        hand, over = call(
+        outs = call(
             functools.partial(next_kernel, turn, plane),
-            [window, window] if last else [blocks, blocks],
-            [VMEM, VMEM, VMEM, HBM],
+            [window, window] if last else [blocks],
+            [VMEM] * 5,
             scratch[:2] + [scratch[0]] + scratch[2:],
-            (handed, crossed, coefficient, entering),
+            (handed, crossed, entered, coefficient[turn], entering),
             flops,
         )
-    mine, send = hand, over
+        hand = over = outs[0]
+    earlier = lax.ppermute(send, "lat", swap)
+    mine, send = outs
     got = lax.ppermute(send, "lat", swap)
     (early,) = call(
         early_kernel,
         [f32(OFFSETS, tiles, strip_rows, LANES)],
-        [VMEM] * len(pairs),
+        [VMEM] * TURNS,
         [],
-        pairs,
+        (*mines, earlier),
     )
     return tuple(
         call(
@@ -643,5 +669,6 @@
         P(),
     )
     out_specs = (P("depth", None, "lat", None), P("depth", None, "lat", None))
-    local = paired if mesh.shape["lat"] == 2 else grouped
+    pair = mesh.shape["lat"] == 2
+    local = paired if pair else grouped
     return jax.shard_map(local, mesh=mesh, in_specs=in_specs, out_specs=out_specs, check_vma=False)

time: 31.9 us -> 29.1 us (0.912)
  the two profiles are of different devices: /device:TPU:0 before, /device:TPU:20 now
where the time goes in v3:
time: 29.1 us; the launch traced here: 29 us
  waiting for transfers between devices  12.7 us (44%)
  Pallas kernels  10.6 us (36%)
  starting transfers between devices  4.93 us (17%)
  between operations  0.73 us (3%)
    pallas_call x12, Pallas kernels, call(): pl.pallas_call(kernel, out_shape=outs, in_specs=in_specs, out_specs=out_s...  10.6 us
    ppermute x2, waiting for transfers between devices, paired(): got = lax.ppermute(send, 'lat', swap)  6.92 us
    ppermute x2, waiting for transfers between devices, paired(): handed = lax.ppermute(hand, 'depth', ring)  5.78 us
    ppermute x2, starting transfers between devices, paired(): crossed = lax.ppermute(over, ('depth', 'lat'), cross[min(turn, 2)])  3.1 us
    ppermute x2, starting transfers between devices, paired(): got = lax.ppermute(send, 'lat', swap)  1.14 us
  transfers between devices with their start and end apart: 7, of which 4 were waited for; matrix products, arithmetic and copies ran while one was open for 0% of the time, Pallas kernels for 17%

profile of v3, /device:TPU:20, one launch (start us, length us, event | category | flops | bytes accessed | tf_op | source)
XLA Modules:
  0.0 29.0 jit_solution(10191451019789076846)
XLA Ops:
  0.6 0.0 copy-start
  0.6 1.0 %shard_map.68 = (f32[3,32,256]{2,1,0:T(8,128)S(1)}, f32[3,32,256]{2,1,0:T(8,128)S(1)}) custom-call(f32[1,4,32,256]{3,2,1,0:T(8,128)} %in_ref.1, s32[1,32,256]{2,1,0:T(8,128)} %class_ref.1), custom_call_target="tpu_custom_call" | custom-call | bytes 360448 | tf_op jit(solution)/shard_map/pallas_call | solution.py:34
  1.6 0.6 %collective-permute-start = (f32[3,32,256]{2,1,0:T(8,128)S(1)}, f32[3,32,256]{2,1,0:T(8,128)S(1)}, u32[]{:S(2)}, u32[]{:S(2)}) collective-permute-start(f32[3,32,256]{2,1,0:T(8,128)S(1)} %get-tuple-element.18), channel_id=1, source_target_pairs={{0,1},{1,0},{2,3},{3,2},{4,5},{5,4},{6,7},{7,6},{8,9},{9,8},{10,11... | collective-permute-start | bytes 294920 | tf_op jit(solution)/shard_map/ppermute | solution.py:503
  2.2 0.2 shard_map.69.own_ref
  2.3 0.8 %shard_map.70.table_ref = f32[3,16,8,128]{3,2,1,0:T(8,128)S(1)} custom-call(f32[18]{0:T(128)} %phase_hbm, f32[1,32]{1,0:T(1,128)} %bitcast.1), custom_call_target="tpu_custom_call" | custom-call | bytes 196808 | tf_op jit(solution)/shard_map/pallas_call | solution.py:34
  3.2 3.1 %collective-permute-done.got_ref = f32[3,32,256]{2,1,0:T(8,128)S(1)} collective-permute-done((f32[3,32,256]{2,1,0:T(8,128)S(1)}, f32[3,32,256]{2,1,0:T(8,128)S(1)}, u32[]{:S(2)}, u32[]{:S(2)}) %collective-permute-start) | collective-permute-done | bytes 98336 | tf_op jit(solution)/shard_map/ppermute | solution.py:503
  6.3 0.0 copy-done
  6.3 2.2 %shard_map.71 = (f32[2,8,2,8,128]{4,3,2,1,0:T(8,128)S(1)}, f32[2,8,2,8,128]{4,3,2,1,0:T(8,128)S(1)}, s32[8,2,8,128]{3,2,1,0:T(8,128)S(1)}) custom-call(f32[3,2,32,128]{3,2,1,0:T(8,128)S(1)} %shard_map.69.own_ref, f32[3,32,256]{2,1,0:T(8,128)S(1)} %collective-permute-done.got_ref, f32[3,16,8,128]{3,2,1,0:T(8,128)S(1)} %shard_map.70.table_ref, ...), custom_call_target="tpu_custom_call" | custom-call | flops 10485760 | bytes 983040 | tf_op jit(solution)/shard_map/pallas_call | solution.py:34
  8.5 0.1 collective-permute-start.1
  8.5 1.6 %collective-permute-start.2 = (f32[2,8,2,8,128]{4,3,2,1,0:T(8,128)S(1)}, f32[2,8,2,8,128]{4,3,2,1,0:T(8,128)S(1)}, u32[]{:S(2)}, u32[]{:S(2)}) collective-permute-start(f32[2,8,2,8,128]{4,3,2,1,0:T(8,128)S(1)} %get-tuple-element.22), channel_id=1, source_target_pairs={{0,1},{1,0},{2,4},{3,5},{4,2},{5,3},{6,8},{7,9},{8,12},{9,13},{10,... | collective-permute-start | bytes 393224 | tf_op jit(solution)/shard_map/ppermute | solution.py:518
  10.1 0.8 %shard_map.73.coefficient_ref = f32[16,8,2,8,128]{4,3,2,1,0:T(8,128)S(1)} custom-call(s32[8,2,8,128]{3,2,1,0:T(8,128)S(1)} %get-tuple-element.23.blocks_ref, f32[3,16,8,128]{3,2,1,0:T(8,128)S(1)} %shard_map.70.table_ref), custom_call_target="tpu_custom_call" | custom-call | bytes 1310720 | tf_op jit(solution)/shard_map/pallas_call | solution.py:34
  10.8 0.8 %shard_map.74.coefficient_ref = f32[16,8,2,8,128]{4,3,2,1,0:T(8,128)S(1)} custom-call(s32[8,2,8,128]{3,2,1,0:T(8,128)S(1)} %get-tuple-element.23.blocks_ref, f32[3,16,8,128]{3,2,1,0:T(8,128)S(1)} %shard_map.70.table_ref), custom_call_target="tpu_custom_call" | custom-call | bytes 1310720 | tf_op jit(solution)/shard_map/pallas_call | solution.py:34
  11.6 0.3 shard_map.72
  11.9 2.4 %collective-permute-done.1.got_ref = f32[2,8,2,8,128]{4,3,2,1,0:T(8,128)S(1)} collective-permute-done((f32[2,8,2,8,128]{4,3,2,1,0:T(8,128)S(1)}, f32[2,8,2,8,128]{4,3,2,1,0:T(8,128)S(1)}, u32[]{:S(2)}, u32[]{:S(2)}) %collective-permute-start.1) | collective-permute-done | bytes 131104 | tf_op jit(solution)/shard_map/ppermute | solution.py:517
  14.3 0.0 collective-permute-done.2.crossed_ref.entered_ref
  14.3 1.6 %shard_map.75.blocks_ref = f32[2,8,2,8,128]{4,3,2,1,0:T(8,128)S(1)} custom-call(f32[2,8,2,8,128]{4,3,2,1,0:T(8,128)S(1)} %collective-permute-done.1.got_ref, f32[2,8,2,8,128]{4,3,2,1,0:T(8,128)S(1)} %collective-permute-done.2.crossed_ref.entered_ref, f32[2,8,2,8,128]{4,3,2,1,0:T(8,128)S(1)} %collective-permute-done.2.crossed_ref.entered_ref, ...), custom_call_target="tpu_custom_call" | custom-call | flops 10485760 | bytes 1835008 | tf_op jit(solution)/shard_map/pallas_call | solution.py:34
  15.9 0.1 collective-permute-start.4
  16.0 1.6 %collective-permute-start.5 = (f32[2,8,2,8,128]{4,3,2,1,0:T(8,128)S(1)}, f32[2,8,2,8,128]{4,3,2,1,0:T(8,128)S(1)}, u32[]{:S(2)}, u32[]{:S(2)}) collective-permute-start(f32[2,8,2,8,128]{4,3,2,1,0:T(8,128)S(1)} %shard_map.75.blocks_ref), channel_id=1, source_target_pairs={{0,2},{1,3},{2,0},{3,1},{4,5},{5,4},{6,8},{7,9},{8,12},{9,13},{10,... | collective-permute-start | bytes 393224 | tf_op jit(solution)/shard_map/ppermute | solution.py:518
  17.6 0.3 shard_map.76
  17.8 0.6 %collective-permute-start.3 = (f32[2,2,2,40,128]{4,3,2,1,0:T(8,128)S(1)}, f32[2,2,2,40,128]{4,3,2,1,0:T(8,128)S(1)}, u32[]{:S(2)}, u32[]{:S(2)}) collective-permute-start(f32[2,2,2,40,128]{4,3,2,1,0:T(8,128)S(1)} %get-tuple-element.28), channel_id=1, source_target_pairs={{0,1},{1,0},{2,3},{3,2},{4,5},{5,4},{6,7},{7,6},{8,9},{9,8},{10,11... | collective-permute-start | bytes 491528 | tf_op jit(solution)/shard_map/ppermute | solution.py:553
  18.4 3.4 %collective-permute-done.4.got_ref = f32[2,8,2,8,128]{4,3,2,1,0:T(8,128)S(1)} collective-permute-done((f32[2,8,2,8,128]{4,3,2,1,0:T(8,128)S(1)}, f32[2,8,2,8,128]{4,3,2,1,0:T(8,128)S(1)}, u32[]{:S(2)}, u32[]{:S(2)}) %collective-permute-start.4) | collective-permute-done | bytes 131104 | tf_op jit(solution)/shard_map/ppermute | solution.py:517
  21.8 0.0 collective-permute-done.5.crossed_ref
  21.8 1.9 %shard_map.78 = (f32[2,2,40,128]{3,2,1,0:T(8,128)S(1)}, f32[2,2,40,128]{3,2,1,0:T(8,128)S(1)}) custom-call(f32[2,8,2,8,128]{4,3,2,1,0:T(8,128)S(1)} %collective-permute-done.4.got_ref, f32[2,8,2,8,128]{4,3,2,1,0:T(8,128)S(1)} %collective-permute-done.5.crossed_ref, f32[2,8,2,8,128]{4,3,2,1,0:T(8,128)S(1)} %collective-permute-done.2.crossed_ref.entered_ref, ...), custom_call_target="tpu_custom_call" | custom-call | flops 10485760 | bytes 1867776 | tf_op jit(solution)/shard_map/pallas_call | solution.py:34
  23.7 0.6 %collective-permute-start.6 = (f32[2,2,40,128]{3,2,1,0:T(8,128)S(1)}, f32[2,2,40,128]{3,2,1,0:T(8,128)S(1)}, u32[]{:S(2)}, u32[]{:S(2)}) collective-permute-start(f32[2,2,40,128]{3,2,1,0:T(8,128)S(1)} %get-tuple-element.31), channel_id=1, source_target_pairs={{0,1},{1,0},{2,3},{3,2},{4,5},{5,4},{6,7},{7,6},{8,9},{9,8},{10,11... | collective-permute-start | bytes 245768 | tf_op jit(solution)/shard_map/ppermute | solution.py:555
  24.2 0.0 collective-permute-done.3.refs_2_
  24.2 0.1 shard_map.77.early_ref
  24.4 3.8 %collective-permute-done.6.got_ref = f32[2,2,40,128]{3,2,1,0:T(8,128)S(1)} collective-permute-done((f32[2,2,40,128]{3,2,1,0:T(8,128)S(1)}, f32[2,2,40,128]{3,2,1,0:T(8,128)S(1)}, u32[]{:S(2)}, u32[]{:S(2)}) %collective-permute-start.6) | collective-permute-done | bytes 81952 | tf_op jit(solution)/shard_map/ppermute | solution.py:555
  28.2 0.8 %shard_map.79 = (f32[1,8,32,256]{3,2,1,0:T(8,128)}, f32[1,4,32,256]{3,2,1,0:T(8,128)}) custom-call(f32[8,2,32,128]{3,2,1,0:T(8,128)S(1)} %shard_map.77.early_ref, f32[2,2,40,128]{3,2,1,0:T(8,128)S(1)} %get-tuple-element.30.mine_ref, f32[2,2,40,128]{3,2,1,0:T(8,128)S(1)} %collective-permute-done.6.got_ref), custom_call_target="tpu_custom_call" | custom-call | bytes 819200 | tf_op jit(solution)/shard_map/pallas_call | solution.py:34
Async XLA Ops:
  0.6 5.7 %copy-start = (f32[2,4,32,256]{3,2,1,0:T(8,128)S(1)}, f32[2,4,32,256]{3,2,1,0:T(8,128)}, u32[]{:S(2)}) copy-start(f32[2,4,32,256]{3,2,1,0:T(8,128)} %enter_ref.5) | copy-start | bytes 786436
  1.6 4.7 %collective-permute-start = (f32[3,32,256]{2,1,0:T(8,128)S(1)}, f32[3,32,256]{2,1,0:T(8,128)S(1)}, u32[]{:S(2)}, u32[]{:S(2)}) collective-permute-start(f32[3,32,256]{2,1,0:T(8,128)S(1)} %get-tuple-element.18), channel_id=1, source_target_pairs={{0,1},{1,0},{2,3},{3,2},{4,5},{5,4},{6,7},{7,6},{8,9},{9,8},{10,11... | collective-permute-start | bytes 294920 | tf_op jit(solution)/shard_map/ppermute | solution.py:503
  8.5 5.8 %collective-permute-start.1 = (f32[2,8,2,8,128]{4,3,2,1,0:T(8,128)S(1)}, f32[2,8,2,8,128]{4,3,2,1,0:T(8,128)S(1)}, u32[]{:S(2)}, u32[]{:S(2)}) collective-permute-start(f32[2,8,2,8,128]{4,3,2,1,0:T(8,128)S(1)} %get-tuple-element.20.blocks_ref), channel_id=1, source_target_pairs={{0,2},{2,4},{4,6},{6,0},{8,10},{10,12},{12,14},{14,8},{16,18},{18,... | collective-permute-start | bytes 393224 | tf_op jit(solution)/shard_map/ppermute | solution.py:517
  8.5 5.8 %collective-permute-start.2 = (f32[2,8,2,8,128]{4,3,2,1,0:T(8,128)S(1)}, f32[2,8,2,8,128]{4,3,2,1,0:T(8,128)S(1)}, u32[]{:S(2)}, u32[]{:S(2)}) collective-permute-start(f32[2,8,2,8,128]{4,3,2,1,0:T(8,128)S(1)} %get-tuple-element.22), channel_id=1, source_target_pairs={{0,1},{1,0},{2,4},{3,5},{4,2},{5,3},{6,8},{7,9},{8,12},{9,13},{10,... | collective-permute-start | bytes 393224 | tf_op jit(solution)/shard_map/ppermute | solution.py:518
  15.9 5.8 %collective-permute-start.4 = (f32[2,8,2,8,128]{4,3,2,1,0:T(8,128)S(1)}, f32[2,8,2,8,128]{4,3,2,1,0:T(8,128)S(1)}, u32[]{:S(2)}, u32[]{:S(2)}) collective-permute-start(f32[2,8,2,8,128]{4,3,2,1,0:T(8,128)S(1)} %shard_map.75.blocks_ref), channel_id=1, source_target_pairs={{0,2},{2,4},{4,6},{6,0},{8,10},{10,12},{12,14},{14,8},{16,18},{18,... | collective-permute-start | bytes 393224 | tf_op jit(solution)/shard_map/ppermute | solution.py:517
  16.0 5.8 %collective-permute-start.5 = (f32[2,8,2,8,128]{4,3,2,1,0:T(8,128)S(1)}, f32[2,8,2,8,128]{4,3,2,1,0:T(8,128)S(1)}, u32[]{:S(2)}, u32[]{:S(2)}) collective-permute-start(f32[2,8,2,8,128]{4,3,2,1,0:T(8,128)S(1)} %shard_map.75.blocks_ref), channel_id=1, source_target_pairs={{0,2},{1,3},{2,0},{3,1},{4,5},{5,4},{6,8},{7,9},{8,12},{9,13},{10,... | collective-permute-start | bytes 393224 | tf_op jit(solution)/shard_map/ppermute | solution.py:518
  17.8 6.4 %collective-permute-start.3 = (f32[2,2,2,40,128]{4,3,2,1,0:T(8,128)S(1)}, f32[2,2,2,40,128]{4,3,2,1,0:T(8,128)S(1)}, u32[]{:S(2)}, u32[]{:S(2)}) collective-permute-start(f32[2,2,2,40,128]{4,3,2,1,0:T(8,128)S(1)} %get-tuple-element.28), channel_id=1, source_target_pairs={{0,1},{1,0},{2,3},{3,2},{4,5},{5,4},{6,7},{7,6},{8,9},{9,8},{10,11... | collective-permute-start | bytes 491528 | tf_op jit(solution)/shard_map/ppermute | solution.py:553
  23.7 4.5 %collective-permute-start.6 = (f32[2,2,40,128]{3,2,1,0:T(8,128)S(1)}, f32[2,2,40,128]{3,2,1,0:T(8,128)S(1)}, u32[]{:S(2)}, u32[]{:S(2)}) collective-permute-start(f32[2,2,40,128]{3,2,1,0:T(8,128)S(1)} %get-tuple-element.31), channel_id=1, source_target_pairs={{0,1},{1,0},{2,3},{3,2},{4,5},{5,4},{6,7},{7,6},{8,9},{9,8},{10,11... | collective-permute-start | bytes 245768 | tf_op jit(solution)/shard_map/ppermute | solution.py:555

commit v4 on v3

--- a/solution.py
+++ b/solution.py
@@ -252,6 +252,8 @@
             for h in range(tiles):
                 natural[h, pl.ds(PAD + c * rows + i, BLOCKS, stride=length), :] = blocks[c, i, h]
     for ref, strip in ((own_ref, side), (send_ref, 1 - side)):
+        if ref is None:
+            continue
         begin = strip * strip_rows - MARGIN
         for component in range(2):
             for r in range(0, strip_rows + 2 * MARGIN, SUBLANES):
@@ -268,6 +270,10 @@
     for ref in before:
         send_ref[: ref.shape[0]] = ref[...]
     windows(blocks_ref, natural, own_ref, send_ref.at[send_ref.shape[0] - 1])
+
+
+def own_window_kernel(blocks_ref, own_ref, natural):
+    windows(blocks_ref, natural, own_ref, None)
 
 
 def place(natural, source, component, rows, row):
@@ -363,7 +369,7 @@
 
 
 def next_kernel(turn, plane, got_ref, crossed_ref, entered_ref, coefficient_ref, enter_ref, *rest):
-    *outs, a, b, total, natural = rest
+    *outs, a, b, natural = rest
     side = lax.axis_index("lat")
     slab = lax.axis_index("depth")
     strip_rows = enter_ref.shape[2]
@@ -385,8 +391,8 @@
         a[...] = got_ref[...]
 
     if turn == TURNS - 1:
-        advance(a, b, total, stored(coefficient_ref), None)
-        windows(total, natural, *outs)
+        advance(a, b, outs[0], stored(coefficient_ref), None)
+        windows(outs[0], natural, None, outs[1])
     else:
         advance(a, b, outs[0], stored(coefficient_ref), None)
 
@@ -473,19 +479,20 @@
     swap = [(0, 1), (1, 0)]
     plane = PLANE if depth % PLANE == 0 else depth
     ring = [(i, i - i % plane + (i + 1) % plane) for i in range(depth)]
-    across, spare = {}, []
-    for first in range(plane, depth, plane):
-        across[first - 1], across[first], across[first + 2] = first, first + 2, first - 1
-        spare.append(first + 1)
-
-    def crossing(pairs):
-        ways = dict(across)
-        if across:
-            for one, other in (*pairs, *zip(spare[0::2], spare[1::2])):
-                ways[one], ways[other] = other, one
+
+    def crossing(loops):
+        ways = {}
+        for loop in loops:
+            ways.update(zip(loop, (*loop[1:], loop[0])))
         return [(2 * d + c, 2 * ways[d] + c if d in ways else 2 * d + 1 - c) for d in range(depth) for c in range(2)]
 
-    cross = {1: crossing([(1, 2)]), 2: crossing([(0, 1)])}
+    starts = range(plane, depth, plane)
+    loops = [(first - 1, first, first - 3) for first in starts]
+    later = [(first - 1, first, first + 2) for first in starts]
+    if loops:
+        loops.append((depth - 2, depth - 1))
+        later += [(0, 1), *((first + 1, first + 1 + plane) for first in starts[:-1:2])]
+    cross = {1: crossing(loops), 2: crossing(later)}
     blocks = f32(2, length, tiles, BLOCKS, LANES)
     window = f32(2, tiles, strip_rows + 2 * MARGIN, LANES)
     natural = pltpu.VMEM((tiles, 2 * BLOCKS * length + 2 * PAD, LANES), jnp.float32)
@@ -543,16 +550,17 @@
         last = turn == TURNS - 1
         outs = call(
             functools.partial(next_kernel, turn, plane),
-            [window, window] if last else [blocks],
+            [blocks, window] if last else [blocks],
             [VMEM] * 5,
-            scratch[:2] + [scratch[0]] + scratch[2:],
+            scratch,
             (handed, crossed, entered, coefficient[turn], entering),
             flops,
         )
         hand = over = outs[0]
     earlier = lax.ppermute(send, "lat", swap)
-    mine, send = outs
+    hand, send = outs
     got = lax.ppermute(send, "lat", swap)
+    (mine,) = call(own_window_kernel, [window], [VMEM], [natural], (hand,))
     (early,) = call(
         early_kernel,
         [f32(OFFSETS, tiles, strip_rows, LANES)],

time: 29.1 us -> 29 us (level)
  the two profiles are of different devices: /device:TPU:20 before, /device:TPU:16 now
where the time goes in v4:
time: 29 us; the launch traced here: 28.9 us
  Pallas kernels  10.7 us (37%)
  waiting for transfers between devices  9.65 us (33%)
  starting transfers between devices  7.82 us (27%)
  between operations  0.73 us (3%)
    pallas_call x13, Pallas kernels, call(): pl.pallas_call(kernel, out_shape=outs, in_specs=in_specs, out_specs=out_s...  10.7 us
    ppermute x2, waiting for transfers between devices, paired(): handed = lax.ppermute(hand, 'depth', ring)  4.93 us
    ppermute x2, waiting for transfers between devices, paired(): got = lax.ppermute(send, 'lat', swap)  4.71 us
    ppermute x2, starting transfers between devices, paired(): got = lax.ppermute(send, 'lat', swap)  3.17 us
    ppermute x2, starting transfers between devices, paired(): crossed = lax.ppermute(over, ('depth', 'lat'), cross[min(turn, 2)])  2.75 us
    ppermute x1, starting transfers between devices, paired(): earlier = lax.ppermute(send, 'lat', swap)  1.59 us
  transfers between devices with their start and end apart: 7, of which 4 were waited for; matrix products, arithmetic and copies ran while one was open for 0% of the time, Pallas kernels for 18%

profile of v4, /device:TPU:16, one launch (start us, length us, event | category | flops | bytes accessed | tf_op | source)
XLA Modules:
  0.0 28.9 jit_solution(6762279517425792237)
XLA Ops:
  0.6 0.0 copy-start
  0.6 1.0 %shard_map.68 = (f32[3,32,256]{2,1,0:T(8,128)S(1)}, f32[3,32,256]{2,1,0:T(8,128)S(1)}) custom-call(f32[1,4,32,256]{3,2,1,0:T(8,128)} %in_ref.1, s32[1,32,256]{2,1,0:T(8,128)} %class_ref.1), custom_call_target="tpu_custom_call" | custom-call | bytes 360448 | tf_op jit(solution)/shard_map/pallas_call | solution.py:34
  1.6 1.6 %collective-permute-start = (f32[3,32,256]{2,1,0:T(8,128)S(1)}, f32[3,32,256]{2,1,0:T(8,128)S(1)}, u32[]{:S(2)}, u32[]{:S(2)}) collective-permute-start(f32[3,32,256]{2,1,0:T(8,128)S(1)} %get-tuple-element.18), channel_id=1, source_target_pairs={{0,1},{1,0},{2,3},{3,2},{4,5},{5,4},{6,7},{7,6},{8,9},{9,8},{10,11... | collective-permute-start | bytes 294920 | tf_op jit(solution)/shard_map/ppermute | solution.py:510
  3.2 0.2 shard_map.69.own_ref
  3.4 0.8 %shard_map.70.table_ref = f32[3,16,8,128]{3,2,1,0:T(8,128)S(1)} custom-call(f32[18]{0:T(128)} %phase_hbm, f32[1,32]{1,0:T(1,128)} %bitcast.1), custom_call_target="tpu_custom_call" | custom-call | bytes 196808 | tf_op jit(solution)/shard_map/pallas_call | solution.py:34
  4.2 2.1 %collective-permute-done.got_ref = f32[3,32,256]{2,1,0:T(8,128)S(1)} collective-permute-done((f32[3,32,256]{2,1,0:T(8,128)S(1)}, f32[3,32,256]{2,1,0:T(8,128)S(1)}, u32[]{:S(2)}, u32[]{:S(2)}) %collective-permute-start) | collective-permute-done | bytes 98336 | tf_op jit(solution)/shard_map/ppermute | solution.py:510
  6.3 0.0 copy-done
  6.3 2.2 %shard_map.71 = (f32[2,8,2,8,128]{4,3,2,1,0:T(8,128)S(1)}, f32[2,8,2,8,128]{4,3,2,1,0:T(8,128)S(1)}, s32[8,2,8,128]{3,2,1,0:T(8,128)S(1)}) custom-call(f32[3,2,32,128]{3,2,1,0:T(8,128)S(1)} %shard_map.69.own_ref, f32[3,32,256]{2,1,0:T(8,128)S(1)} %collective-permute-done.got_ref, f32[3,16,8,128]{3,2,1,0:T(8,128)S(1)} %shard_map.70.table_ref, ...), custom_call_target="tpu_custom_call" | custom-call | flops 10485760 | bytes 983040 | tf_op jit(solution)/shard_map/pallas_call | solution.py:34
  8.5 0.1 collective-permute-start.1
  8.5 1.6 %collective-permute-start.2 = (f32[2,8,2,8,128]{4,3,2,1,0:T(8,128)S(1)}, f32[2,8,2,8,128]{4,3,2,1,0:T(8,128)S(1)}, u32[]{:S(2)}, u32[]{:S(2)}) collective-permute-start(f32[2,8,2,8,128]{4,3,2,1,0:T(8,128)S(1)} %get-tuple-element.22), channel_id=1, source_target_pairs={{0,1},{1,0},{2,6},{3,7},{4,5},{5,4},{6,8},{7,9},{8,2},{9,3},{10,14... | collective-permute-start | bytes 393224 | tf_op jit(solution)/shard_map/ppermute | solution.py:525
  10.2 0.8 %shard_map.73.coefficient_ref = f32[16,8,2,8,128]{4,3,2,1,0:T(8,128)S(1)} custom-call(s32[8,2,8,128]{3,2,1,0:T(8,128)S(1)} %get-tuple-element.23.blocks_ref, f32[3,16,8,128]{3,2,1,0:T(8,128)S(1)} %shard_map.70.table_ref), custom_call_target="tpu_custom_call" | custom-call | bytes 1310720 | tf_op jit(solution)/shard_map/pallas_call | solution.py:34
  10.9 0.8 %shard_map.74.coefficient_ref = f32[16,8,2,8,128]{4,3,2,1,0:T(8,128)S(1)} custom-call(s32[8,2,8,128]{3,2,1,0:T(8,128)S(1)} %get-tuple-element.23.blocks_ref, f32[3,16,8,128]{3,2,1,0:T(8,128)S(1)} %shard_map.70.table_ref), custom_call_target="tpu_custom_call" | custom-call | bytes 1310720 | tf_op jit(solution)/shard_map/pallas_call | solution.py:34
  11.7 0.3 shard_map.72
  12.0 2.3 %collective-permute-done.1.got_ref = f32[2,8,2,8,128]{4,3,2,1,0:T(8,128)S(1)} collective-permute-done((f32[2,8,2,8,128]{4,3,2,1,0:T(8,128)S(1)}, f32[2,8,2,8,128]{4,3,2,1,0:T(8,128)S(1)}, u32[]{:S(2)}, u32[]{:S(2)}) %collective-permute-start.1) | collective-permute-done | bytes 131104 | tf_op jit(solution)/shard_map/ppermute | solution.py:524
  14.3 0.0 collective-permute-done.2.crossed_ref.entered_ref
  14.3 1.6 %shard_map.75.blocks_ref = f32[2,8,2,8,128]{4,3,2,1,0:T(8,128)S(1)} custom-call(f32[2,8,2,8,128]{4,3,2,1,0:T(8,128)S(1)} %collective-permute-done.1.got_ref, f32[2,8,2,8,128]{4,3,2,1,0:T(8,128)S(1)} %collective-permute-done.2.crossed_ref.entered_ref, f32[2,8,2,8,128]{4,3,2,1,0:T(8,128)S(1)} %collective-permute-done.2.crossed_ref.entered_ref, ...), custom_call_target="tpu_custom_call" | custom-call | flops 10485760 | bytes 1835008 | tf_op jit(solution)/shard_map/pallas_call | solution.py:34
  15.9 0.3 collective-permute-start.4
  16.2 1.1 %collective-permute-start.5 = (f32[2,8,2,8,128]{4,3,2,1,0:T(8,128)S(1)}, f32[2,8,2,8,128]{4,3,2,1,0:T(8,128)S(1)}, u32[]{:S(2)}, u32[]{:S(2)}) collective-permute-start(f32[2,8,2,8,128]{4,3,2,1,0:T(8,128)S(1)} %shard_map.75.blocks_ref), channel_id=1, source_target_pairs={{0,2},{1,3},{2,0},{3,1},{4,5},{5,4},{6,8},{7,9},{8,12},{9,13},{10,... | collective-permute-start | bytes 393224 | tf_op jit(solution)/shard_map/ppermute | solution.py:525
  17.3 0.3 shard_map.76
  17.6 1.6 %collective-permute-start.3 = (f32[2,2,2,40,128]{4,3,2,1,0:T(8,128)S(1)}, f32[2,2,2,40,128]{4,3,2,1,0:T(8,128)S(1)}, u32[]{:S(2)}, u32[]{:S(2)}) collective-permute-start(f32[2,2,2,40,128]{4,3,2,1,0:T(8,128)S(1)} %get-tuple-element.28), channel_id=1, source_target_pairs={{0,1},{1,0},{2,3},{3,2},{4,5},{5,4},{6,7},{7,6},{8,9},{9,8},{10,11... | collective-permute-start | bytes 491528 | tf_op jit(solution)/shard_map/ppermute | solution.py:560
  19.2 2.6 %collective-permute-done.4.got_ref = f32[2,8,2,8,128]{4,3,2,1,0:T(8,128)S(1)} collective-permute-done((f32[2,8,2,8,128]{4,3,2,1,0:T(8,128)S(1)}, f32[2,8,2,8,128]{4,3,2,1,0:T(8,128)S(1)}, u32[]{:S(2)}, u32[]{:S(2)}) %collective-permute-start.4) | collective-permute-done | bytes 131104 | tf_op jit(solution)/shard_map/ppermute | solution.py:524
  21.8 0.0 collective-permute-done.5.crossed_ref
  21.8 1.8 %shard_map.78 = (f32[2,8,2,8,128]{4,3,2,1,0:T(8,128)S(1)}, f32[2,2,40,128]{3,2,1,0:T(8,128)S(1)}) custom-call(f32[2,8,2,8,128]{4,3,2,1,0:T(8,128)S(1)} %collective-permute-done.4.got_ref, f32[2,8,2,8,128]{4,3,2,1,0:T(8,128)S(1)} %collective-permute-done.5.crossed_ref, f32[2,8,2,8,128]{4,3,2,1,0:T(8,128)S(1)} %collective-permute-done.2.crossed_ref.entered_ref, ...), custom_call_target="tpu_custom_call" | custom-call | flops 10485760 | bytes 1916928 | tf_op jit(solution)/shard_map/pallas_call | solution.py:34
  23.6 1.6 %collective-permute-start.6 = (f32[2,2,40,128]{3,2,1,0:T(8,128)S(1)}, f32[2,2,40,128]{3,2,1,0:T(8,128)S(1)}, u32[]{:S(2)}, u32[]{:S(2)}) collective-permute-start(f32[2,2,40,128]{3,2,1,0:T(8,128)S(1)} %get-tuple-element.31), channel_id=1, source_target_pairs={{0,1},{1,0},{2,3},{3,2},{4,5},{5,4},{6,7},{7,6},{8,9},{9,8},{10,11... | collective-permute-start | bytes 245768 | tf_op jit(solution)/shard_map/ppermute | solution.py:562
  25.2 0.2 shard_map.79.mine_ref
  25.3 0.0 collective-permute-done.3.refs_2_
  25.3 0.1 shard_map.77.early_ref
  25.5 2.6 %collective-permute-done.6.got_ref = f32[2,2,40,128]{3,2,1,0:T(8,128)S(1)} collective-permute-done((f32[2,2,40,128]{3,2,1,0:T(8,128)S(1)}, f32[2,2,40,128]{3,2,1,0:T(8,128)S(1)}, u32[]{:S(2)}, u32[]{:S(2)}) %collective-permute-start.6) | collective-permute-done | bytes 81952 | tf_op jit(solution)/shard_map/ppermute | solution.py:562
  28.1 0.8 %shard_map.80 = (f32[1,8,32,256]{3,2,1,0:T(8,128)}, f32[1,4,32,256]{3,2,1,0:T(8,128)}) custom-call(f32[8,2,32,128]{3,2,1,0:T(8,128)S(1)} %shard_map.77.early_ref, f32[2,2,40,128]{3,2,1,0:T(8,128)S(1)} %shard_map.79.mine_ref, f32[2,2,40,128]{3,2,1,0:T(8,128)S(1)} %collective-permute-done.6.got_ref), custom_call_target="tpu_custom_call" | custom-call | bytes 819200 | tf_op jit(solution)/shard_map/pallas_call | solution.py:34
Async XLA Ops:
  0.6 5.7 %copy-start = (f32[2,4,32,256]{3,2,1,0:T(8,128)S(1)}, f32[2,4,32,256]{3,2,1,0:T(8,128)}, u32[]{:S(2)}) copy-start(f32[2,4,32,256]{3,2,1,0:T(8,128)} %enter_ref.5) | copy-start | bytes 786436
  1.6 4.7 %collective-permute-start = (f32[3,32,256]{2,1,0:T(8,128)S(1)}, f32[3,32,256]{2,1,0:T(8,128)S(1)}, u32[]{:S(2)}, u32[]{:S(2)}) collective-permute-start(f32[3,32,256]{2,1,0:T(8,128)S(1)} %get-tuple-element.18), channel_id=1, source_target_pairs={{0,1},{1,0},{2,3},{3,2},{4,5},{5,4},{6,7},{7,6},{8,9},{9,8},{10,11... | collective-permute-start | bytes 294920 | tf_op jit(solution)/shard_map/ppermute | solution.py:510
  8.5 5.8 %collective-permute-start.1 = (f32[2,8,2,8,128]{4,3,2,1,0:T(8,128)S(1)}, f32[2,8,2,8,128]{4,3,2,1,0:T(8,128)S(1)}, u32[]{:S(2)}, u32[]{:S(2)}) collective-permute-start(f32[2,8,2,8,128]{4,3,2,1,0:T(8,128)S(1)} %get-tuple-element.20.blocks_ref), channel_id=1, source_target_pairs={{0,2},{2,4},{4,6},{6,0},{8,10},{10,12},{12,14},{14,8},{16,18},{18,... | collective-permute-start | bytes 393224 | tf_op jit(solution)/shard_map/ppermute | solution.py:524
  8.5 5.8 %collective-permute-start.2 = (f32[2,8,2,8,128]{4,3,2,1,0:T(8,128)S(1)}, f32[2,8,2,8,128]{4,3,2,1,0:T(8,128)S(1)}, u32[]{:S(2)}, u32[]{:S(2)}) collective-permute-start(f32[2,8,2,8,128]{4,3,2,1,0:T(8,128)S(1)} %get-tuple-element.22), channel_id=1, source_target_pairs={{0,1},{1,0},{2,6},{3,7},{4,5},{5,4},{6,8},{7,9},{8,2},{9,3},{10,14... | collective-permute-start | bytes 393224 | tf_op jit(solution)/shard_map/ppermute | solution.py:525
  15.9 5.8 %collective-permute-start.4 = (f32[2,8,2,8,128]{4,3,2,1,0:T(8,128)S(1)}, f32[2,8,2,8,128]{4,3,2,1,0:T(8,128)S(1)}, u32[]{:S(2)}, u32[]{:S(2)}) collective-permute-start(f32[2,8,2,8,128]{4,3,2,1,0:T(8,128)S(1)} %shard_map.75.blocks_ref), channel_id=1, source_target_pairs={{0,2},{2,4},{4,6},{6,0},{8,10},{10,12},{12,14},{14,8},{16,18},{18,... | collective-permute-start | bytes 393224 | tf_op jit(solution)/shard_map/ppermute | solution.py:524
  16.2 5.6 %collective-permute-start.5 = (f32[2,8,2,8,128]{4,3,2,1,0:T(8,128)S(1)}, f32[2,8,2,8,128]{4,3,2,1,0:T(8,128)S(1)}, u32[]{:S(2)}, u32[]{:S(2)}) collective-permute-start(f32[2,8,2,8,128]{4,3,2,1,0:T(8,128)S(1)} %shard_map.75.blocks_ref), channel_id=1, source_target_pairs={{0,2},{1,3},{2,0},{3,1},{4,5},{5,4},{6,8},{7,9},{8,12},{9,13},{10,... | collective-permute-start | bytes 393224 | tf_op jit(solution)/shard_map/ppermute | solution.py:525
  17.6 7.8 %collective-permute-start.3 = (f32[2,2,2,40,128]{4,3,2,1,0:T(8,128)S(1)}, f32[2,2,2,40,128]{4,3,2,1,0:T(8,128)S(1)}, u32[]{:S(2)}, u32[]{:S(2)}) collective-permute-start(f32[2,2,2,40,128]{4,3,2,1,0:T(8,128)S(1)} %get-tuple-element.28), channel_id=1, source_target_pairs={{0,1},{1,0},{2,3},{3,2},{4,5},{5,4},{6,7},{7,6},{8,9},{9,8},{10,11... | collective-permute-start | bytes 491528 | tf_op jit(solution)/shard_map/ppermute | solution.py:560
  23.6 4.5 %collective-permute-start.6 = (f32[2,2,40,128]{3,2,1,0:T(8,128)S(1)}, f32[2,2,40,128]{3,2,1,0:T(8,128)S(1)}, u32[]{:S(2)}, u32[]{:S(2)}) collective-permute-start(f32[2,2,40,128]{3,2,1,0:T(8,128)S(1)} %get-tuple-element.31), channel_id=1, source_target_pairs={{0,1},{1,0},{2,3},{3,2},{4,5},{5,4},{6,7},{7,6},{8,9},{9,8},{10,11... | collective-permute-start | bytes 245768 | tf_op jit(solution)/shard_map/ppermute | solution.py:562

commit v5 on v4

--- a/solution.py
+++ b/solution.py
@@ -98,7 +98,7 @@
     )
 
 
-def advance(a, b, total, coefficients_of, valid_rows):
+def advance(a, b, total, coefficients_of, valid_rows, unrolled=False):
     length, tiles = a.shape[1], a.shape[2]
     tile = (SUBLANES, LANES)
     lane = lax.broadcasted_iota(jnp.int32, tile, 1)
@@ -174,7 +174,11 @@
         sweep(a, b, 2 * n + 1, True, False)
         return carry
 
-    lax.fori_loop(1, TERMS // 2, pair, 0)
+    if unrolled:
+        for n in range(1, TERMS // 2):
+            pair(n, 0)
+    else:
+        lax.fori_loop(1, TERMS // 2, pair, 0)
 
 
 def looked_up(classes, table, turn, side):
@@ -356,7 +360,7 @@
         lay(natural, own_ref[component], component, rows, side * strip_rows)
         place(natural, got_ref[component], component, rows, (1 - side) * strip_rows)
     gather_blocks(natural, a)
-    advance(a, b, hand_ref, looked_up(blocks_ref, table_ref, 0, side), None)
+    advance(a, b, hand_ref, looked_up(blocks_ref, table_ref, 0, side), None, unrolled=True)
     top = lax.axis_index("depth") == 0
 
     @pl.when(top)

time: 29 us -> 28.7 us (0.990)
  Pallas kernels: 10.7 us -> 10.3 us
    pallas_call x13, Pallas kernels: 10.7 us -> 10.3 us  [call(): pl.pallas_call(kernel, out_shape=outs, in_specs=in_specs, out_specs=out_s...]
where the time goes in v5:
time: 28.7 us; the launch traced here: 28.6 us
  Pallas kernels  10.3 us (36%)
  waiting for transfers between devices  9.65 us (34%)
  starting transfers between devices  7.82 us (27%)
  between operations  0.73 us (3%)
    pallas_call x13, Pallas kernels, call(): pl.pallas_call(kernel, out_shape=outs, in_specs=in_specs, out_specs=out_s...  10.3 us
    ppermute x2, waiting for transfers between devices, paired(): handed = lax.ppermute(hand, 'depth', ring)  4.93 us
    ppermute x2, waiting for transfers between devices, paired(): got = lax.ppermute(send, 'lat', swap)  4.71 us
    ppermute x2, starting transfers between devices, paired(): got = lax.ppermute(send, 'lat', swap)  3.17 us
    ppermute x2, starting transfers between devices, paired(): crossed = lax.ppermute(over, ('depth', 'lat'), cross[min(turn, 2)])  2.75 us
    ppermute x1, starting transfers between devices, paired(): earlier = lax.ppermute(send, 'lat', swap)  1.59 us
  transfers between devices with their start and end apart: 7, of which 4 were waited for; matrix products, arithmetic and copies ran while one was open for 0% of the time, Pallas kernels for 18%

profile of v5, /device:TPU:16, one launch (start us, length us, event | category | flops | bytes accessed | tf_op | source)
XLA Modules:
  0.0 28.6 jit_solution(11961847228656800203)
XLA Ops:
  0.6 0.0 copy-start
  0.6 1.0 %shard_map.68 = (f32[3,32,256]{2,1,0:T(8,128)S(1)}, f32[3,32,256]{2,1,0:T(8,128)S(1)}) custom-call(f32[1,4,32,256]{3,2,1,0:T(8,128)} %in_ref.1, s32[1,32,256]{2,1,0:T(8,128)} %class_ref.1), custom_call_target="tpu_custom_call" | custom-call | bytes 360448 | tf_op jit(solution)/shard_map/pallas_call | solution.py:34
  1.6 1.6 %collective-permute-start = (f32[3,32,256]{2,1,0:T(8,128)S(1)}, f32[3,32,256]{2,1,0:T(8,128)S(1)}, u32[]{:S(2)}, u32[]{:S(2)}) collective-permute-start(f32[3,32,256]{2,1,0:T(8,128)S(1)} %get-tuple-element.18), channel_id=1, source_target_pairs={{0,1},{1,0},{2,3},{3,2},{4,5},{5,4},{6,7},{7,6},{8,9},{9,8},{10,11... | collective-permute-start | bytes 294920 | tf_op jit(solution)/shard_map/ppermute | solution.py:514
  3.2 0.2 shard_map.69.own_ref
  3.4 0.8 %shard_map.70.table_ref = f32[3,16,8,128]{3,2,1,0:T(8,128)S(1)} custom-call(f32[18]{0:T(128)} %phase_hbm, f32[1,32]{1,0:T(1,128)} %bitcast.1), custom_call_target="tpu_custom_call" | custom-call | bytes 196808 | tf_op jit(solution)/shard_map/pallas_call | solution.py:34
  4.2 2.1 %collective-permute-done.got_ref = f32[3,32,256]{2,1,0:T(8,128)S(1)} collective-permute-done((f32[3,32,256]{2,1,0:T(8,128)S(1)}, f32[3,32,256]{2,1,0:T(8,128)S(1)}, u32[]{:S(2)}, u32[]{:S(2)}) %collective-permute-start) | collective-permute-done | bytes 98336 | tf_op jit(solution)/shard_map/ppermute | solution.py:514
  6.3 0.0 copy-done
  6.3 1.8 %shard_map.71 = (f32[2,8,2,8,128]{4,3,2,1,0:T(8,128)S(1)}, f32[2,8,2,8,128]{4,3,2,1,0:T(8,128)S(1)}, s32[8,2,8,128]{3,2,1,0:T(8,128)S(1)}) custom-call(f32[3,2,32,128]{3,2,1,0:T(8,128)S(1)} %shard_map.69.own_ref, f32[3,32,256]{2,1,0:T(8,128)S(1)} %collective-permute-done.got_ref, f32[3,16,8,128]{3,2,1,0:T(8,128)S(1)} %shard_map.70.table_ref, ...), custom_call_target="tpu_custom_call" | custom-call | flops 10485760 | bytes 983040 | tf_op jit(solution)/shard_map/pallas_call | solution.py:34
  8.1 0.1 collective-permute-start.1
  8.2 1.6 %collective-permute-start.2 = (f32[2,8,2,8,128]{4,3,2,1,0:T(8,128)S(1)}, f32[2,8,2,8,128]{4,3,2,1,0:T(8,128)S(1)}, u32[]{:S(2)}, u32[]{:S(2)}) collective-permute-start(f32[2,8,2,8,128]{4,3,2,1,0:T(8,128)S(1)} %get-tuple-element.22), channel_id=1, source_target_pairs={{0,1},{1,0},{2,6},{3,7},{4,5},{5,4},{6,8},{7,9},{8,2},{9,3},{10,14... | collective-permute-start | bytes 393224 | tf_op jit(solution)/shard_map/ppermute | solution.py:529
  9.9 0.8 %shard_map.73.coefficient_ref = f32[16,8,2,8,128]{4,3,2,1,0:T(8,128)S(1)} custom-call(s32[8,2,8,128]{3,2,1,0:T(8,128)S(1)} %get-tuple-element.23.blocks_ref, f32[3,16,8,128]{3,2,1,0:T(8,128)S(1)} %shard_map.70.table_ref), custom_call_target="tpu_custom_call" | custom-call | bytes 1310720 | tf_op jit(solution)/shard_map/pallas_call | solution.py:34
  10.6 0.8 %shard_map.74.coefficient_ref = f32[16,8,2,8,128]{4,3,2,1,0:T(8,128)S(1)} custom-call(s32[8,2,8,128]{3,2,1,0:T(8,128)S(1)} %get-tuple-element.23.blocks_ref, f32[3,16,8,128]{3,2,1,0:T(8,128)S(1)} %shard_map.70.table_ref), custom_call_target="tpu_custom_call" | custom-call | bytes 1310720 | tf_op jit(solution)/shard_map/pallas_call | solution.py:34
  11.4 0.3 shard_map.72
  11.7 2.3 %collective-permute-done.1.got_ref = f32[2,8,2,8,128]{4,3,2,1,0:T(8,128)S(1)} collective-permute-done((f32[2,8,2,8,128]{4,3,2,1,0:T(8,128)S(1)}, f32[2,8,2,8,128]{4,3,2,1,0:T(8,128)S(1)}, u32[]{:S(2)}, u32[]{:S(2)}) %collective-permute-start.1) | collective-permute-done | bytes 131104 | tf_op jit(solution)/shard_map/ppermute | solution.py:528
  14.0 0.0 collective-permute-done.2.crossed_ref.entered_ref
  14.0 1.6 %shard_map.75.blocks_ref = f32[2,8,2,8,128]{4,3,2,1,0:T(8,128)S(1)} custom-call(f32[2,8,2,8,128]{4,3,2,1,0:T(8,128)S(1)} %collective-permute-done.1.got_ref, f32[2,8,2,8,128]{4,3,2,1,0:T(8,128)S(1)} %collective-permute-done.2.crossed_ref.entered_ref, f32[2,8,2,8,128]{4,3,2,1,0:T(8,128)S(1)} %collective-permute-done.2.crossed_ref.entered_ref, ...), custom_call_target="tpu_custom_call" | custom-call | flops 10485760 | bytes 1835008 | tf_op jit(solution)/shard_map/pallas_call | solution.py:34
  15.6 0.3 collective-permute-start.4
  15.9 1.1 %collective-permute-start.5 = (f32[2,8,2,8,128]{4,3,2,1,0:T(8,128)S(1)}, f32[2,8,2,8,128]{4,3,2,1,0:T(8,128)S(1)}, u32[]{:S(2)}, u32[]{:S(2)}) collective-permute-start(f32[2,8,2,8,128]{4,3,2,1,0:T(8,128)S(1)} %shard_map.75.blocks_ref), channel_id=1, source_target_pairs={{0,2},{1,3},{2,0},{3,1},{4,5},{5,4},{6,8},{7,9},{8,12},{9,13},{10,... | collective-permute-start | bytes 393224 | tf_op jit(solution)/shard_map/ppermute | solution.py:529
  17.0 0.3 shard_map.76
  17.3 1.6 %collective-permute-start.3 = (f32[2,2,2,40,128]{4,3,2,1,0:T(8,128)S(1)}, f32[2,2,2,40,128]{4,3,2,1,0:T(8,128)S(1)}, u32[]{:S(2)}, u32[]{:S(2)}) collective-permute-start(f32[2,2,2,40,128]{4,3,2,1,0:T(8,128)S(1)} %get-tuple-element.28), channel_id=1, source_target_pairs={{0,1},{1,0},{2,3},{3,2},{4,5},{5,4},{6,7},{7,6},{8,9},{9,8},{10,11... | collective-permute-start | bytes 491528 | tf_op jit(solution)/shard_map/ppermute | solution.py:564
  18.8 2.6 %collective-permute-done.4.got_ref = f32[2,8,2,8,128]{4,3,2,1,0:T(8,128)S(1)} collective-permute-done((f32[2,8,2,8,128]{4,3,2,1,0:T(8,128)S(1)}, f32[2,8,2,8,128]{4,3,2,1,0:T(8,128)S(1)}, u32[]{:S(2)}, u32[]{:S(2)}) %collective-permute-start.4) | collective-permute-done | bytes 131104 | tf_op jit(solution)/shard_map/ppermute | solution.py:528
  21.5 0.0 collective-permute-done.5.crossed_ref
  21.5 1.8 %shard_map.78 = (f32[2,8,2,8,128]{4,3,2,1,0:T(8,128)S(1)}, f32[2,2,40,128]{3,2,1,0:T(8,128)S(1)}) custom-call(f32[2,8,2,8,128]{4,3,2,1,0:T(8,128)S(1)} %collective-permute-done.4.got_ref, f32[2,8,2,8,128]{4,3,2,1,0:T(8,128)S(1)} %collective-permute-done.5.crossed_ref, f32[2,8,2,8,128]{4,3,2,1,0:T(8,128)S(1)} %collective-permute-done.2.crossed_ref.entered_ref, ...), custom_call_target="tpu_custom_call" | custom-call | flops 10485760 | bytes 1916928 | tf_op jit(solution)/shard_map/pallas_call | solution.py:34
  23.3 1.6 %collective-permute-start.6 = (f32[2,2,40,128]{3,2,1,0:T(8,128)S(1)}, f32[2,2,40,128]{3,2,1,0:T(8,128)S(1)}, u32[]{:S(2)}, u32[]{:S(2)}) collective-permute-start(f32[2,2,40,128]{3,2,1,0:T(8,128)S(1)} %get-tuple-element.31), channel_id=1, source_target_pairs={{0,1},{1,0},{2,3},{3,2},{4,5},{5,4},{6,7},{7,6},{8,9},{9,8},{10,11... | collective-permute-start | bytes 245768 | tf_op jit(solution)/shard_map/ppermute | solution.py:566
  24.8 0.2 shard_map.79.mine_ref
  25.0 0.0 collective-permute-done.3.refs_2_
  25.0 0.1 shard_map.77.early_ref
  25.2 2.6 %collective-permute-done.6.got_ref = f32[2,2,40,128]{3,2,1,0:T(8,128)S(1)} collective-permute-done((f32[2,2,40,128]{3,2,1,0:T(8,128)S(1)}, f32[2,2,40,128]{3,2,1,0:T(8,128)S(1)}, u32[]{:S(2)}, u32[]{:S(2)}) %collective-permute-start.6) | collective-permute-done | bytes 81952 | tf_op jit(solution)/shard_map/ppermute | solution.py:566
  27.8 0.8 %shard_map.80 = (f32[1,8,32,256]{3,2,1,0:T(8,128)}, f32[1,4,32,256]{3,2,1,0:T(8,128)}) custom-call(f32[8,2,32,128]{3,2,1,0:T(8,128)S(1)} %shard_map.77.early_ref, f32[2,2,40,128]{3,2,1,0:T(8,128)S(1)} %shard_map.79.mine_ref, f32[2,2,40,128]{3,2,1,0:T(8,128)S(1)} %collective-permute-done.6.got_ref), custom_call_target="tpu_custom_call" | custom-call | bytes 819200 | tf_op jit(solution)/shard_map/pallas_call | solution.py:34
Async XLA Ops:
  0.6 5.7 %copy-start = (f32[2,4,32,256]{3,2,1,0:T(8,128)S(1)}, f32[2,4,32,256]{3,2,1,0:T(8,128)}, u32[]{:S(2)}) copy-start(f32[2,4,32,256]{3,2,1,0:T(8,128)} %enter_ref.5) | copy-start | bytes 786436
  1.6 4.7 %collective-permute-start = (f32[3,32,256]{2,1,0:T(8,128)S(1)}, f32[3,32,256]{2,1,0:T(8,128)S(1)}, u32[]{:S(2)}, u32[]{:S(2)}) collective-permute-start(f32[3,32,256]{2,1,0:T(8,128)S(1)} %get-tuple-element.18), channel_id=1, source_target_pairs={{0,1},{1,0},{2,3},{3,2},{4,5},{5,4},{6,7},{7,6},{8,9},{9,8},{10,11... | collective-permute-start | bytes 294920 | tf_op jit(solution)/shard_map/ppermute | solution.py:514
  8.1 5.8 %collective-permute-start.1 = (f32[2,8,2,8,128]{4,3,2,1,0:T(8,128)S(1)}, f32[2,8,2,8,128]{4,3,2,1,0:T(8,128)S(1)}, u32[]{:S(2)}, u32[]{:S(2)}) collective-permute-start(f32[2,8,2,8,128]{4,3,2,1,0:T(8,128)S(1)} %get-tuple-element.20.blocks_ref), channel_id=1, source_target_pairs={{0,2},{2,4},{4,6},{6,0},{8,10},{10,12},{12,14},{14,8},{16,18},{18,... | collective-permute-start | bytes 393224 | tf_op jit(solution)/shard_map/ppermute | solution.py:528
  8.2 5.8 %collective-permute-start.2 = (f32[2,8,2,8,128]{4,3,2,1,0:T(8,128)S(1)}, f32[2,8,2,8,128]{4,3,2,1,0:T(8,128)S(1)}, u32[]{:S(2)}, u32[]{:S(2)}) collective-permute-start(f32[2,8,2,8,128]{4,3,2,1,0:T(8,128)S(1)} %get-tuple-element.22), channel_id=1, source_target_pairs={{0,1},{1,0},{2,6},{3,7},{4,5},{5,4},{6,8},{7,9},{8,2},{9,3},{10,14... | collective-permute-start | bytes 393224 | tf_op jit(solution)/shard_map/ppermute | solution.py:529
  15.6 5.8 %collective-permute-start.4 = (f32[2,8,2,8,128]{4,3,2,1,0:T(8,128)S(1)}, f32[2,8,2,8,128]{4,3,2,1,0:T(8,128)S(1)}, u32[]{:S(2)}, u32[]{:S(2)}) collective-permute-start(f32[2,8,2,8,128]{4,3,2,1,0:T(8,128)S(1)} %shard_map.75.blocks_ref), channel_id=1, source_target_pairs={{0,2},{2,4},{4,6},{6,0},{8,10},{10,12},{12,14},{14,8},{16,18},{18,... | collective-permute-start | bytes 393224 | tf_op jit(solution)/shard_map/ppermute | solution.py:528
  15.9 5.6 %collective-permute-start.5 = (f32[2,8,2,8,128]{4,3,2,1,0:T(8,128)S(1)}, f32[2,8,2,8,128]{4,3,2,1,0:T(8,128)S(1)}, u32[]{:S(2)}, u32[]{:S(2)}) collective-permute-start(f32[2,8,2,8,128]{4,3,2,1,0:T(8,128)S(1)} %shard_map.75.blocks_ref), channel_id=1, source_target_pairs={{0,2},{1,3},{2,0},{3,1},{4,5},{5,4},{6,8},{7,9},{8,12},{9,13},{10,... | collective-permute-start | bytes 393224 | tf_op jit(solution)/shard_map/ppermute | solution.py:529
  17.3 7.8 %collective-permute-start.3 = (f32[2,2,2,40,128]{4,3,2,1,0:T(8,128)S(1)}, f32[2,2,2,40,128]{4,3,2,1,0:T(8,128)S(1)}, u32[]{:S(2)}, u32[]{:S(2)}) collective-permute-start(f32[2,2,2,40,128]{4,3,2,1,0:T(8,128)S(1)} %get-tuple-element.28), channel_id=1, source_target_pairs={{0,1},{1,0},{2,3},{3,2},{4,5},{5,4},{6,7},{7,6},{8,9},{9,8},{10,11... | collective-permute-start | bytes 491528 | tf_op jit(solution)/shard_map/ppermute | solution.py:564
  23.3 4.5 %collective-permute-start.6 = (f32[2,2,40,128]{3,2,1,0:T(8,128)S(1)}, f32[2,2,40,128]{3,2,1,0:T(8,128)S(1)}, u32[]{:S(2)}, u32[]{:S(2)}) collective-permute-start(f32[2,2,40,128]{3,2,1,0:T(8,128)S(1)} %get-tuple-element.31), channel_id=1, source_target_pairs={{0,1},{1,0},{2,3},{3,2},{4,5},{5,4},{6,7},{7,6},{8,9},{9,8},{10,11... | collective-permute-start | bytes 245768 | tf_op jit(solution)/shard_map/ppermute | solution.py:566

commit v6 on v5

--- a/solution.py
+++ b/solution.py
@@ -178,7 +178,8 @@
         for n in range(1, TERMS // 2):
             pair(n, 0)
     else:
-        lax.fori_loop(1, TERMS // 2, pair, 0)
+        pair(1, 0)
+        lax.fori_loop(1, TERMS // 4, lambda n, carry: pair(2 * n + 1, pair(2 * n, carry)), 0)
 
 
 def looked_up(classes, table, turn, side):
@@ -289,22 +290,18 @@
             natural[h, pl.ds(at, SUBLANES), :] = part
 
 
-def split_kernel(in_ref, class_ref, own_ref, send_ref, whole_classes, sem):
-    side = lax.axis_index("lat")
+def strips_of(in_ref, class_ref, which, target, whole_classes, sem):
     cells = pltpu.make_async_copy(class_ref.at[0], whole_classes, sem.at[0])
+    fields = pltpu.make_async_copy(in_ref.at[0, pl.ds(2 * which, 2)], target.at[pl.ds(0, 2)], sem.at[1])
     cells.start()
-    copies = [
-        pltpu.make_async_copy(in_ref.at[0, pl.ds(2 * which, 2)], ref.at[pl.ds(0, 2)], sem.at[j])
-        for j, (ref, which) in enumerate(((send_ref, 1 - side), (own_ref, side)), 1)
-    ]
-    for copy in copies:
-        copy.start()
+    fields.start()
     cells.wait()
-    as_float = whole_classes[...].astype(jnp.float32)
-    own_ref[2] = as_float
-    send_ref[2] = as_float
-    for copy in copies:
-        copy.wait()
+    target[2] = whole_classes[...].astype(jnp.float32)
+    fields.wait()
+
+
+def split_kernel(in_ref, class_ref, send_ref, whole_classes, sem):
+    strips_of(in_ref, class_ref, 1 - lax.axis_index("lat"), send_ref, whole_classes, sem)
 
 
 def pack(fields, first, target):
@@ -327,7 +324,8 @@
             natural[h, pl.ds(at, SUBLANES), :] = part
 
 
-def weave_kernel(strips_ref, out_ref):
+def weave_kernel(in_ref, class_ref, out_ref, strips_ref, whole_classes, sem):
+    strips_of(in_ref, class_ref, lax.axis_index("lat"), strips_ref, whole_classes, sem)
     tiles = out_ref.shape[1]
     for n in range(strips_ref.shape[0]):
         for r in range(0, strips_ref.shape[1], SUBLANES):
@@ -504,16 +502,17 @@
     strips = f32(3, strip_rows, width)
     flops = 20 * TERMS * 4 * strip_rows * width
 
-    own, send = call(
-        split_kernel,
-        [strips, strips],
+    loads = [pltpu.VMEM((strip_rows, width), jnp.int32), pltpu.SemaphoreType.DMA((2,))]
+    (send,) = call(split_kernel, [strips], [HBM, HBM], loads, in_hbm(in_flight, classes))
+    got = lax.ppermute(send, "lat", swap)
+    freq_phase, in_flight, _ = lax.optimization_barrier((freq_phase, in_flight, send))
+    (own,) = call(
+        weave_kernel,
+        [f32(3, tiles, strip_rows, LANES)],
         [HBM, HBM],
-        [pltpu.VMEM((strip_rows, width), jnp.int32), pltpu.SemaphoreType.DMA((3,))],
+        [pltpu.VMEM(strips.shape, jnp.float32), *loads],
         in_hbm(in_flight, classes),
     )
-    got = lax.ppermute(send, "lat", swap)
-    freq_phase, _ = lax.optimization_barrier((freq_phase, own))
-    (own,) = call(weave_kernel, [f32(3, tiles, strip_rows, LANES)], [VMEM], [], (own,))
     table = coefficients(freq_phase, class_slowness)
     hand, over, cells = call(
         first_kernel,

time: 28.7 us -> 28.7 us (level)
  Pallas kernels: 10.3 us -> 11.2 us
  waiting for transfers between devices: 9.65 us -> 8.77 us
    ppermute x2, waiting for transfers between devices: 4.71 us -> 3.82 us  [paired(): got = lax.ppermute(send, 'lat', swap)]
    pallas_call x13, Pallas kernels: 10.3 us -> 11.2 us  [call(): pl.pallas_call(kernel, out_shape=outs, in_specs=in_specs, out_specs=out_s...]
  transfers between devices with their start and end apart: 7 -> 7, of which waited for: 4 -> 4; matrix products, arithmetic and copies ran while one was open for 0% -> 0% of each run, Pallas kernels for 18% -> 21%
where the time goes in v6:
time: 28.7 us; the launch traced here: 28.5 us
  Pallas kernels  11.2 us (39%)
  waiting for transfers between devices  8.77 us (31%)
  starting transfers between devices  7.82 us (27%)
  between operations  0.73 us (3%)
    pallas_call x13, Pallas kernels, call(): pl.pallas_call(kernel, out_shape=outs, in_specs=in_specs, out_specs=out_s...  11.2 us
    ppermute x2, waiting for transfers between devices, paired(): handed = lax.ppermute(hand, 'depth', ring)  4.93 us
    ppermute x2, waiting for transfers between devices, paired(): got = lax.ppermute(send, 'lat', swap)  3.82 us
    ppermute x2, starting transfers between devices, paired(): got = lax.ppermute(send, 'lat', swap)  3.17 us
    ppermute x2, starting transfers between devices, paired(): crossed = lax.ppermute(over, ('depth', 'lat'), cross[min(turn, 2)])  2.75 us
    ppermute x1, starting transfers between devices, paired(): earlier = lax.ppermute(send, 'lat', swap)  1.59 us
  transfers between devices with their start and end apart: 7, of which 4 were waited for; matrix products, arithmetic and copies ran while one was open for 0% of the time, Pallas kernels for 21%

profile of v6, /device:TPU:16, one launch (start us, length us, event | category | flops | bytes accessed | tf_op | source)
XLA Modules:
  0.0 28.5 jit_solution(15889653232093395342)
XLA Ops:
  0.6 0.9 %shard_map.68 = f32[3,32,256]{2,1,0:T(8,128)S(1)} custom-call(f32[1,4,32,256]{3,2,1,0:T(8,128)} %in_ref.2, s32[1,32,256]{2,1,0:T(8,128)} %class_ref.3), custom_call_target="tpu_custom_call" | custom-call | bytes 262144 | tf_op jit(solution)/shard_map/pallas_call | solution.py:34
  1.5 0.0 copy-start
  1.5 1.6 %collective-permute-start = (f32[3,32,256]{2,1,0:T(8,128)S(1)}, f32[3,32,256]{2,1,0:T(8,128)S(1)}, u32[]{:S(2)}, u32[]{:S(2)}) collective-permute-start(f32[3,32,256]{2,1,0:T(8,128)S(1)} %shard_map.68), channel_id=1, source_target_pairs={{0,1},{1,0},{2,3},{3,2},{4,5},{5,4},{6,7},{7,6},{8,9},{9,8},{10,11... | collective-permute-start | bytes 294920 | tf_op jit(solution)/shard_map/ppermute | solution.py:507
  3.1 1.1 %shard_map.69.own_ref = f32[3,2,32,128]{3,2,1,0:T(8,128)S(1)} custom-call(f32[1,4,32,256]{3,2,1,0:T(8,128)} %in_ref.2, s32[1,32,256]{2,1,0:T(8,128)} %class_ref.3), custom_call_target="tpu_custom_call" | custom-call | bytes 262144 | tf_op jit(solution)/shard_map/pallas_call | solution.py:34
  4.2 0.8 %shard_map.70.table_ref = f32[3,16,8,128]{3,2,1,0:T(8,128)S(1)} custom-call(f32[18]{0:T(128)} %phase_hbm, f32[1,32]{1,0:T(1,128)} %bitcast.1), custom_call_target="tpu_custom_call" | custom-call | bytes 196808 | tf_op jit(solution)/shard_map/pallas_call | solution.py:34
  5.0 1.2 %collective-permute-done.got_ref = f32[3,32,256]{2,1,0:T(8,128)S(1)} collective-permute-done((f32[3,32,256]{2,1,0:T(8,128)S(1)}, f32[3,32,256]{2,1,0:T(8,128)S(1)}, u32[]{:S(2)}, u32[]{:S(2)}) %collective-permute-start) | collective-permute-done | bytes 98336 | tf_op jit(solution)/shard_map/ppermute | solution.py:507
  6.2 0.0 copy-done
  6.2 1.8 %shard_map.71 = (f32[2,8,2,8,128]{4,3,2,1,0:T(8,128)S(1)}, f32[2,8,2,8,128]{4,3,2,1,0:T(8,128)S(1)}, s32[8,2,8,128]{3,2,1,0:T(8,128)S(1)}) custom-call(f32[3,2,32,128]{3,2,1,0:T(8,128)S(1)} %shard_map.69.own_ref, f32[3,32,256]{2,1,0:T(8,128)S(1)} %collective-permute-done.got_ref, f32[3,16,8,128]{3,2,1,0:T(8,128)S(1)} %shard_map.70.table_ref, ...), custom_call_target="tpu_custom_call" | custom-call | flops 10485760 | bytes 983040 | tf_op jit(solution)/shard_map/pallas_call | solution.py:34
  8.1 0.1 collective-permute-start.1
  8.1 1.6 %collective-permute-start.2 = (f32[2,8,2,8,128]{4,3,2,1,0:T(8,128)S(1)}, f32[2,8,2,8,128]{4,3,2,1,0:T(8,128)S(1)}, u32[]{:S(2)}, u32[]{:S(2)}) collective-permute-start(f32[2,8,2,8,128]{4,3,2,1,0:T(8,128)S(1)} %get-tuple-element.20), channel_id=1, source_target_pairs={{0,1},{1,0},{2,6},{3,7},{4,5},{5,4},{6,8},{7,9},{8,2},{9,3},{10,14... | collective-permute-start | bytes 393224 | tf_op jit(solution)/shard_map/ppermute | solution.py:528
  9.8 0.8 %shard_map.73.coefficient_ref = f32[16,8,2,8,128]{4,3,2,1,0:T(8,128)S(1)} custom-call(s32[8,2,8,128]{3,2,1,0:T(8,128)S(1)} %get-tuple-element.21.blocks_ref, f32[3,16,8,128]{3,2,1,0:T(8,128)S(1)} %shard_map.70.table_ref), custom_call_target="tpu_custom_call" | custom-call | bytes 1310720 | tf_op jit(solution)/shard_map/pallas_call | solution.py:34
  10.5 0.8 %shard_map.74.coefficient_ref = f32[16,8,2,8,128]{4,3,2,1,0:T(8,128)S(1)} custom-call(s32[8,2,8,128]{3,2,1,0:T(8,128)S(1)} %get-tuple-element.21.blocks_ref, f32[3,16,8,128]{3,2,1,0:T(8,128)S(1)} %shard_map.70.table_ref), custom_call_target="tpu_custom_call" | custom-call | bytes 1310720 | tf_op jit(solution)/shard_map/pallas_call | solution.py:34
  11.3 0.3 shard_map.72
  11.6 2.3 %collective-permute-done.1.got_ref = f32[2,8,2,8,128]{4,3,2,1,0:T(8,128)S(1)} collective-permute-done((f32[2,8,2,8,128]{4,3,2,1,0:T(8,128)S(1)}, f32[2,8,2,8,128]{4,3,2,1,0:T(8,128)S(1)}, u32[]{:S(2)}, u32[]{:S(2)}) %collective-permute-start.1) | collective-permute-done | bytes 131104 | tf_op jit(solution)/shard_map/ppermute | solution.py:527
  13.9 0.0 collective-permute-done.2.crossed_ref.entered_ref
  13.9 1.6 %shard_map.75.blocks_ref = f32[2,8,2,8,128]{4,3,2,1,0:T(8,128)S(1)} custom-call(f32[2,8,2,8,128]{4,3,2,1,0:T(8,128)S(1)} %collective-permute-done.1.got_ref, f32[2,8,2,8,128]{4,3,2,1,0:T(8,128)S(1)} %collective-permute-done.2.crossed_ref.entered_ref, f32[2,8,2,8,128]{4,3,2,1,0:T(8,128)S(1)} %collective-permute-done.2.crossed_ref.entered_ref, ...), custom_call_target="tpu_custom_call" | custom-call | flops 10485760 | bytes 1835008 | tf_op jit(solution)/shard_map/pallas_call | solution.py:34
  15.6 0.3 collective-permute-start.4
  15.8 1.1 %collective-permute-start.5 = (f32[2,8,2,8,128]{4,3,2,1,0:T(8,128)S(1)}, f32[2,8,2,8,128]{4,3,2,1,0:T(8,128)S(1)}, u32[]{:S(2)}, u32[]{:S(2)}) collective-permute-start(f32[2,8,2,8,128]{4,3,2,1,0:T(8,128)S(1)} %shard_map.75.blocks_ref), channel_id=1, source_target_pairs={{0,2},{1,3},{2,0},{3,1},{4,5},{5,4},{6,8},{7,9},{8,12},{9,13},{10,... | collective-permute-start | bytes 393224 | tf_op jit(solution)/shard_map/ppermute | solution.py:528
  16.9 0.3 shard_map.76
  17.2 1.6 %collective-permute-start.3 = (f32[2,2,2,40,128]{4,3,2,1,0:T(8,128)S(1)}, f32[2,2,2,40,128]{4,3,2,1,0:T(8,128)S(1)}, u32[]{:S(2)}, u32[]{:S(2)}) collective-permute-start(f32[2,2,2,40,128]{4,3,2,1,0:T(8,128)S(1)} %get-tuple-element.26), channel_id=1, source_target_pairs={{0,1},{1,0},{2,3},{3,2},{4,5},{5,4},{6,7},{7,6},{8,9},{9,8},{10,11... | collective-permute-start | bytes 491528 | tf_op jit(solution)/shard_map/ppermute | solution.py:563
  18.8 2.6 %collective-permute-done.4.got_ref = f32[2,8,2,8,128]{4,3,2,1,0:T(8,128)S(1)} collective-permute-done((f32[2,8,2,8,128]{4,3,2,1,0:T(8,128)S(1)}, f32[2,8,2,8,128]{4,3,2,1,0:T(8,128)S(1)}, u32[]{:S(2)}, u32[]{:S(2)}) %collective-permute-start.4) | collective-permute-done | bytes 131104 | tf_op jit(solution)/shard_map/ppermute | solution.py:527
  21.4 0.0 collective-permute-done.5.crossed_ref
  21.4 1.8 %shard_map.78 = (f32[2,8,2,8,128]{4,3,2,1,0:T(8,128)S(1)}, f32[2,2,40,128]{3,2,1,0:T(8,128)S(1)}) custom-call(f32[2,8,2,8,128]{4,3,2,1,0:T(8,128)S(1)} %collective-permute-done.4.got_ref, f32[2,8,2,8,128]{4,3,2,1,0:T(8,128)S(1)} %collective-permute-done.5.crossed_ref, f32[2,8,2,8,128]{4,3,2,1,0:T(8,128)S(1)} %collective-permute-done.2.crossed_ref.entered_ref, ...), custom_call_target="tpu_custom_call" | custom-call | flops 10485760 | bytes 1916928 | tf_op jit(solution)/shard_map/pallas_call | solution.py:34
  23.2 1.6 %collective-permute-start.6 = (f32[2,2,40,128]{3,2,1,0:T(8,128)S(1)}, f32[2,2,40,128]{3,2,1,0:T(8,128)S(1)}, u32[]{:S(2)}, u32[]{:S(2)}) collective-permute-start(f32[2,2,40,128]{3,2,1,0:T(8,128)S(1)} %get-tuple-element.29), channel_id=1, source_target_pairs={{0,1},{1,0},{2,3},{3,2},{4,5},{5,4},{6,7},{7,6},{8,9},{9,8},{10,11... | collective-permute-start | bytes 245768 | tf_op jit(solution)/shard_map/ppermute | solution.py:565
  24.8 0.2 shard_map.79.mine_ref
  25.0 0.0 collective-permute-done.3.refs_2_
  25.0 0.1 shard_map.77.early_ref
  25.1 2.6 %collective-permute-done.6.got_ref = f32[2,2,40,128]{3,2,1,0:T(8,128)S(1)} collective-permute-done((f32[2,2,40,128]{3,2,1,0:T(8,128)S(1)}, f32[2,2,40,128]{3,2,1,0:T(8,128)S(1)}, u32[]{:S(2)}, u32[]{:S(2)}) %collective-permute-start.6) | collective-permute-done | bytes 81952 | tf_op jit(solution)/shard_map/ppermute | solution.py:565
  27.7 0.8 %shard_map.80 = (f32[1,8,32,256]{3,2,1,0:T(8,128)}, f32[1,4,32,256]{3,2,1,0:T(8,128)}) custom-call(f32[8,2,32,128]{3,2,1,0:T(8,128)S(1)} %shard_map.77.early_ref, f32[2,2,40,128]{3,2,1,0:T(8,128)S(1)} %shard_map.79.mine_ref, f32[2,2,40,128]{3,2,1,0:T(8,128)S(1)} %collective-permute-done.6.got_ref), custom_call_target="tpu_custom_call" | custom-call | bytes 819200 | tf_op jit(solution)/shard_map/pallas_call | solution.py:34
Async XLA Ops:
  1.5 4.7 %copy-start = (f32[2,4,32,256]{3,2,1,0:T(8,128)S(1)}, f32[2,4,32,256]{3,2,1,0:T(8,128)}, u32[]{:S(2)}) copy-start(f32[2,4,32,256]{3,2,1,0:T(8,128)} %enter_ref.5) | copy-start | bytes 786436
  1.5 4.7 %collective-permute-start = (f32[3,32,256]{2,1,0:T(8,128)S(1)}, f32[3,32,256]{2,1,0:T(8,128)S(1)}, u32[]{:S(2)}, u32[]{:S(2)}) collective-permute-start(f32[3,32,256]{2,1,0:T(8,128)S(1)} %shard_map.68), channel_id=1, source_target_pairs={{0,1},{1,0},{2,3},{3,2},{4,5},{5,4},{6,7},{7,6},{8,9},{9,8},{10,11... | collective-permute-start | bytes 294920 | tf_op jit(solution)/shard_map/ppermute | solution.py:507
  8.1 5.8 %collective-permute-start.1 = (f32[2,8,2,8,128]{4,3,2,1,0:T(8,128)S(1)}, f32[2,8,2,8,128]{4,3,2,1,0:T(8,128)S(1)}, u32[]{:S(2)}, u32[]{:S(2)}) collective-permute-start(f32[2,8,2,8,128]{4,3,2,1,0:T(8,128)S(1)} %get-tuple-element.18.blocks_ref), channel_id=1, source_target_pairs={{0,2},{2,4},{4,6},{6,0},{8,10},{10,12},{12,14},{14,8},{16,18},{18,... | collective-permute-start | bytes 393224 | tf_op jit(solution)/shard_map/ppermute | solution.py:527
  8.1 5.8 %collective-permute-start.2 = (f32[2,8,2,8,128]{4,3,2,1,0:T(8,128)S(1)}, f32[2,8,2,8,128]{4,3,2,1,0:T(8,128)S(1)}, u32[]{:S(2)}, u32[]{:S(2)}) collective-permute-start(f32[2,8,2,8,128]{4,3,2,1,0:T(8,128)S(1)} %get-tuple-element.20), channel_id=1, source_target_pairs={{0,1},{1,0},{2,6},{3,7},{4,5},{5,4},{6,8},{7,9},{8,2},{9,3},{10,14... | collective-permute-start | bytes 393224 | tf_op jit(solution)/shard_map/ppermute | solution.py:528
  15.6 5.8 %collective-permute-start.4 = (f32[2,8,2,8,128]{4,3,2,1,0:T(8,128)S(1)}, f32[2,8,2,8,128]{4,3,2,1,0:T(8,128)S(1)}, u32[]{:S(2)}, u32[]{:S(2)}) collective-permute-start(f32[2,8,2,8,128]{4,3,2,1,0:T(8,128)S(1)} %shard_map.75.blocks_ref), channel_id=1, source_target_pairs={{0,2},{2,4},{4,6},{6,0},{8,10},{10,12},{12,14},{14,8},{16,18},{18,... | collective-permute-start | bytes 393224 | tf_op jit(solution)/shard_map/ppermute | solution.py:527
  15.8 5.6 %collective-permute-start.5 = (f32[2,8,2,8,128]{4,3,2,1,0:T(8,128)S(1)}, f32[2,8,2,8,128]{4,3,2,1,0:T(8,128)S(1)}, u32[]{:S(2)}, u32[]{:S(2)}) collective-permute-start(f32[2,8,2,8,128]{4,3,2,1,0:T(8,128)S(1)} %shard_map.75.blocks_ref), channel_id=1, source_target_pairs={{0,2},{1,3},{2,0},{3,1},{4,5},{5,4},{6,8},{7,9},{8,12},{9,13},{10,... | collective-permute-start | bytes 393224 | tf_op jit(solution)/shard_map/ppermute | solution.py:528
  17.2 7.8 %collective-permute-start.3 = (f32[2,2,2,40,128]{4,3,2,1,0:T(8,128)S(1)}, f32[2,2,2,40,128]{4,3,2,1,0:T(8,128)S(1)}, u32[]{:S(2)}, u32[]{:S(2)}) collective-permute-start(f32[2,2,2,40,128]{4,3,2,1,0:T(8,128)S(1)} %get-tuple-element.26), channel_id=1, source_target_pairs={{0,1},{1,0},{2,3},{3,2},{4,5},{5,4},{6,7},{7,6},{8,9},{9,8},{10,11... | collective-permute-start | bytes 491528 | tf_op jit(solution)/shard_map/ppermute | solution.py:563
  23.2 4.5 %collective-permute-start.6 = (f32[2,2,40,128]{3,2,1,0:T(8,128)S(1)}, f32[2,2,40,128]{3,2,1,0:T(8,128)S(1)}, u32[]{:S(2)}, u32[]{:S(2)}) collective-permute-start(f32[2,2,40,128]{3,2,1,0:T(8,128)S(1)} %get-tuple-element.29), channel_id=1, source_target_pairs={{0,1},{1,0},{2,3},{3,2},{4,5},{5,4},{6,7},{7,6},{8,9},{9,8},{10,11... | collective-permute-start | bytes 245768 | tf_op jit(solution)/shard_map/ppermute | solution.py:565
